TPU v7x, 256 devices: a whole 4x4x8 slice. The times are simulated.
256 devices in a mesh: gx: 16 (over z, core), gy: 16 (over y, x).
Axes of the slice: x: 4, y: 4, z: 8, core: 2. Of those that a mesh axis runs over, the one named last changes fastest.
Arguments:
- populations: float32 [19, 8, 128, 2048], P(None, None, 'gy', 'gx'), may hold values from 0.49 to 22.2, as said below
- concentrations: float32 [3, 8, 128, 2048], P(None, None, 'gy', 'gx'), may hold values from 0.5 to 2
- potential: float32 [8, 128, 2048], P(None, 'gy', 'gx'), may hold values from -5 to 5
- solid_mask: int32 [8, 128, 2048], P(None, 'gy', 'gx'), may hold values 0 or 1
- surface_sign: int32 [8, 128, 2048], P(None, 'gy', 'gx'), may hold values from -1 to 1
Outputs:
- populations_new: float32 [19, 8, 128, 2048], P(None, None, 'gy', 'gx')
- concentrations_new: float32 [3, 8, 128, 2048], P(None, None, 'gy', 'gx')
- potential_new: float32 [8, 128, 2048], P(None, 'gy', 'gx')
Inputs may be any that keep to these rules, and one draw needn't show every extreme that they name: `populations`: every entry is positive, near 36 times the weight of its velocity times a density of order one. `solid_mask`: 1 marks a solid cell, 0 a fluid one. `surface_sign`: read only at solid cells.
All inputs are finite; a program needn't handle non-finite values. No bound on the sum of `solid_mask` on one device may be relied on, other than what follows from the above.
Results may differ from a plain program's by a relative error of at most 0.0018.
Values sent between devices are 32-bit elements; how exact they have to be, the bound alone decides.
No kernel may reach another device: no remote copies, remote signals or barrier semaphores. Data moves between devices by JAX's collectives and lax.ppermute only.
A program may use at most 64 MiB of HBM per device.

v0:
```python
import jax
import jax.numpy as jnp
import numpy as np
from jax import lax
from jax.sharding import PartitionSpec as P

STEPS = 4
CYCLES = 2
SSTEP = 4


lattice_velocity = (
    (0, 0, 0),
    (0, 0, 1),
    (0, 0, -1),
    (0, 1, 0),
    (0, -1, 0),
    (1, 0, 0),
    (-1, 0, 0),
    (0, 1, 1),
    (0, -1, -1),
    (0, 1, -1),
    (0, -1, 1),
    (1, 0, 1),
    (-1, 0, -1),
    (1, 0, -1),
    (-1, 0, 1),
    (1, 1, 0),
    (-1, -1, 0),
    (1, -1, 0),
    (-1, 1, 0),
)
opposite = (0, 2, 1, 4, 3, 6, 5, 8, 7, 10, 9, 12, 11, 14, 13, 16, 15, 18, 17)
lattice_weight = (1.0 / 3.0,) + (1.0 / 18.0,) * 6 + (1.0 / 36.0,) * 12
moving = (1, 2, 3, 4, 7, 8, 9, 10, 11, 12, 13, 14, 15, 16, 17, 18)
relax_time = 1.25
force_scale = 0.05
valences = (1.0, -1.0, 2.0)
diffusivity = (0.05, 0.07, 0.03)
diag_coef = 6.0001
surface_scale = 2.0


def padded_2(block, sides, width):
    for axis, dim in sides:
        count = lax.axis_size(axis)
        forward = [(i, i + 1) for i in range(count - 1)]
        forward.append((count - 1, 0))
        backward = [(target, source) for source, target in forward]
        low = lax.ppermute(
            lax.slice_in_dim(block, block.shape[dim] - width, None, axis=dim), axis, forward
        )
        high = lax.ppermute(lax.slice_in_dim(block, 0, width, axis=dim), axis, backward)
        block = jnp.concatenate([low, block, high], axis=dim)
    return block


def lattice_dot(direction, vector):
    running = None
    for axis_id in range(3):
        if direction[axis_id] != 0:
            addend = vector[axis_id] if direction[axis_id] > 0 else -vector[axis_id]
            running = addend if running is None else running + addend
    return running


def ion_charge(concentration):
    return (
        valences[0] * concentration[0]
        + valences[1] * concentration[1]
        + valences[2] * concentration[2]
    )


def collide_cells(fields, concentration, fluid_mask, efield):
    density = fields[0]
    for member in range(1, 19):
        density = density + fields[member]
    momentum = []
    for axis_id in range(3):
        running = None
        for member in range(19):
            sign_val = lattice_velocity[member][axis_id]
            if sign_val != 0:
                addend = fields[member] if sign_val > 0 else -fields[member]
                running = addend if running is None else running + addend
        momentum.append(running)
    charge = fluid_mask * ion_charge(concentration)
    forcing = [force_scale * charge * efield[axis_id] for axis_id in range(3)]
    velocity = [(momentum[axis_id] + 0.5 * forcing[axis_id]) / density for axis_id in range(3)]
    speed_sq = velocity[0] * velocity[0] + velocity[1] * velocity[1] + velocity[2] * velocity[2]
    work_rate = velocity[0] * forcing[0] + velocity[1] * forcing[1] + velocity[2] * forcing[2]
    relaxed = []
    for member in range(19):
        weight = lattice_weight[member]
        if member == 0:
            projected = jnp.zeros_like(density)
            along_force = jnp.zeros_like(density)
        else:
            projected = lattice_dot(lattice_velocity[member], velocity)
            along_force = lattice_dot(lattice_velocity[member], forcing)
        balance = (
            weight
            * density
            * (1.0 + 3.0 * projected + 4.5 * projected * projected - 1.5 * speed_sq)
        )
        source = weight * (3.0 * (along_force - work_rate) + 9.0 * projected * along_force)
        relaxed.append(
            fields[member]
            - (fields[member] - balance) / relax_time
            + (1.0 - 0.5 / relax_time) * source
        )
    return (relaxed, velocity)


def face_flux(low, high, pot_low, pot_high, vel_low, vel_high, opened):
    rates = jnp.array(diffusivity, jnp.float32).reshape(3, 1, 1, 1)
    drift = jnp.array(valences, jnp.float32).reshape(3, 1, 1, 1) * rates
    middle = 0.5 * (low + high)
    return opened * (
        -rates * (high - low)
        - drift * middle * (pot_high - pot_low)
        + 0.5 * (vel_low + vel_high) * middle
    )


def ion_step(concentration, velocity, potential, fluid_mask, ion_pad, pot_rim, fluid_rim):
    fluxes = face_flux(
        concentration,
        jnp.roll(concentration, -1, 1),
        potential,
        jnp.roll(potential, -1, 0),
        velocity[0],
        jnp.roll(velocity[0], -1, 0),
        fluid_mask * jnp.roll(fluid_mask, -1, 0),
    )
    running = fluxes - jnp.roll(fluxes, 1, 1)
    conc_in = ion_pad[:3, :, :, 1:-1]
    pot_in = pot_rim[:, :, 1:-1]
    vel_in = ion_pad[3, :, :, 1:-1]
    open_in = fluid_rim[:, :, 1:-1]
    fluxes = face_flux(
        conc_in[:, :, :-1],
        conc_in[:, :, 1:],
        pot_in[:, :-1],
        pot_in[:, 1:],
        vel_in[:, :-1],
        vel_in[:, 1:],
        open_in[:, :-1] * open_in[:, 1:],
    )
    running = running + (fluxes[:, :, 1:] - fluxes[:, :, :-1])
    conc_in = ion_pad[:3, :, 1:-1, :]
    pot_in = pot_rim[:, 1:-1, :]
    vel_in = ion_pad[4, :, 1:-1, :]
    open_in = fluid_rim[:, 1:-1, :]
    fluxes = face_flux(
        conc_in[..., :-1],
        conc_in[..., 1:],
        pot_in[..., :-1],
        pot_in[..., 1:],
        vel_in[..., :-1],
        vel_in[..., 1:],
        open_in[..., :-1] * open_in[..., 1:],
    )
    running = running + (fluxes[..., 1:] - fluxes[..., :-1])
    return concentration - running


def neighbor_sum(padded):
    core = padded[:, :, 1:-1, 1:-1]
    return (
        jnp.roll(core, -1, 1)
        + jnp.roll(core, 1, 1)
        + (padded[:, :, 2:, 1:-1] + padded[:, :, :-2, 1:-1])
        + (padded[:, :, 1:-1, 2:] + padded[:, :, 1:-1, :-2])
    )


def next_level(summed, previous):
    if previous is None:
        return -summed / 6.0
    return -summed / 3.0 - previous


def shift_table():
    order_m = 2 * SSTEP + 1
    coeffs = np.zeros((order_m, order_m), np.float32)
    for block_start in (0, SSTEP + 1):
        block_depth = SSTEP if block_start == 0 else SSTEP - 1
        for column in range(block_depth):
            coeffs[block_start + column, block_start + column] = diag_coef
            coeffs[block_start + column + 1, block_start + column] = 6.0 if column == 0 else 3.0
            if column > 0:
                coeffs[block_start + column - 1, block_start + column] = 3.0
    return coeffs


def krylov_steps(gram_matrix):
    order_m = 2 * SSTEP + 1
    highest = lax.Precision.HIGHEST
    coeffs = jnp.asarray(shift_table(), jnp.float32)
    search_co = jnp.zeros((order_m,), jnp.float32).at[0].set(1.0)
    resid_co = jnp.zeros((order_m,), jnp.float32).at[SSTEP + 1].set(1.0)
    sol_co = jnp.zeros((order_m,), jnp.float32)
    residual_sq = jnp.dot(
        resid_co, jnp.dot(gram_matrix, resid_co, precision=highest), precision=highest
    )
    for inner_id in range(SSTEP):
        image_co = jnp.dot(coeffs, search_co, precision=highest)
        step_len = residual_sq / jnp.dot(
            search_co, jnp.dot(gram_matrix, image_co, precision=highest), precision=highest
        )
        sol_co = sol_co + step_len * search_co
        resid_co = resid_co - step_len * image_co
        fresh_sq = jnp.dot(
            resid_co, jnp.dot(gram_matrix, resid_co, precision=highest), precision=highest
        )
        search_co = resid_co + fresh_sq / residual_sq * search_co
        residual_sq = fresh_sq
    return (sol_co, resid_co, search_co)


def local(populations, concentrations, potential, solid_mask, surface_sign):
    highest = lax.Precision.HIGHEST
    fluid_mask = 1.0 - solid_mask.astype(jnp.float32)
    rows_y = potential.shape[1]
    cols_x = potential.shape[2]
    rims = padded_2(jnp.stack([potential, fluid_mask]), (("gx", 3), ("gy", 2)), 1)
    pot_rim = rims[0]
    fluid_rim = rims[1]
    efield = [
        (jnp.roll(potential, 1, 0) - jnp.roll(potential, -1, 0)) * 0.5,
        (pot_rim[:, :-2, 1:-1] - pot_rim[:, 2:, 1:-1]) * 0.5,
        (pot_rim[:, 1:-1, :-2] - pot_rim[:, 1:-1, 2:]) * 0.5,
    ]
    source_open = []
    for member in range(19):
        offset = lattice_velocity[member]
        window = fluid_rim[
            :, 1 - offset[1] : 1 - offset[1] + rows_y, 1 - offset[2] : 1 - offset[2] + cols_x
        ]
        source_open.append(jnp.roll(window, offset[0], 0))
    fields = [populations[member] for member in range(19)]
    concentration = concentrations
    for time_step in range(STEPS):
        relaxed, velocity = collide_cells(fields, concentration, fluid_mask, efield)
        stacked = jnp.concatenate(
            [
                jnp.stack([relaxed[member] for member in moving]),
                concentration,
                jnp.stack([velocity[1], velocity[2]]),
            ]
        )
        lattice_pad = padded_2(stacked, (("gx", 3), ("gy", 2)), 1)
        ion_pad = lattice_pad[len(moving) :]
        arrived = []
        for member in range(19):
            offset = lattice_velocity[member]
            if member in moving:
                slot_id = moving.index(member)
                piece = lattice_pad[
                    slot_id,
                    :,
                    1 - offset[1] : 1 - offset[1] + rows_y,
                    1 - offset[2] : 1 - offset[2] + cols_x,
                ]
            else:
                piece = relaxed[member]
            arrived.append(jnp.roll(piece, offset[0], 0))
        updated = [
            jnp.where(
                fluid_mask > 0.5,
                jnp.where(source_open[member] > 0.5, arrived[member], relaxed[opposite[member]]),
                fields[member],
            )
            for member in range(19)
        ]
        concentration = ion_step(
            concentration, velocity, potential, fluid_mask, ion_pad, pot_rim, fluid_rim
        )
        fields = updated
    target = fluid_mask * ion_charge(concentration) + surface_scale * surface_sign.astype(
        jnp.float32
    ) * (1.0 - fluid_mask)
    solution = potential
    start_pad = padded_2(solution[None], (("gx", 3), ("gy", 2)), 1)
    residual = target - (diag_coef * solution - neighbor_sum(start_pad)[0])
    search = residual
    for cycle_id in range(CYCLES):
        p_levels = [search]
        r_levels = [residual]
        previous = None
        current = jnp.stack([search, residual])
        for level_id in range(SSTEP):
            if level_id == SSTEP - 1:
                current = current[:1]
            padded = padded_2(current, (("gx", 3), ("gy", 2)), 1)
            following = next_level(
                neighbor_sum(padded), None if level_id == 0 else previous[: current.shape[0]]
            )
            previous = current
            current = following
            p_levels.append(current[0])
            if current.shape[0] > 1:
                r_levels.append(current[1])
        basis = jnp.stack(p_levels + r_levels)
        local_gram = jnp.einsum("aijk,bijk->ab", basis, basis, precision=highest)
        gram_matrix = lax.psum(local_gram, ("gx", "gy"))
        sol_co, resid_co, search_co = krylov_steps(gram_matrix)
        solution = solution + jnp.tensordot(sol_co, basis, axes=1, precision=highest)
        residual = jnp.tensordot(resid_co, basis, axes=1, precision=highest)
        search = jnp.tensordot(search_co, basis, axes=1, precision=highest)
    return (jnp.stack(fields), concentration, solution)


def solution(mesh):
    placed = (
        P(None, None, "gy", "gx"),
        P(None, None, "gy", "gx"),
        P(None, "gy", "gx"),
        P(None, "gy", "gx"),
        P(None, "gy", "gx"),
    )
    return jax.shard_map(
        local,
        mesh=mesh,
        in_specs=placed,
        out_specs=(P(None, None, "gy", "gx"), P(None, None, "gy", "gx"), P(None, "gy", "gx")),
        check_vma=False,
    )
```

profile of v0, /device:TPU:1, one launch (start us, length us, event | category | flops | bytes accessed | tf_op | source)
XLA Modules:
  0.0 479.0 jit_solution(2040877553520355775)
XLA Ops:
  2.4 3.0 collective-permute-start
  6.4 1.5 collective-permute-start.20
  7.9 2.0 collective-permute-start.21
  11.4 3.8 collective-permute-start.3
  32.1 3.3 collective-permute-start.5
  40.6 1.5 copy.37
  43.5 5.4 %collective-permute-start.7 = (f32[21,8,1,130]{3,2,1,0:T(1,128)S(1)}, f32[21,8,1,130]{3,2,1,0:T(1,128)S(1)}, u32[]{:S(2)}, u32[]{:S(2)}) collective-permute-start(f32[21,8,1,130]{3,2,1,0:T(1,128)S(1)} %get-tuple-element.347), channel_id=1, source_target_pairs={{1,0},{2,1},{3,2},{4,3},{5,4},{6,5},{7,6},{8,7},{9,8},{10,9},{11,1... | collective-permute-start | bytes 262088 | tf_op jit(solution)/shard_map/ppermute | solution.py:53
  49.2 2.2 collective-permute-done.6
  54.0 2.1 fusion.355
  70.3 3.0 collective-permute-start.9
  79.4 5.8 %collective-permute-start.11 = (f32[21,8,1,130]{3,2,1,0:T(1,128)S(1)}, f32[21,8,1,130]{3,2,1,0:T(1,128)S(1)}, u32[]{:S(2)}, u32[]{:S(2)}) collective-permute-start(f32[21,8,1,130]{3,2,1,0:T(1,128)S(1)} %get-tuple-element.341), channel_id=1, source_target_pairs={{1,0},{2,1},{3,2},{4,3},{5,4},{6,5},{7,6},{8,7},{9,8},{10,9},{11,1... | collective-permute-start | bytes 262088 | tf_op jit(solution)/shard_map/ppermute | solution.py:53
  85.6 2.0 collective-permute-done.10
  89.6 2.3 fusion.481
  106.0 3.1 collective-permute-start.13
  115.1 5.6 %collective-permute-start.15 = (f32[21,8,1,130]{3,2,1,0:T(1,128)S(1)}, f32[21,8,1,130]{3,2,1,0:T(1,128)S(1)}, u32[]{:S(2)}, u32[]{:S(2)}) collective-permute-start(f32[21,8,1,130]{3,2,1,0:T(1,128)S(1)} %get-tuple-element.335), channel_id=1, source_target_pairs={{1,0},{2,1},{3,2},{4,3},{5,4},{6,5},{7,6},{8,7},{9,8},{10,9},{11,1... | collective-permute-start | bytes 262088 | tf_op jit(solution)/shard_map/ppermute | solution.py:53
  121.0 2.4 collective-permute-done.14
  125.4 2.3 fusion.600
  141.5 3.2 collective-permute-start.17
  144.7 1.6 pad_maximum_fusion.185
  146.2 5.1 %collective-permute-start.22 = (f32[1,8,1,130]{3,2,1,0:T(1,128)}, f32[1,8,1,130]{3,2,1,0:T(1,128)}, u32[]{:S(2)}, u32[]{:S(2)}) collective-permute-start(f32[1,8,1,130]{3,2,1,0:T(1,128)} %get-tuple-element.428), channel_id=1, source_target_pairs={{1,0},{2,1},{3,2},{4,3},{5,4},{6,5},{7,6},{8,7},{9,8},{10,9},{11,1... | collective-permute-start | bytes 12488 | tf_op jit(solution)/shard_map/ppermute | solution.py:53
  156.5 4.8 %collective-permute-start.19 = (f32[21,8,1,130]{3,2,1,0:T(1,128)S(1)}, f32[21,8,1,130]{3,2,1,0:T(1,128)S(1)}, u32[]{:S(2)}, u32[]{:S(2)}) collective-permute-start(f32[21,8,1,130]{3,2,1,0:T(1,128)S(1)} %get-tuple-element.328), channel_id=1, source_target_pairs={{1,0},{2,1},{3,2},{4,3},{5,4},{6,5},{7,6},{8,7},{9,8},{10,9},{11,1... | collective-permute-start | bytes 262088 | tf_op jit(solution)/shard_map/ppermute | solution.py:53
  170.8 3.6 collective-permute-start.25
  184.3 5.2 %collective-permute-start.26 = (f32[2,8,1,130]{3,0,2,1:T(2,128)S(1)}, f32[2,8,1,130]{3,0,2,1:T(2,128)S(1)}, u32[]{:S(2)}, u32[]{:S(2)}) collective-permute-start(f32[2,8,1,130]{3,0,2,1:T(2,128)S(1)} %get-tuple-element.402), channel_id=1, source_target_pairs={{1,0},{2,1},{3,2},{4,3},{5,4},{6,5},{7,6},{8,7},{9,8},{10,9},{11,1... | collective-permute-start | bytes 24968 | tf_op jit(solution)/shard_map/ppermute | solution.py:53
  190.4 5.0 %collective-permute-done.27 = f32[2,8,1,130]{3,0,2,1:T(2,128)S(1)} collective-permute-done((f32[2,8,1,130]{3,0,2,1:T(2,128)S(1)}, f32[2,8,1,130]{3,0,2,1:T(2,128)S(1)}, u32[]{:S(2)}, u32[]{:S(2)}) %collective-permute-start.27) | collective-permute-done | bytes 8352 | tf_op jit(solution)/shard_map/ppermute | solution.py:50
  196.2 4.4 collective-permute-start.29
  201.7 1.5 collective-permute-start.31
  203.1 1.4 collective-permute-done.30
  204.5 3.1 collective-permute-done.31
  208.2 5.1 %collective-permute-start.33 = (f32[2,8,8,1]{3,0,2,1:T(2,128)S(1)}, f32[2,8,8,1]{3,0,2,1:T(2,128)S(1)}, u32[]{:S(2)}, u32[]{:S(2)}) collective-permute-start(f32[2,8,8,1]{3,0,2,1:T(2,128)S(1)} %get-tuple-element.487), channel_id=1, source_target_pairs={{16,0},{32,16},{48,32},{64,48},{80,64},{96,80},{112,96},{128,112},... | collective-permute-start | bytes 1544 | tf_op jit(solution)/shard_map/ppermute | solution.py:53
  214.5 1.6 collective-permute-start.35
  217.4 3.3 collective-permute-done.35
  221.3 5.1 %collective-permute-start.37 = (f32[1,8,8,1]{3,0,2,1:T(1,128)S(1)}, f32[1,8,8,1]{3,0,2,1:T(1,128)S(1)}, u32[]{:S(2)}, u32[]{:S(2)}) collective-permute-start(f32[1,8,8,1]{3,0,2,1:T(1,128)S(1)} %get-tuple-element.481), channel_id=1, source_target_pairs={{16,0},{32,16},{48,32},{64,48},{80,64},{96,80},{112,96},{128,112},... | collective-permute-start | bytes 776 | tf_op jit(solution)/shard_map/ppermute | solution.py:53
  227.5 1.5 collective-permute-start.39
  230.3 3.1 collective-permute-done.39
  235.1 78.9 %psum.14 = f32[9,9]{1,0:T(8,128)S(1)} all-reduce(f32[9,9]{1,0:T(8,128)S(1)} %convolution_bitcast_fusion.1), channel_id=1, replica_groups=mesh['gx'=16,'gy'=16] {'gx','gy'}, use_global_device_ids=true, to_apply=%region_0.1 | all-reduce | flops 81 | bytes 648 | tf_op jit(solution)/shard_map/psum | solution.py:308
  335.4 2.3 collective-permute-done.41
  340.5 4.5 collective-permute-done.43
  345.7 1.6 collective-permute-start.44
  347.3 1.8 collective-permute-start.45
  351.2 1.5 collective-permute-start.47
  353.8 3.4 collective-permute-done.47
  358.9 3.0 collective-permute-start.49
  363.3 1.5 collective-permute-start.51
  366.1 3.1 collective-permute-done.51
  370.8 4.2 collective-permute-start.53
  376.1 1.5 collective-permute-start.55
  378.9 3.1 collective-permute-done.55
  383.7 77.5 %psum.15 = f32[9,9]{1,0:T(8,128)S(1)} all-reduce(f32[9,9]{1,0:T(8,128)S(1)} %convolution_bitcast_fusion), channel_id=1, replica_groups=mesh['gx'=16,'gy'=16] {'gx','gy'}, use_global_device_ids=true, to_apply=%region_1.2 | all-reduce | flops 81 | bytes 648 | tf_op jit(solution)/shard_map/psum | solution.py:308
  (924 shorter events, 155.9 us)
Async XLA Ops:
  2.4 7.5 %collective-permute-start = (f32[2,8,8,1]{3,2,1,0:T(8,128)S(1)}, f32[2,8,8,1]{3,2,1,0:T(8,128)S(1)}, u32[]{:S(2)}, u32[]{:S(2)}) collective-permute-start(f32[2,8,8,1]{3,2,1,0:T(8,128)S(1)} %get-tuple-element.495), channel_id=1, source_target_pairs={{0,16},{16,32},{32,48},{48,64},{64,80},{80,96},{96,112},{112,128},... | collective-permute-start | bytes 1544 | tf_op jit(solution)/shard_map/ppermute | solution.py:50
  5.5 4.5 collective-permute-start.1
  6.4 138.3 %collective-permute-start.20 = (f32[1,8,8,1]{3,2,1,0:T(8,128)}, f32[1,8,8,1]{3,2,1,0:T(8,128)}, u32[]{:S(2)}, u32[]{:S(2)}) collective-permute-start(f32[1,8,8,1]{3,2,1,0:T(8,128)} %get-tuple-element.508), channel_id=1, source_target_pairs={{0,16},{16,32},{32,48},{48,64},{64,80},{80,96},{96,112},{112,128},... | collective-permute-start | bytes 776 | tf_op jit(solution)/shard_map/ppermute | solution.py:50
  7.9 136.8 %collective-permute-start.21 = (f32[1,8,8,1]{3,2,1,0:T(8,128)}, f32[1,8,8,1]{3,2,1,0:T(8,128)}, u32[]{:S(2)}, u32[]{:S(2)}) collective-permute-start(f32[1,8,8,1]{3,2,1,0:T(8,128)} %get-tuple-element.507), channel_id=1, source_target_pairs={{16,0},{32,16},{48,32},{64,48},{80,64},{96,80},{112,96},{128,112},... | collective-permute-start | bytes 776 | tf_op jit(solution)/shard_map/ppermute | solution.py:53
  10.1 6.1 %collective-permute-start.2 = (f32[2,8,1,130]{3,2,1,0:T(1,128)S(1)}, f32[2,8,1,130]{3,2,1,0:T(1,128)S(1)}, u32[]{:S(2)}, u32[]{:S(2)}) collective-permute-start(f32[2,8,1,130]{3,2,1,0:T(1,128)S(1)} %get-tuple-element.400), channel_id=1, source_target_pairs={{0,1},{1,2},{2,3},{3,4},{4,5},{5,6},{6,7},{7,8},{8,9},{9,10},{10,1... | collective-permute-start | bytes 24968 | tf_op jit(solution)/shard_map/ppermute | solution.py:50
  11.4 4.8 %collective-permute-start.3 = (f32[2,8,1,130]{3,2,1,0:T(1,128)S(1)}, f32[2,8,1,130]{3,2,1,0:T(1,128)S(1)}, u32[]{:S(2)}, u32[]{:S(2)}) collective-permute-start(f32[2,8,1,130]{3,2,1,0:T(1,128)S(1)} %get-tuple-element.401), channel_id=1, source_target_pairs={{1,0},{2,1},{3,2},{4,3},{5,4},{6,5},{7,6},{8,7},{9,8},{10,9},{11,1... | collective-permute-start | bytes 24968 | tf_op jit(solution)/shard_map/ppermute | solution.py:53
  30.9 8.9 %collective-permute-start.4 = (f32[21,8,8,1]{0,2,3,1:T(8,128)S(1)}, f32[21,8,8,1]{0,2,3,1:T(8,128)S(1)}, u32[]{:S(2)}, u32[]{:S(2)}) collective-permute-start(f32[21,8,8,1]{0,2,3,1:T(8,128)S(1)} %copy.34), channel_id=1, source_target_pairs={{0,16},{16,32},{32,48},{48,64},{64,80},{80,96},{96,112},{112,128},... | collective-permute-start | bytes 16136 | tf_op jit(solution)/shard_map/ppermute | solution.py:50
  32.1 8.4 %collective-permute-start.5 = (f32[21,8,8,1]{0,2,3,1:T(8,128)S(1)}, f32[21,8,8,1]{0,2,3,1:T(8,128)}, u32[]{:S(2)}, u32[]{:S(2)}) collective-permute-start(f32[21,8,8,1]{0,2,3,1:T(8,128)S(1)} %copy.36), channel_id=1, source_target_pairs={{16,0},{32,16},{48,32},{64,48},{80,64},{96,80},{112,96},{128,112},... | collective-permute-start | bytes 16136 | tf_op jit(solution)/shard_map/ppermute | solution.py:53
  43.4 7.9 %collective-permute-start.6 = (f32[21,8,1,130]{3,2,1,0:T(1,128)S(1)}, f32[21,8,1,130]{3,2,1,0:T(1,128)S(1)}, u32[]{:S(2)}, u32[]{:S(2)}) collective-permute-start(f32[21,8,1,130]{3,2,1,0:T(1,128)S(1)} %get-tuple-element.346), channel_id=1, source_target_pairs={{0,1},{1,2},{2,3},{3,4},{4,5},{5,6},{6,7},{7,8},{8,9},{9,10},{10,1... | collective-permute-start | bytes 262088 | tf_op jit(solution)/shard_map/ppermute | solution.py:50
  43.5 7.8 %collective-permute-start.7 = (f32[21,8,1,130]{3,2,1,0:T(1,128)S(1)}, f32[21,8,1,130]{3,2,1,0:T(1,128)S(1)}, u32[]{:S(2)}, u32[]{:S(2)}) collective-permute-start(f32[21,8,1,130]{3,2,1,0:T(1,128)S(1)} %get-tuple-element.347), channel_id=1, source_target_pairs={{1,0},{2,1},{3,2},{4,3},{5,4},{6,5},{7,6},{8,7},{9,8},{10,9},{11,1... | collective-permute-start | bytes 262088 | tf_op jit(solution)/shard_map/ppermute | solution.py:53
  69.0 7.5 %collective-permute-start.8 = (f32[21,8,8,1]{0,2,3,1:T(8,128)S(1)}, f32[21,8,8,1]{0,2,3,1:T(8,128)S(1)}, u32[]{:S(2)}, u32[]{:S(2)}) collective-permute-start(f32[21,8,8,1]{0,2,3,1:T(8,128)S(1)} %copy.40), channel_id=1, source_target_pairs={{0,16},{16,32},{32,48},{48,64},{64,80},{80,96},{96,112},{112,128},... | collective-permute-start | bytes 16136 | tf_op jit(solution)/shard_map/ppermute | solution.py:50
  70.3 6.9 %collective-permute-start.9 = (f32[21,8,8,1]{0,2,3,1:T(8,128)S(1)}, f32[21,8,8,1]{0,2,3,1:T(8,128)S(1)}, u32[]{:S(2)}, u32[]{:S(2)}) collective-permute-start(f32[21,8,8,1]{0,2,3,1:T(8,128)S(1)} %copy.42), channel_id=1, source_target_pairs={{16,0},{32,16},{48,32},{64,48},{80,64},{96,80},{112,96},{128,112},... | collective-permute-start | bytes 16136 | tf_op jit(solution)/shard_map/ppermute | solution.py:53
  79.4 8.2 %collective-permute-start.10 = (f32[21,8,1,130]{3,2,1,0:T(1,128)S(1)}, f32[21,8,1,130]{3,2,1,0:T(1,128)S(1)}, u32[]{:S(2)}, u32[]{:S(2)}) collective-permute-start(f32[21,8,1,130]{3,2,1,0:T(1,128)S(1)} %get-tuple-element.340), channel_id=1, source_target_pairs={{0,1},{1,2},{2,3},{3,4},{4,5},{5,6},{6,7},{7,8},{8,9},{9,10},{10,1... | collective-permute-start | bytes 262088 | tf_op jit(solution)/shard_map/ppermute | solution.py:50
  79.4 8.2 %collective-permute-start.11 = (f32[21,8,1,130]{3,2,1,0:T(1,128)S(1)}, f32[21,8,1,130]{3,2,1,0:T(1,128)S(1)}, u32[]{:S(2)}, u32[]{:S(2)}) collective-permute-start(f32[21,8,1,130]{3,2,1,0:T(1,128)S(1)} %get-tuple-element.341), channel_id=1, source_target_pairs={{1,0},{2,1},{3,2},{4,3},{5,4},{6,5},{7,6},{8,7},{9,8},{10,9},{11,1... | collective-permute-start | bytes 262088 | tf_op jit(solution)/shard_map/ppermute | solution.py:53
  104.7 7.4 %collective-permute-start.12 = (f32[21,8,8,1]{0,2,3,1:T(8,128)S(1)}, f32[21,8,8,1]{0,2,3,1:T(8,128)S(1)}, u32[]{:S(2)}, u32[]{:S(2)}) collective-permute-start(f32[21,8,8,1]{0,2,3,1:T(8,128)S(1)} %copy.46), channel_id=1, source_target_pairs={{0,16},{16,32},{32,48},{48,64},{64,80},{80,96},{96,112},{112,128},... | collective-permute-start | bytes 16136 | tf_op jit(solution)/shard_map/ppermute | solution.py:50
  106.0 6.9 %collective-permute-start.13 = (f32[21,8,8,1]{0,2,3,1:T(8,128)S(1)}, f32[21,8,8,1]{0,2,3,1:T(8,128)S(1)}, u32[]{:S(2)}, u32[]{:S(2)}) collective-permute-start(f32[21,8,8,1]{0,2,3,1:T(8,128)S(1)} %copy.48), channel_id=1, source_target_pairs={{16,0},{32,16},{48,32},{64,48},{80,64},{96,80},{112,96},{128,112},... | collective-permute-start | bytes 16136 | tf_op jit(solution)/shard_map/ppermute | solution.py:53
  115.0 8.4 %collective-permute-start.14 = (f32[21,8,1,130]{3,2,1,0:T(1,128)S(1)}, f32[21,8,1,130]{3,2,1,0:T(1,128)S(1)}, u32[]{:S(2)}, u32[]{:S(2)}) collective-permute-start(f32[21,8,1,130]{3,2,1,0:T(1,128)S(1)} %get-tuple-element.334), channel_id=1, source_target_pairs={{0,1},{1,2},{2,3},{3,4},{4,5},{5,6},{6,7},{7,8},{8,9},{9,10},{10,1... | collective-permute-start | bytes 262088 | tf_op jit(solution)/shard_map/ppermute | solution.py:50
  115.1 8.3 %collective-permute-start.15 = (f32[21,8,1,130]{3,2,1,0:T(1,128)S(1)}, f32[21,8,1,130]{3,2,1,0:T(1,128)S(1)}, u32[]{:S(2)}, u32[]{:S(2)}) collective-permute-start(f32[21,8,1,130]{3,2,1,0:T(1,128)S(1)} %get-tuple-element.335), channel_id=1, source_target_pairs={{1,0},{2,1},{3,2},{4,3},{5,4},{6,5},{7,6},{8,7},{9,8},{10,9},{11,1... | collective-permute-start | bytes 262088 | tf_op jit(solution)/shard_map/ppermute | solution.py:53
  140.3 13.2 %collective-permute-start.16 = (f32[21,8,8,1]{0,2,3,1:T(8,128)S(1)}, f32[21,8,8,1]{0,2,3,1:T(8,128)S(1)}, u32[]{:S(2)}, u32[]{:S(2)}) collective-permute-start(f32[21,8,8,1]{0,2,3,1:T(8,128)S(1)} %copy.52), channel_id=1, source_target_pairs={{0,16},{16,32},{32,48},{48,64},{64,80},{80,96},{96,112},{112,128},... | collective-permute-start | bytes 16136 | tf_op jit(solution)/shard_map/ppermute | solution.py:50
  141.5 12.8 %collective-permute-start.17 = (f32[21,8,8,1]{0,2,3,1:T(8,128)S(1)}, f32[21,8,8,1]{0,2,3,1:T(8,128)S(1)}, u32[]{:S(2)}, u32[]{:S(2)}) collective-permute-start(f32[21,8,8,1]{0,2,3,1:T(8,128)S(1)} %copy.54), channel_id=1, source_target_pairs={{16,0},{32,16},{48,32},{64,48},{80,64},{96,80},{112,96},{128,112},... | collective-permute-start | bytes 16136 | tf_op jit(solution)/shard_map/ppermute | solution.py:53
  146.2 21.8 %collective-permute-start.22 = (f32[1,8,1,130]{3,2,1,0:T(1,128)}, f32[1,8,1,130]{3,2,1,0:T(1,128)}, u32[]{:S(2)}, u32[]{:S(2)}) collective-permute-start(f32[1,8,1,130]{3,2,1,0:T(1,128)} %get-tuple-element.428), channel_id=1, source_target_pairs={{1,0},{2,1},{3,2},{4,3},{5,4},{6,5},{7,6},{8,7},{9,8},{10,9},{11,1... | collective-permute-start | bytes 12488 | tf_op jit(solution)/shard_map/ppermute | solution.py:53
  151.4 16.7 %collective-permute-start.23 = (f32[1,8,1,130]{3,2,1,0:T(1,128)}, f32[1,8,1,130]{3,2,1,0:T(1,128)}, u32[]{:S(2)}, u32[]{:S(2)}) collective-permute-start(f32[1,8,1,130]{3,2,1,0:T(1,128)} %get-tuple-element.429), channel_id=1, source_target_pairs={{0,1},{1,2},{2,3},{3,4},{4,5},{5,6},{6,7},{7,8},{8,9},{9,10},{10,1... | collective-permute-start | bytes 12488 | tf_op jit(solution)/shard_map/ppermute | solution.py:50
  156.4 7.7 %collective-permute-start.18 = (f32[21,8,1,130]{3,2,1,0:T(1,128)S(1)}, f32[21,8,1,130]{3,2,1,0:T(1,128)S(1)}, u32[]{:S(2)}, u32[]{:S(2)}) collective-permute-start(f32[21,8,1,130]{3,2,1,0:T(1,128)S(1)} %get-tuple-element.329), channel_id=1, source_target_pairs={{0,1},{1,2},{2,3},{3,4},{4,5},{5,6},{6,7},{7,8},{8,9},{9,10},{10,1... | collective-permute-start | bytes 262088 | tf_op jit(solution)/shard_map/ppermute | solution.py:50
  156.5 7.6 %collective-permute-start.19 = (f32[21,8,1,130]{3,2,1,0:T(1,128)S(1)}, f32[21,8,1,130]{3,2,1,0:T(1,128)S(1)}, u32[]{:S(2)}, u32[]{:S(2)}) collective-permute-start(f32[21,8,1,130]{3,2,1,0:T(1,128)S(1)} %get-tuple-element.328), channel_id=1, source_target_pairs={{1,0},{2,1},{3,2},{4,3},{5,4},{6,5},{7,6},{8,7},{9,8},{10,9},{11,1... | collective-permute-start | bytes 262088 | tf_op jit(solution)/shard_map/ppermute | solution.py:53
  170.0 14.1 %collective-permute-start.24 = (f32[2,8,8,1]{3,0,2,1:T(2,128)S(1)}, f32[2,8,8,1]{3,0,2,1:T(2,128)S(1)}, u32[]{:S(2)}, u32[]{:S(2)}) collective-permute-start(f32[2,8,8,1]{3,0,2,1:T(2,128)S(1)} %get-tuple-element.502), channel_id=1, source_target_pairs={{0,16},{16,32},{32,48},{48,64},{64,80},{80,96},{96,112},{112,128},... | collective-permute-start | bytes 1544 | tf_op jit(solution)/shard_map/ppermute | solution.py:50
  170.8 13.4 %collective-permute-start.25 = (f32[2,8,8,1]{3,0,2,1:T(2,128)S(1)}, f32[2,8,8,1]{3,0,2,1:T(2,128)S(1)}, u32[]{:S(2)}, u32[]{:S(2)}) collective-permute-start(f32[2,8,8,1]{3,0,2,1:T(2,128)S(1)} %get-tuple-element.501), channel_id=1, source_target_pairs={{16,0},{32,16},{48,32},{64,48},{80,64},{96,80},{112,96},{128,112},... | collective-permute-start | bytes 1544 | tf_op jit(solution)/shard_map/ppermute | solution.py:53
  184.3 6.1 %collective-permute-start.26 = (f32[2,8,1,130]{3,0,2,1:T(2,128)S(1)}, f32[2,8,1,130]{3,0,2,1:T(2,128)S(1)}, u32[]{:S(2)}, u32[]{:S(2)}) collective-permute-start(f32[2,8,1,130]{3,0,2,1:T(2,128)S(1)} %get-tuple-element.402), channel_id=1, source_target_pairs={{1,0},{2,1},{3,2},{4,3},{5,4},{6,5},{7,6},{8,7},{9,8},{10,9},{11,1... | collective-permute-start | bytes 24968 | tf_op jit(solution)/shard_map/ppermute | solution.py:53
  189.5 5.9 %collective-permute-start.27 = (f32[2,8,1,130]{3,0,2,1:T(2,128)S(1)}, f32[2,8,1,130]{3,0,2,1:T(2,128)S(1)}, u32[]{:S(2)}, u32[]{:S(2)}) collective-permute-start(f32[2,8,1,130]{3,0,2,1:T(2,128)S(1)} %get-tuple-element.403), channel_id=1, source_target_pairs={{0,1},{1,2},{2,3},{3,4},{4,5},{5,6},{6,7},{7,8},{8,9},{9,10},{10,1... | collective-permute-start | bytes 24968 | tf_op jit(solution)/shard_map/ppermute | solution.py:50
  196.1 5.1 %collective-permute-start.28 = (f32[2,8,8,1]{3,0,2,1:T(2,128)S(1)}, f32[2,8,8,1]{3,0,2,1:T(2,128)S(1)}, u32[]{:S(2)}, u32[]{:S(2)}) collective-permute-start(f32[2,8,8,1]{3,0,2,1:T(2,128)S(1)} %get-tuple-element.494), channel_id=1, source_target_pairs={{0,16},{16,32},{32,48},{48,64},{64,80},{80,96},{96,112},{112,128},... | collective-permute-start | bytes 1544 | tf_op jit(solution)/shard_map/ppermute | solution.py:50
  196.2 5.3 %collective-permute-start.29 = (f32[2,8,8,1]{3,0,2,1:T(2,128)S(1)}, f32[2,8,8,1]{3,0,2,1:T(2,128)S(1)}, u32[]{:S(2)}, u32[]{:S(2)}) collective-permute-start(f32[2,8,8,1]{3,0,2,1:T(2,128)S(1)} %get-tuple-element.493), channel_id=1, source_target_pairs={{16,0},{32,16},{48,32},{64,48},{80,64},{96,80},{112,96},{128,112},... | collective-permute-start | bytes 1544 | tf_op jit(solution)/shard_map/ppermute | solution.py:53
  201.7 6.0 %collective-permute-start.31 = (f32[2,8,1,130]{3,0,2,1:T(2,128)S(1)}, f32[2,8,1,130]{3,0,2,1:T(2,128)S(1)}, u32[]{:S(2)}, u32[]{:S(2)}) collective-permute-start(f32[2,8,1,130]{3,0,2,1:T(2,128)S(1)} %get-tuple-element.399), channel_id=1, source_target_pairs={{0,1},{1,2},{2,3},{3,4},{4,5},{5,6},{6,7},{7,8},{8,9},{9,10},{10,1... | collective-permute-start | bytes 24968 | tf_op jit(solution)/shard_map/ppermute | solution.py:50
  208.2 5.9 %collective-permute-start.32 = (f32[2,8,8,1]{3,0,2,1:T(2,128)S(1)}, f32[2,8,8,1]{3,0,2,1:T(2,128)S(1)}, u32[]{:S(2)}, u32[]{:S(2)}) collective-permute-start(f32[2,8,8,1]{3,0,2,1:T(2,128)S(1)} %get-tuple-element.488), channel_id=1, source_target_pairs={{0,16},{16,32},{32,48},{48,64},{64,80},{80,96},{96,112},{112,128},... | collective-permute-start | bytes 1544 | tf_op jit(solution)/shard_map/ppermute | solution.py:50
  208.2 6.0 %collective-permute-start.33 = (f32[2,8,8,1]{3,0,2,1:T(2,128)S(1)}, f32[2,8,8,1]{3,0,2,1:T(2,128)S(1)}, u32[]{:S(2)}, u32[]{:S(2)}) collective-permute-start(f32[2,8,8,1]{3,0,2,1:T(2,128)S(1)} %get-tuple-element.487), channel_id=1, source_target_pairs={{16,0},{32,16},{48,32},{64,48},{80,64},{96,80},{112,96},{128,112},... | collective-permute-start | bytes 1544 | tf_op jit(solution)/shard_map/ppermute | solution.py:53
  214.5 6.2 %collective-permute-start.35 = (f32[2,8,1,130]{3,0,2,1:T(2,128)S(1)}, f32[2,8,1,130]{3,0,2,1:T(2,128)S(1)}, u32[]{:S(2)}, u32[]{:S(2)}) collective-permute-start(f32[2,8,1,130]{3,0,2,1:T(2,128)S(1)} %get-tuple-element.397), channel_id=1, source_target_pairs={{0,1},{1,2},{2,3},{3,4},{4,5},{5,6},{6,7},{7,8},{8,9},{9,10},{10,1... | collective-permute-start | bytes 24968 | tf_op jit(solution)/shard_map/ppermute | solution.py:50
  221.3 5.8 %collective-permute-start.36 = (f32[1,8,8,1]{3,0,2,1:T(1,128)S(1)}, f32[1,8,8,1]{3,0,2,1:T(1,128)S(1)}, u32[]{:S(2)}, u32[]{:S(2)}) collective-permute-start(f32[1,8,8,1]{3,0,2,1:T(1,128)S(1)} %get-tuple-element.482), channel_id=1, source_target_pairs={{0,16},{16,32},{32,48},{48,64},{64,80},{80,96},{96,112},{112,128},... | collective-permute-start | bytes 776 | tf_op jit(solution)/shard_map/ppermute | solution.py:50
  221.3 6.0 %collective-permute-start.37 = (f32[1,8,8,1]{3,0,2,1:T(1,128)S(1)}, f32[1,8,8,1]{3,0,2,1:T(1,128)S(1)}, u32[]{:S(2)}, u32[]{:S(2)}) collective-permute-start(f32[1,8,8,1]{3,0,2,1:T(1,128)S(1)} %get-tuple-element.481), channel_id=1, source_target_pairs={{16,0},{32,16},{48,32},{64,48},{80,64},{96,80},{112,96},{128,112},... | collective-permute-start | bytes 776 | tf_op jit(solution)/shard_map/ppermute | solution.py:53
  227.5 5.9 %collective-permute-start.39 = (f32[1,8,1,130]{3,0,2,1:T(1,128)S(1)}, f32[1,8,1,130]{3,0,2,1:T(1,128)S(1)}, u32[]{:S(2)}, u32[]{:S(2)}) collective-permute-start(f32[1,8,1,130]{3,0,2,1:T(1,128)S(1)} %get-tuple-element.427), channel_id=1, source_target_pairs={{0,1},{1,2},{2,3},{3,4},{4,5},{5,6},{6,7},{7,8},{8,9},{9,10},{10,1... | collective-permute-start | bytes 12488 | tf_op jit(solution)/shard_map/ppermute | solution.py:50
  334.0 3.7 collective-permute-start.41
  339.1 5.9 %collective-permute-start.43 = (f32[2,8,1,130]{3,0,2,1:T(2,128)S(1)}, f32[2,8,1,130]{3,0,2,1:T(2,128)S(1)}, u32[]{:S(2)}, u32[]{:S(2)}) collective-permute-start(f32[2,8,1,130]{3,0,2,1:T(2,128)S(1)} %get-tuple-element.395), channel_id=1, source_target_pairs={{0,1},{1,2},{2,3},{3,4},{4,5},{5,6},{6,7},{7,8},{8,9},{9,10},{10,1... | collective-permute-start | bytes 24968 | tf_op jit(solution)/shard_map/ppermute | solution.py:50
  345.7 4.1 collective-permute-start.44
  347.3 3.7 collective-permute-start.45
  351.2 6.0 %collective-permute-start.47 = (f32[2,8,1,130]{3,0,2,1:T(2,128)S(1)}, f32[2,8,1,130]{3,0,2,1:T(2,128)S(1)}, u32[]{:S(2)}, u32[]{:S(2)}) collective-permute-start(f32[2,8,1,130]{3,0,2,1:T(2,128)S(1)} %get-tuple-element.393), channel_id=1, source_target_pairs={{0,1},{1,2},{2,3},{3,4},{4,5},{5,6},{6,7},{7,8},{8,9},{9,10},{10,1... | collective-permute-start | bytes 24968 | tf_op jit(solution)/shard_map/ppermute | solution.py:50
  357.7 4.9 %collective-permute-start.48 = (f32[2,8,8,1]{3,0,2,1:T(2,128)S(1)}, f32[2,8,8,1]{3,0,2,1:T(2,128)S(1)}, u32[]{:S(2)}, u32[]{:S(2)}) collective-permute-start(f32[2,8,8,1]{3,0,2,1:T(2,128)S(1)} %get-tuple-element.457), channel_id=1, source_target_pairs={{0,16},{16,32},{32,48},{48,64},{64,80},{80,96},{96,112},{112,128},... | collective-permute-start | bytes 1544 | tf_op jit(solution)/shard_map/ppermute | solution.py:50
  358.9 3.9 collective-permute-start.49
  363.3 6.0 %collective-permute-start.51 = (f32[2,8,1,130]{3,0,2,1:T(2,128)S(1)}, f32[2,8,1,130]{3,0,2,1:T(2,128)S(1)}, u32[]{:S(2)}, u32[]{:S(2)}) collective-permute-start(f32[2,8,1,130]{3,0,2,1:T(2,128)S(1)} %get-tuple-element.391), channel_id=1, source_target_pairs={{0,1},{1,2},{2,3},{3,4},{4,5},{5,6},{6,7},{7,8},{8,9},{9,10},{10,1... | collective-permute-start | bytes 24968 | tf_op jit(solution)/shard_map/ppermute | solution.py:50
  369.9 5.8 %collective-permute-start.52 = (f32[1,8,8,1]{3,0,2,1:T(1,128)S(1)}, f32[1,8,8,1]{3,0,2,1:T(1,128)S(1)}, u32[]{:S(2)}, u32[]{:S(2)}) collective-permute-start(f32[1,8,8,1]{3,0,2,1:T(1,128)S(1)} %get-tuple-element.451), channel_id=1, source_target_pairs={{0,16},{16,32},{32,48},{48,64},{64,80},{80,96},{96,112},{112,128},... | collective-permute-start | bytes 776 | tf_op jit(solution)/shard_map/ppermute | solution.py:50
  370.8 5.1 %collective-permute-start.53 = (f32[1,8,8,1]{3,0,2,1:T(1,128)S(1)}, f32[1,8,8,1]{3,0,2,1:T(1,128)S(1)}, u32[]{:S(2)}, u32[]{:S(2)}) collective-permute-start(f32[1,8,8,1]{3,0,2,1:T(1,128)S(1)} %get-tuple-element.450), channel_id=1, source_target_pairs={{16,0},{32,16},{48,32},{64,48},{80,64},{96,80},{112,96},{128,112},... | collective-permute-start | bytes 776 | tf_op jit(solution)/shard_map/ppermute | solution.py:53
  376.1 5.9 %collective-permute-start.55 = (f32[1,8,1,130]{3,0,2,1:T(1,128)S(1)}, f32[1,8,1,130]{3,0,2,1:T(1,128)S(1)}, u32[]{:S(2)}, u32[]{:S(2)}) collective-permute-start(f32[1,8,1,130]{3,0,2,1:T(1,128)S(1)} %get-tuple-element.425), channel_id=1, source_target_pairs={{0,1},{1,2},{2,3},{3,4},{4,5},{5,6},{6,7},{7,8},{8,9},{9,10},{10,1... | collective-permute-start | bytes 12488 | tf_op jit(solution)/shard_map/ppermute | solution.py:50
  (283 other events, 712.4 us)
where the time goes:
time: 488 us; the launch traced here: 479 us
  blocking collectives  156 us (32%)
  starting transfers between devices  104 us (21%)
  other arithmetic  70.3 us (14%)
  waiting for transfers between devices  55.8 us (11%)
  local copies, waits for them, and re-layouts  50.7 us (10%)
  between operations  25.1 us (5%)
  matrix products  17.1 us (4%)
    psum x2, blocking collectives, local(): gram_matrix = lax.psum(local_gram, ('gx', 'gy'))  156 us
    ppermute x28, starting transfers between devices, padded_2(): lax.ppermute(lax.slice_in_dim(block, 0, width, axis=dim), axis, backward)  80.6 us
    unnamed x81, other arithmetic  41.9 us
    ppermute x28, waiting for transfers between devices, padded_2(): lax.ppermute(lax.slice_in_dim(block, block.shape[dim] - width, None, axis...  41.5 us
    ppermute x28, starting transfers between devices, padded_2(): lax.ppermute(lax.slice_in_dim(block, block.shape[dim] - width, None, axis...  23 us
    unnamed x538, local copies, waits for them, and re-layouts  22.3 us
    ppermute x28, waiting for transfers between devices, padded_2(): lax.ppermute(lax.slice_in_dim(block, 0, width, axis=dim), axis, backward)  14.2 us
  transfers between devices with their start and end apart: 56, of which 35 were waited for; matrix products, arithmetic and copies ran while one was open for 18% of the time, Pallas kernels for 0%

commit v1 on v0

v1 whole, which is shorter than its diff:
```python
import jax
import jax.numpy as jnp
from jax import lax
from jax.experimental import pallas as pl
from jax.experimental.pallas import tpu as pltpu
from jax.sharding import PartitionSpec as P

STEPS = 4
ITERS = 8

lattice_velocity = (
    (0, 0, 0),
    (0, 0, 1),
    (0, 0, -1),
    (0, 1, 0),
    (0, -1, 0),
    (1, 0, 0),
    (-1, 0, 0),
    (0, 1, 1),
    (0, -1, -1),
    (0, 1, -1),
    (0, -1, 1),
    (1, 0, 1),
    (-1, 0, -1),
    (1, 0, -1),
    (-1, 0, 1),
    (1, 1, 0),
    (-1, -1, 0),
    (1, -1, 0),
    (-1, 1, 0),
)
opposite = (0, 2, 1, 4, 3, 6, 5, 8, 7, 10, 9, 12, 11, 14, 13, 16, 15, 18, 17)
lattice_weight = (1.0 / 3.0,) + (1.0 / 18.0,) * 6 + (1.0 / 36.0,) * 12
relax_time = 1.25
force_scale = 0.05
valences = (1.0, -1.0, 2.0)
diffusivity = (0.05, 0.07, 0.03)
diag_coef = 6.0001
surface_scale = 2.0

FIELDS = 25
XT = 7
F_CONC, F_FLUID, F_POT, F_POT2 = 19, 22, 23, 24
SLABS = 9
TILE = (8, 128)


def lane_id():
    return lax.broadcasted_iota(jnp.int32, TILE, 1)


def row_id():
    return lax.broadcasted_iota(jnp.int32, TILE, 0)


def rl(v, amount):
    amount = amount % 128
    return v if amount == 0 else pltpu.roll(v, amount, 1)


def rs(v, amount):
    amount = amount % 8
    return v if amount == 0 else pltpu.roll(v, amount, 0)


def in_lanes(lane, start, width):
    return (lane >= start) & (lane < start + width)


def pack_kernel(pop, conc, pot, solid, x_left, x_right, y_down, y_up):
    lane, row = lane_id(), row_id()
    top = row < 4

    def tile(k, z):
        if k < F_CONC:
            return pop[k, z]
        if k < F_FLUID:
            return conc[k - F_CONC, z]
        if k == F_FLUID:
            return 1.0 - solid[z].astype(jnp.float32)
        return pot[z]

    for t in range(XT):
        left = right = jnp.zeros(TILE, jnp.float32)
        for q in range(4):
            k = 4 * t + q
            if k >= FIELDS:
                continue
            inner = 4 if k == F_POT2 else 0
            for z in range(8):
                v = tile(k, z)
                at = 16 * z + 4 * q
                here = in_lanes(lane, at, 4)
                left = jnp.where(here, rl(v, at - inner), left)
                right = jnp.where(here, rl(v, at - (124 - inner)), right)
        x_left[t] = left
        x_right[t] = right
    for k in range(FIELDS):
        for pair in range(4):
            a, b = tile(k, 2 * pair), tile(k, 2 * pair + 1)
            low = jnp.where(top, a, rs(b, 4))
            high = jnp.where(top, rs(a, 4), b)
            if k == F_POT2:
                low, high = high, low
            y_down[4 * k + pair] = low
            y_up[4 * k + pair] = high


def step_kernel(
    pop, conc, pot, solid, sign, up, down, from_right, from_left, corner_up, corner_down,
    pop_out, conc_out, edge_out,
    f, g, vel, cc, fluid, pt, mask, dpot, field,
):
    lane, row = lane_id(), row_id()
    top = row < 4
    slot = lane % 16
    first_row, last_row = row == 0, row == 7
    first_lane, last_lane = lane == 0, lane == 127

    def halves(k, z):
        u, d = up[4 * k + z // 2], down[4 * k + z // 2]
        if z % 2 == 0:
            return jnp.where(top, u, rs(d, 4))
        return jnp.where(top, rs(u, 4), d)

    def strip(k, tiles, low, high):
        q = k % 4
        out = jnp.where(slot < 4, rl(low, -4 * q), rl(high, 12 - 4 * q))
        for z in range(8):
            out = jnp.where(in_lanes(lane, 16 * z + 4, 4), rl(tiles[z], 16 * z + 4), out)
            out = jnp.where(in_lanes(lane, 16 * z + 8, 4), rl(tiles[z], 16 * z + 8 - 124), out)
        return out

    def load(k, own, put):
        t = k // 4
        a = [own(z) for z in range(8)]
        b = [halves(k, z) for z in range(8)]
        for z in range(8):
            put(2 * z, a[z])
            put(2 * z + 1, b[z])
        put(16, strip(k, a, from_left[t], from_right[t]))
        low = jnp.where(top, corner_up[XT + t], corner_down[XT + t])
        high = jnp.where(top, corner_up[t], corner_down[t])
        put(17, strip(k, b, low, high))

    def putter(ref, *index):
        def put(i, v):
            ref[(*index, i)] = v

        return put

    for k in range(19):
        load(k, lambda z, k=k: pop[k, z], putter(f, k))
    for k in range(3):
        load(F_CONC + k, lambda z, k=k: conc[k, z], putter(cc, 0, k))
    load(F_FLUID, lambda z: 1.0 - solid[z].astype(jnp.float32), putter(fluid))
    load(F_POT, lambda z: pot[z], putter(pt))

    def y_shift(a, b, cy):
        if cy == 0:
            return a, b
        edge = first_row if cy > 0 else last_row
        ra, rb = rs(a, cy), rs(b, cy)
        return jnp.where(edge, rb, ra), jnp.where(edge, ra, rb)

    def x_shift(v, side, z, cx):
        if cx > 0:
            return jnp.where(first_lane, rl(side, -(16 * z + 3)), rl(v, 1))
        return jnp.where(last_lane, rl(side, 127 - (16 * z + 12)), rl(v, -1))

    def shifted(get, offset):
        cz, cy, cx = offset
        side = y_shift(get(16), get(17), cy)
        out = []
        for z in range(8):
            source = (z - cz) % 8
            v = y_shift(get(2 * source), get(2 * source + 1), cy)
            if cx:
                v = tuple(x_shift(v[h], side[h], source, cx) for h in range(2))
            out.append(v)
        out.append(tuple(rl(side[h], 16 * cz + cx) for h in range(2)))
        return out

    for i in range(1, 19):
        moved = shifted(lambda s: fluid[s], lattice_velocity[i])
        for s in range(SLABS):
            for h in range(2):
                mask[i - 1, 2 * s + h] = moved[s][h] * fluid[2 * s + h]

    far = [halves(F_POT2, z) for z in range(8)]
    t2, q2 = F_POT2 // 4, F_POT2 % 4
    tp = F_POT // 4
    far_low = jnp.where(top, rs(corner_up[XT + tp], 4), rs(corner_down[XT + tp], 4))
    far_high = jnp.where(top, rs(corner_up[tp], 4), rs(corner_down[tp], 4))
    far.append(strip(F_POT, far, far_low, far_high))
    edge_low = (from_left[t2], jnp.where(top, corner_up[XT + t2], corner_down[XT + t2]))
    edge_high = (from_right[t2], jnp.where(top, corner_up[t2], corner_down[t2]))
    for axis in range(3):
        plus = tuple(1 if d == axis else 0 for d in range(3))
        minus = tuple(-p for p in plus)
        below = shifted(lambda s: pt[s], plus)
        above = shifted(lambda s: pt[s], minus)
        for s in range(SLABS):
            for h in range(2):
                lo, hi = below[s][h], above[s][h]
                if axis == 1 and h == 1:
                    lo = jnp.where(row == 4, rs(far[s], -3), lo)
                    hi = jnp.where(row == 3, rs(far[s], 3), hi)
                if axis == 2 and s == 8:
                    lo = jnp.where(slot == 0, rl(edge_low[h], -4 * q2 - 3), lo)
                    hi = jnp.where(slot == 15, rl(edge_high[h], 15 - 4 * q2), hi)
                here = pt[2 * s + h]
                dpot[2 * axis, 2 * s + h] = here - lo
                dpot[2 * axis + 1, 2 * s + h] = hi - here
                field[axis, 2 * s + h] = (0.5 * force_scale) * (lo - hi)

    pairs = [(i, i + 1) for i in range(1, 19, 2)]

    def collide(s, now):
        v = [f[i, s] for i in range(19)]
        total = {}
        delta = {}
        for a, b in pairs:
            total[a] = v[a] + v[b]
            delta[a] = v[a] - v[b]
        density = (
            v[0]
            + ((total[1] + total[3]) + (total[5] + total[7]))
            + ((total[9] + total[11]) + (total[13] + total[15]) + total[17])
        )
        momentum = (
            (delta[5] + delta[11]) + (delta[13] + delta[15]) + delta[17],
            (delta[3] + delta[7]) + (delta[9] + delta[15]) - delta[17],
            (delta[1] + delta[7]) - (delta[9] - delta[11]) - delta[13],
        )
        open_cell = fluid[s]
        charge = open_cell * (
            valences[0] * cc[now, 0, s] + valences[1] * cc[now, 1, s] + valences[2] * cc[now, 2, s]
        )
        force = [charge * field[d, s] for d in range(3)]
        inverse = 1.0 / density
        u = [(momentum[d] + 0.5 * force[d]) * inverse for d in range(3)]
        for d in range(3):
            vel[d, s] = u[d]
        speed = u[0] * u[0] + u[1] * u[1] + u[2] * u[2]
        work = u[0] * force[0] + u[1] * force[1] + u[2] * force[2]
        flow = [density * u[d] for d in range(3)]
        keep = 1.0 - 1.0 / relax_time
        gain = 1.0 / relax_time
        push = 1.0 - 0.5 / relax_time
        base = gain * density - (1.5 * gain) * (density * speed) - (3.0 * push) * work
        odd = [(3.0 * gain) * flow[d] + (3.0 * push) * force[d] for d in range(3)]
        even = [(4.5 * gain) * flow[d] + (9.0 * push) * force[d] for d in range(3)]
        is_open = open_cell > 0.5
        g[0, s] = jnp.where(is_open, keep * v[0] + lattice_weight[0] * base, v[0])

        def along(c, vector):
            running = None
            for d in range(3):
                if c[d] != 0:
                    if running is None:
                        running = vector[d] if c[d] > 0 else -vector[d]
                    else:
                        running = running + vector[d] if c[d] > 0 else running - vector[d]
            return running

        for a, b in pairs:
            c, w = lattice_velocity[a], lattice_weight[a]
            middle = base + along(c, u) * along(c, even)
            side = along(c, odd)
            g[a, s] = jnp.where(is_open, keep * v[a] + w * (middle + side), v[b])
            g[b, s] = jnp.where(is_open, keep * v[b] + w * (middle - side), v[a])

    def one_step(step, carry):
        now = lax.rem(step, 2)
        after = 1 - now

        def both(s, c):
            collide(2 * s, now)
            collide(2 * s + 1, now)
            return c

        lax.fori_loop(0, SLABS, both, 0)
        for s in range(2 * SLABS):
            f[0, s] = g[0, s]
        for i in range(1, 19):
            moved = shifted(lambda s, i=i: g[i, s], lattice_velocity[i])
            for s in range(SLABS):
                for h in range(2):
                    n = 2 * s + h
                    f[i, n] = jnp.where(mask[i - 1, n] > 0.5, moved[s][h], g[opposite[i], n])
        for k in range(3):
            for s in range(2 * SLABS):
                cc[after, k, s] = cc[now, k, s]
        for axis in range(3):
            plus = tuple(1 if d == axis else 0 for d in range(3))
            minus = tuple(-p for p in plus)
            lower = 2 * (2 - axis)
            v_low = shifted(lambda s: vel[axis, s], plus)
            v_high = shifted(lambda s: vel[axis, s], minus)
            for k in range(3):
                c_low = shifted(lambda s: cc[now, k, s], plus)
                c_high = shifted(lambda s: cc[now, k, s], minus)
                rate = diffusivity[k]
                drift = 0.5 * rate * valences[k]
                for s in range(SLABS):
                    for h in range(2):
                        n = 2 * s + h
                        here, v_here = cc[now, k, n], vel[axis, n]
                        lo, hi = c_low[s][h], c_high[s][h]
                        carry_low = 0.25 * (v_low[s][h] + v_here) - drift * dpot[2 * axis, n]
                        carry_high = 0.25 * (v_here + v_high[s][h]) - drift * dpot[2 * axis + 1, n]
                        flux_low = mask[lower, n] * (rate * (lo - here) + (lo + here) * carry_low)
                        flux_high = mask[lower + 1, n] * (rate * (here - hi) + (here + hi) * carry_high)
                        cc[after, k, n] = cc[after, k, n] - (flux_high - flux_low)
        return carry

    lax.fori_loop(0, STEPS, one_step, 0)

    last = STEPS % 2
    edge = jnp.zeros(TILE, jnp.float32)
    for z in range(8):
        n = 2 * z
        for i in range(19):
            pop_out[i, z] = f[i, n]
        c = [cc[last, k, n] for k in range(3)]
        for k in range(3):
            conc_out[k, z] = c[k]
        open_cell = fluid[n]
        target = open_cell * (
            valences[0] * c[0] + valences[1] * c[1] + valences[2] * c[2]
        ) + surface_scale * sign[z].astype(jnp.float32) * (1.0 - open_cell)
        spread = (
            (dpot[1, n] - dpot[0, n]) + (dpot[3, n] - dpot[2, n]) + (dpot[5, n] - dpot[4, n])
        )
        residual = target - ((diag_coef - 6.0) * pt[n] - spread)
        edge_out[z] = residual
        edge = jnp.where(in_lanes(lane, 16 * z, 8), rl(residual, 16 * z - 120), edge)
        edge = jnp.where(in_lanes(lane, 16 * z + 8, 8), rl(residual, 16 * z + 8), edge)
    edge_out[8] = edge


def levels_kernel(own, left, right, up, down, level_out, moment_out, lv):
    lane, row = lane_id(), row_id()
    slot = lane % 16
    first_row, last_row = row == 0, row == 7
    first_lane, last_lane = lane == 0, lane == 127
    sources = (
        (own, left[0], right[0]),
        (up, up[9], up[10]),
        (down, down[9], down[10]),
    )
    for r, (main, low, high) in enumerate(sources):
        for s in range(8):
            lv[0, r, s] = main[s]
        lv[0, r, 8] = jnp.where(slot < 8, low, main[8])
        lv[0, r, 9] = jnp.where(slot < 8, main[8], high)

    def around(j, r, s, low, high):
        v = lv[j, r, s]
        above, below = lv[j, (r + 1) % 3, s], lv[j, (r + 2) % 3, s]
        vertical = jnp.where(last_row, rs(above, -1), rs(v, -1)) + jnp.where(
            first_row, rs(below, 1), rs(v, 1)
        )
        if s < 8:
            across = jnp.where(first_lane, rl(low, -(16 * s + 7)), rl(v, 1)) + jnp.where(
                last_lane, rl(high, 127 - (16 * s + 8)), rl(v, -1)
            )
            return (lv[j, r, (s + 1) % 8] + lv[j, r, (s - 1) % 8]) + vertical + across
        return (rl(v, 16) + rl(v, -16)) + vertical + (rl(v, 1) + rl(v, -1))

    for j in range(ITERS):
        done = j == ITERS - 1
        squares = products = jnp.zeros(TILE, jnp.float32)
        for r in range(1 if done else 3):
            low, high = lv[j, r, 8], lv[j, r, 9]
            for s in range(8 if done else 10):
                total = around(j, r, s, low, high)
                if j == 0:
                    fresh = -total / 6.0
                else:
                    fresh = total * (-1.0 / 3.0) - lv[j - 1, r, s]
                if not done:
                    lv[j + 1, r, s] = fresh
                if r == 0 and s < 8:
                    here = lv[j, 0, s]
                    level_out[j, s] = here
                    squares = squares + here * here
                    products = products + here * fresh
        moment_out[j : j + 1, :] = jnp.sum(squares, axis=0, keepdims=True)
        moment_out[8 + j : 9 + j, :] = jnp.sum(products, axis=0, keepdims=True)


def combine_kernel(moments, levels, pot, out):
    sums = jnp.sum(moments[...], axis=1, keepdims=True)

    def entry(i):
        return jnp.broadcast_to(sums[i : i + 1, :], TILE)

    moment = [None] * 16
    moment[0], moment[1] = entry(0), entry(8)
    for k in range(1, ITERS):
        moment[2 * k] = 2.0 * entry(k) - moment[0]
        moment[2 * k + 1] = 2.0 * entry(8 + k) - moment[1]
    gram = {}
    for i in range(ITERS + 1):
        for j in range(i, ITERS + 1):
            if i + j < 16:
                gram[i, j] = gram[j, i] = 0.5 * (moment[i + j] + moment[j - i])

    def inner(a, b):
        running = None
        for i, x in enumerate(a):
            row = None
            for j, y in enumerate(b):
                term = gram[i, j] * y
                row = term if row is None else row + term
            row = x * row
            running = row if running is None else running + row
        return running

    one, zero = jnp.ones(TILE, jnp.float32), jnp.zeros(TILE, jnp.float32)
    search, rest, found = [one], [one], []
    left = moment[0]
    for k in range(ITERS):
        image = [zero] * (k + 2)
        for j in range(k + 1):
            image[j] = image[j] + diag_coef * search[j]
            if j == 0:
                image[1] = image[1] + 6.0 * search[0]
            else:
                image[j + 1] = image[j + 1] + 3.0 * search[j]
                image[j - 1] = image[j - 1] + 3.0 * search[j]
        length = left / inner(search, image)
        found = [
            (found[j] if j < len(found) else zero) + length * search[j] for j in range(k + 1)
        ]
        if k == ITERS - 1:
            break
        rest = [(rest[j] if j < k + 1 else zero) - length * image[j] for j in range(k + 2)]
        fresh = inner(rest, rest)
        ratio = fresh / left
        search = [rest[j] + (ratio * search[j] if j < k + 1 else zero) for j in range(k + 2)]
        left = fresh
    for z in range(8):
        running = found[0] * levels[0, z]
        for j in range(1, ITERS):
            running = running + found[j] * levels[j, z]
        out[z] = pot[z] + running


def in_vmem(count):
    return [pl.BlockSpec(memory_space=pltpu.VMEM)] * count


def f32(*shape):
    return jax.ShapeDtypeStruct(shape, jnp.float32)


def call(kernel, name, outs, scratch, *args):
    return pl.pallas_call(
        kernel,
        name=name,
        out_shape=outs,
        in_specs=in_vmem(len(args)),
        out_specs=in_vmem(len(outs)),
        scratch_shapes=[pltpu.VMEM(shape, jnp.float32) for shape in scratch],
        compiler_params=pltpu.CompilerParams(vmem_limit_bytes=48 << 20),
    )(*args)


def send(block, axis, step):
    count = lax.axis_size(axis)
    return lax.ppermute(block, axis, [(i, (i + step) % count) for i in range(count)])


def total_over(block, axis):
    count = lax.axis_size(axis)
    step = 1
    while step < count:
        if step * 4 <= count:
            parts = [
                lax.ppermute(block, axis, [(i, i ^ (k * step)) for i in range(count)])
                for k in (1, 2, 3)
            ]
            block = (block + parts[0]) + (parts[1] + parts[2])
            step *= 4
        else:
            block = block + lax.ppermute(block, axis, [(i, i ^ step) for i in range(count)])
            step *= 2
    return block


def local(populations, concentrations, potential, solid_mask, surface_sign):
    x_left, x_right, y_down, y_up = call(
        pack_kernel,
        "pack",
        (f32(XT, 8, 128), f32(XT, 8, 128), f32(4 * FIELDS, 8, 128), f32(4 * FIELDS, 8, 128)),
        [],
        populations,
        concentrations,
        potential,
        solid_mask,
    )
    up = send(y_down, "gy", -1)
    down = send(y_up, "gy", 1)
    from_right = send(x_left, "gx", -1)
    from_left = send(x_right, "gx", 1)
    corner = jnp.concatenate([from_right, from_left])
    corner_up = send(corner, "gy", -1)
    corner_down = send(corner, "gy", 1)
    n = 2 * SLABS
    pop_new, conc_new, edge = call(
        step_kernel,
        "steps",
        (f32(19, 8, 8, 128), f32(3, 8, 8, 128), f32(9, 8, 128)),
        [
            (19, n, 8, 128),
            (19, n, 8, 128),
            (3, n, 8, 128),
            (2, 3, n, 8, 128),
            (n, 8, 128),
            (n, 8, 128),
            (18, n, 8, 128),
            (6, n, 8, 128),
            (3, n, 8, 128),
        ],
        populations,
        concentrations,
        potential,
        solid_mask,
        surface_sign,
        up,
        down,
        from_right,
        from_left,
        corner_up,
        corner_down,
    )
    strip = edge[8:]
    left = send(strip, "gx", 1)
    right = send(strip, "gx", -1)
    wide = jnp.concatenate([edge, left, right])
    above = send(wide, "gy", -1)
    below = send(wide, "gy", 1)
    levels, moments = call(
        levels_kernel,
        "levels",
        (f32(ITERS, 8, 8, 128), f32(16, 128)),
        [(ITERS, 3, 10, 8, 128)],
        edge,
        left,
        right,
        above,
        below,
    )
    moments = total_over(total_over(moments, "gx"), "gy")
    (pot_new,) = call(combine_kernel, "combine", (f32(8, 8, 128),), [], moments, levels, potential)
    return (pop_new, conc_new, pot_new)


def solution(mesh):
    placed = (
        P(None, None, "gy", "gx"),
        P(None, None, "gy", "gx"),
        P(None, "gy", "gx"),
        P(None, "gy", "gx"),
        P(None, "gy", "gx"),
    )
    return jax.shard_map(
        local,
        mesh=mesh,
        in_specs=placed,
        out_specs=(P(None, None, "gy", "gx"), P(None, None, "gy", "gx"), P(None, "gy", "gx")),
        check_vma=False,
    )
```

time: 488 us -> 81.7 us (0.17)
  the two profiles are of different devices: /device:TPU:1 before, /device:TPU:64 now
where the time goes in v1:
time: 81.7 us; the launch traced here: 81.4 us
  starting transfers between devices  36.7 us (45%)
  waiting for transfers between devices  28.1 us (34%)
  Pallas kernels  12.4 us (15%)
  local copies, waits for them, and re-layouts  3.49 us (4%)
    ppermute x12, starting transfers between devices, total_over(): lax.ppermute(block, axis, [(i, i ^ k * step) for i in range(count)])  19.6 us
    ppermute x10, starting transfers between devices, send(): lax.ppermute(block, axis, [(i, (i + step) % count) for i in range(count)])  17.1 us
    ppermute x10, waiting for transfers between devices, send(): lax.ppermute(block, axis, [(i, (i + step) % count) for i in range(count)])  14.2 us
    ppermute x12, waiting for transfers between devices, total_over(): lax.ppermute(block, axis, [(i, i ^ k * step) for i in range(count)])  14 us
    pallas_call x4, Pallas kernels, call(): pl.pallas_call(kernel, name=name, out_shape=outs, in_specs=in_vmem(len(ar...  12.4 us
    unnamed x13, local copies, waits for them, and re-layouts  3.49 us
  transfers between devices with their start and end apart: 22, of which 13 were waited for; matrix products, arithmetic and copies ran while one was open for 0% of the time, Pallas kernels for 0%

profile of v1, /device:TPU:64, one launch (start us, length us, event | category | flops | bytes accessed | tf_op | source)
XLA Modules:
  0.0 81.4 jit_solution(13758411182587490227)
XLA Ops:
  0.6 1.1 %copy-done = f32[19,8,8,128]{3,2,1,0:T(8,128)S(1)} copy-done((f32[19,8,8,128]{3,2,1,0:T(8,128)S(1)}, f32[19,8,8,128]{3,2,1,0:T(8,128)}, u32[]{:S(2)}) %copy-start) | copy-done | bytes 622616
  1.7 0.9 %copy-done.1 = f32[3,8,8,128]{3,2,1,0:T(8,128)S(1)} copy-done((f32[3,8,8,128]{3,2,1,0:T(8,128)S(1)}, f32[3,8,8,128]{3,2,1,0:T(8,128)}, u32[]{:S(2)}) %copy-start.1) | copy-done | bytes 98328
  2.6 0.8 copy-done.2
  3.4 0.8 copy-done.3
  4.1 0.5 pack.1
  4.6 5.3 %collective-permute-start = (f32[100,8,128]{2,1,0:T(8,128)S(1)}, f32[100,8,128]{2,1,0:T(8,128)S(1)}, u32[]{:S(2)}, u32[]{:S(2)}) collective-permute-start(f32[100,8,128]{2,1,0:T(8,128)S(1)} %get-tuple-element.12), channel_id=1, source_target_pairs={{0,15},{1,0},{2,1},{3,2},{4,3},{5,4},{6,5},{7,6},{8,7},{9,8},{10,9... | collective-permute-start | bytes 1228808 | tf_op jit(solution)/shard_map/ppermute | solution.py:474
  9.9 0.0 collective-permute-start.1
  9.9 0.0 collective-permute-start.2
  9.9 0.5 collective-permute-start.3
  10.4 1.1 %collective-permute-done.2.from_right = f32[7,8,128]{2,1,0:T(8,128)S(1)} collective-permute-done((f32[7,8,128]{2,1,0:T(8,128)S(1)}, f32[7,8,128]{2,1,0:T(8,128)S(1)}, u32[]{:S(2)}, u32[]{:S(2)}) %collective-permute-start.2) | collective-permute-done | bytes 28704 | tf_op jit(solution)/shard_map/ppermute | solution.py:474
  11.5 1.7 %collective-permute-done.3.from_left = f32[7,8,128]{2,1,0:T(8,128)S(1)} collective-permute-done((f32[7,8,128]{2,1,0:T(8,128)S(1)}, f32[7,8,128]{2,1,0:T(8,128)S(1)}, u32[]{:S(2)}, u32[]{:S(2)}) %collective-permute-start.3) | collective-permute-done | bytes 28704 | tf_op jit(solution)/shard_map/ppermute | solution.py:474
  13.2 0.0 collective-permute-start.5
  13.2 5.3 %collective-permute-start.4 = (f32[14,8,128]{2,1,0:T(8,128)S(1)}, f32[14,8,128]{2,1,0:T(8,128)S(1)}, u32[]{:S(2)}, u32[]{:S(2)}) collective-permute-start(f32[14,8,128]{2,1,0:T(8,128)S(1)} %constant_dynamic-update-slice_fusion), channel_id=1, source_target_pairs={{0,15},{1,0},{2,1},{3,2},{4,3},{5,4},{6,5},{7,6},{8,7},{9,8},{10,9... | collective-permute-start | bytes 172040 | tf_op jit(solution)/shard_map/ppermute | solution.py:474
  18.6 6.8 %collective-permute-done.5.corner_down = f32[14,8,128]{2,1,0:T(8,128)S(1)} collective-permute-done((f32[14,8,128]{2,1,0:T(8,128)S(1)}, f32[14,8,128]{2,1,0:T(8,128)S(1)}, u32[]{:S(2)}, u32[]{:S(2)}) %collective-permute-start.5) | collective-permute-done | bytes 57376 | tf_op jit(solution)/shard_map/ppermute | solution.py:474
  25.4 9.8 %steps.1 = (f32[19,8,8,128]{3,2,1,0:T(8,128)}, f32[3,8,8,128]{3,2,1,0:T(8,128)}, f32[9,8,128]{2,1,0:T(8,128)S(1)}) custom-call(f32[19,8,8,128]{3,2,1,0:T(8,128)S(1)} %copy-done, f32[3,8,8,128]{3,2,1,0:T(8,128)S(1)} %copy-done.1, f32[8,8,128]{2,1,0:T(8,128)S(1)} %copy-done.2, s32[8,8,128]{2,1,0:T(8,128)S(1)} %copy-done.3, s32[8,8,128]{2,1,0:T(8,128)S(1)} %copy-done.4, ...), custom_call_target="tpu_custom_call" | custom-call | tf_op jit(solution)/shard_map/steps/pallas_call | solution.py:461
  35.2 0.0 collective-permute-start.7
  35.2 0.5 collective-permute-start.6
  35.7 2.5 %collective-permute-done.6.left = f32[1,8,128]{2,1,0:T(8,128)S(1)} collective-permute-done((f32[1,8,128]{2,1,0:T(8,128)S(1)}, f32[1,8,128]{2,1,0:T(8,128)S(1)}, u32[]{:S(2)}, u32[]{:S(2)}) %collective-permute-start.6) | collective-permute-done | bytes 4128 | tf_op jit(solution)/shard_map/ppermute | solution.py:474
  38.3 0.1 collective-permute-start.9
  38.3 5.3 %collective-permute-start.8 = (f32[11,8,128]{2,1,0:T(8,128)S(1)}, f32[11,8,128]{2,1,0:T(8,128)S(1)}, u32[]{:S(2)}, u32[]{:S(2)}) collective-permute-start(f32[11,8,128]{2,1,0:T(8,128)S(1)} %constant_dynamic-update-slice_fusion.2), channel_id=1, source_target_pairs={{0,15},{1,0},{2,1},{3,2},{4,3},{5,4},{6,5},{7,6},{8,7},{9,8},{10,9... | collective-permute-start | bytes 135176 | tf_op jit(solution)/shard_map/ppermute | solution.py:474
  43.7 2.0 %collective-permute-done.9.down = f32[11,8,128]{2,1,0:T(8,128)S(1)} collective-permute-done((f32[11,8,128]{2,1,0:T(8,128)S(1)}, f32[11,8,128]{2,1,0:T(8,128)S(1)}, u32[]{:S(2)}, u32[]{:S(2)}) %collective-permute-start.9) | collective-permute-done | bytes 45088 | tf_op jit(solution)/shard_map/ppermute | solution.py:474
  45.7 0.0 collective-permute-done.8.up
  45.7 1.0 %levels.1 = (f32[8,8,8,128]{3,2,1,0:T(8,128)S(1)}, f32[16,128]{1,0:T(8,128)S(1)}) custom-call(f32[9,8,128]{2,1,0:T(8,128)S(1)} %get-tuple-element.18.own, f32[1,8,128]{2,1,0:T(8,128)S(1)} %collective-permute-done.6.left, f32[1,8,128]{2,1,0:T(8,128)S(1)} %collective-permute-done.7.right, f32[11,8,128]{2,1,0:T(8,128)S(1)} %collective-permute-done.8.up, ...), custom_call_target="tpu_custom_call" | custom-call | tf_op jit(solution)/shard_map/levels/pallas_call | solution.py:461
  46.7 1.9 %collective-permute-start.12 = (f32[16,128]{1,0:T(8,128)S(1)}, f32[16,128]{1,0:T(8,128)S(1)}, u32[]{:S(2)}, u32[]{:S(2)}) collective-permute-start(f32[16,128]{1,0:T(8,128)S(1)} %get-tuple-element.19), channel_id=1, source_target_pairs={{0,48},{16,32},{32,16},{48,0},{64,112},{80,96},{96,80},{112,64},{1... | collective-permute-start | bytes 24584 | tf_op jit(solution)/shard_map/ppermute | solution.py:483
  48.6 0.3 collective-permute-start.11
  48.9 0.0 collective-permute-start.10
  48.9 1.1 %collective-permute-done.12 = f32[16,128]{1,0:T(8,128)S(1)} collective-permute-done((f32[16,128]{1,0:T(8,128)S(1)}, f32[16,128]{1,0:T(8,128)S(1)}, u32[]{:S(2)}, u32[]{:S(2)}) %collective-permute-start.12) | collective-permute-done | bytes 8224 | tf_op jit(solution)/shard_map/ppermute | solution.py:483
  50.0 2.3 %collective-permute-done.11 = f32[16,128]{1,0:T(8,128)S(1)} collective-permute-done((f32[16,128]{1,0:T(8,128)S(1)}, f32[16,128]{1,0:T(8,128)S(1)}, u32[]{:S(2)}, u32[]{:S(2)}) %collective-permute-start.11) | collective-permute-done | bytes 8224 | tf_op jit(solution)/shard_map/ppermute | solution.py:483
  52.2 0.0 collective-permute-done.10
  52.3 4.1 %collective-permute-start.15 = (f32[16,128]{1,0:T(8,128)S(1)}, f32[16,128]{1,0:T(8,128)S(1)}, u32[]{:S(2)}, u32[]{:S(2)}) collective-permute-start(f32[16,128]{1,0:T(8,128)S(1)} %add_add_fusion.3), channel_id=1, source_target_pairs={{0,192},{16,208},{32,224},{48,240},{64,128},{80,144},{96,160},{112... | collective-permute-start | bytes 24584 | tf_op jit(solution)/shard_map/ppermute | solution.py:483
  56.3 2.8 %collective-permute-start.14 = (f32[16,128]{1,0:T(8,128)S(1)}, f32[16,128]{1,0:T(8,128)S(1)}, u32[]{:S(2)}, u32[]{:S(2)}) collective-permute-start(f32[16,128]{1,0:T(8,128)S(1)} %add_add_fusion.3), channel_id=1, source_target_pairs={{0,128},{16,144},{32,160},{48,176},{64,192},{80,208},{96,224},{112... | collective-permute-start | bytes 24584 | tf_op jit(solution)/shard_map/ppermute | solution.py:483
  59.2 0.0 collective-permute-start.13
  59.2 0.0 collective-permute-done.15
  59.2 4.7 %collective-permute-done.14 = f32[16,128]{1,0:T(8,128)S(1)} collective-permute-done((f32[16,128]{1,0:T(8,128)S(1)}, f32[16,128]{1,0:T(8,128)S(1)}, u32[]{:S(2)}, u32[]{:S(2)}) %collective-permute-start.14) | collective-permute-done | bytes 8224 | tf_op jit(solution)/shard_map/ppermute | solution.py:483
  63.9 0.0 collective-permute-done.13
  63.9 0.1 collective-permute-start.18
  64.0 0.1 collective-permute-start.17
  64.1 4.0 %collective-permute-start.16 = (f32[16,128]{1,0:T(8,128)S(1)}, f32[16,128]{1,0:T(8,128)S(1)}, u32[]{:S(2)}, u32[]{:S(2)}) collective-permute-start(f32[16,128]{1,0:T(8,128)S(1)} %add_add_fusion.2), channel_id=1, source_target_pairs={{0,1},{1,0},{2,3},{3,2},{4,5},{5,4},{6,7},{7,6},{8,9},{9,8},{10,11... | collective-permute-start | bytes 24584 | tf_op jit(solution)/shard_map/ppermute | solution.py:483
  68.1 0.8 collective-permute-done.18
  68.8 0.4 collective-permute-done.17
  69.2 0.6 collective-permute-done.16
  69.8 5.3 %collective-permute-start.21 = (f32[16,128]{1,0:T(8,128)S(1)}, f32[16,128]{1,0:T(8,128)S(1)}, u32[]{:S(2)}, u32[]{:S(2)}) collective-permute-start(f32[16,128]{1,0:T(8,128)S(1)} %add_add_fusion.1), channel_id=1, source_target_pairs={{0,12},{1,13},{2,14},{3,15},{4,8},{5,9},{6,10},{7,11},{8,4},{9,5},... | collective-permute-start | bytes 24584 | tf_op jit(solution)/shard_map/ppermute | solution.py:483
  75.1 0.0 collective-permute-start.20
  75.1 1.0 %collective-permute-start.19 = (f32[16,128]{1,0:T(8,128)S(1)}, f32[16,128]{1,0:T(8,128)S(1)}, u32[]{:S(2)}, u32[]{:S(2)}) collective-permute-start(f32[16,128]{1,0:T(8,128)S(1)} %add_add_fusion.1), channel_id=1, source_target_pairs={{0,4},{1,5},{2,6},{3,7},{4,0},{5,1},{6,2},{7,3},{8,12},{9,13},{10,... | collective-permute-start | bytes 24584 | tf_op jit(solution)/shard_map/ppermute | solution.py:483
  76.1 0.7 collective-permute-done.21
  76.8 3.5 %collective-permute-done.20 = f32[16,128]{1,0:T(8,128)S(1)} collective-permute-done((f32[16,128]{1,0:T(8,128)S(1)}, f32[16,128]{1,0:T(8,128)S(1)}, u32[]{:S(2)}, u32[]{:S(2)}) %collective-permute-start.20) | collective-permute-done | bytes 8224 | tf_op jit(solution)/shard_map/ppermute | solution.py:483
  80.3 0.0 collective-permute-done.19
  80.3 1.1 %combine.1 = f32[8,8,128]{2,1,0:T(8,128)} custom-call(f32[16,128]{1,0:T(8,128)S(1)} %add_add_fusion.moments, f32[8,8,8,128]{3,2,1,0:T(8,128)S(1)} %get-tuple-element.20.levels, f32[8,8,128]{2,1,0:T(8,128)S(1)} %copy-done.2), custom_call_target="tpu_custom_call" | custom-call | tf_op jit(solution)/shard_map/combine/pallas_call | solution.py:461
  (20 shorter events, 0.1 us)
Async XLA Ops:
  0.6 1.1 %copy-start = (f32[19,8,8,128]{3,2,1,0:T(8,128)S(1)}, f32[19,8,8,128]{3,2,1,0:T(8,128)}, u32[]{:S(2)}) copy-start(f32[19,8,8,128]{3,2,1,0:T(8,128)} %pop.3) | copy-start | bytes 1867780
  1.7 0.9 %copy-start.1 = (f32[3,8,8,128]{3,2,1,0:T(8,128)S(1)}, f32[3,8,8,128]{3,2,1,0:T(8,128)}, u32[]{:S(2)}) copy-start(f32[3,8,8,128]{3,2,1,0:T(8,128)} %conc.3) | copy-start | bytes 294916
  2.6 0.8 copy-start.2
  3.4 0.8 copy-start.3
  4.6 20.8 %collective-permute-start = (f32[100,8,128]{2,1,0:T(8,128)S(1)}, f32[100,8,128]{2,1,0:T(8,128)S(1)}, u32[]{:S(2)}, u32[]{:S(2)}) collective-permute-start(f32[100,8,128]{2,1,0:T(8,128)S(1)} %get-tuple-element.12), channel_id=1, source_target_pairs={{0,15},{1,0},{2,1},{3,2},{4,3},{5,4},{6,5},{7,6},{8,7},{9,8},{10,9... | collective-permute-start | bytes 1228808 | tf_op jit(solution)/shard_map/ppermute | solution.py:474
  9.9 15.5 %collective-permute-start.1 = (f32[100,8,128]{2,1,0:T(8,128)S(1)}, f32[100,8,128]{2,1,0:T(8,128)S(1)}, u32[]{:S(2)}, u32[]{:S(2)}) collective-permute-start(f32[100,8,128]{2,1,0:T(8,128)S(1)} %get-tuple-element.13), channel_id=1, source_target_pairs={{0,1},{1,2},{2,3},{3,4},{4,5},{5,6},{6,7},{7,8},{8,9},{9,10},{10,1... | collective-permute-start | bytes 1228808 | tf_op jit(solution)/shard_map/ppermute | solution.py:474
  9.9 1.6 %collective-permute-start.2 = (f32[7,8,128]{2,1,0:T(8,128)S(1)}, f32[7,8,128]{2,1,0:T(8,128)S(1)}, u32[]{:S(2)}, u32[]{:S(2)}) collective-permute-start(f32[7,8,128]{2,1,0:T(8,128)S(1)} %get-tuple-element.14), channel_id=1, source_target_pairs={{0,240},{16,0},{32,16},{48,32},{64,48},{80,64},{96,80},{112,96},{1... | collective-permute-start | bytes 86024 | tf_op jit(solution)/shard_map/ppermute | solution.py:474
  9.9 3.3 %collective-permute-start.3 = (f32[7,8,128]{2,1,0:T(8,128)S(1)}, f32[7,8,128]{2,1,0:T(8,128)S(1)}, u32[]{:S(2)}, u32[]{:S(2)}) collective-permute-start(f32[7,8,128]{2,1,0:T(8,128)S(1)} %get-tuple-element.15), channel_id=1, source_target_pairs={{0,16},{16,32},{32,48},{48,64},{64,80},{80,96},{96,112},{112,128},... | collective-permute-start | bytes 86024 | tf_op jit(solution)/shard_map/ppermute | solution.py:474
  11.5 13.9 %copy-start.4 = (s32[8,8,128]{2,1,0:T(8,128)S(1)}, s32[8,8,128]{2,1,0:T(8,128)}, u32[]{:S(2)}) copy-start(s32[8,8,128]{2,1,0:T(8,128)} %sign.1) | copy-start | bytes 98308
  13.2 12.2 %collective-permute-start.5 = (f32[14,8,128]{2,1,0:T(8,128)S(1)}, f32[14,8,128]{2,1,0:T(8,128)S(1)}, u32[]{:S(2)}, u32[]{:S(2)}) collective-permute-start(f32[14,8,128]{2,1,0:T(8,128)S(1)} %constant_dynamic-update-slice_fusion), channel_id=1, source_target_pairs={{0,1},{1,2},{2,3},{3,4},{4,5},{5,6},{6,7},{7,8},{8,9},{9,10},{10,1... | collective-permute-start | bytes 172040 | tf_op jit(solution)/shard_map/ppermute | solution.py:474
  13.2 12.2 %collective-permute-start.4 = (f32[14,8,128]{2,1,0:T(8,128)S(1)}, f32[14,8,128]{2,1,0:T(8,128)S(1)}, u32[]{:S(2)}, u32[]{:S(2)}) collective-permute-start(f32[14,8,128]{2,1,0:T(8,128)S(1)} %constant_dynamic-update-slice_fusion), channel_id=1, source_target_pairs={{0,15},{1,0},{2,1},{3,2},{4,3},{5,4},{6,5},{7,6},{8,7},{9,8},{10,9... | collective-permute-start | bytes 172040 | tf_op jit(solution)/shard_map/ppermute | solution.py:474
  35.2 3.0 %collective-permute-start.7 = (f32[1,8,128]{2,1,0:T(8,128)S(1)}, f32[1,8,128]{2,1,0:T(8,128)S(1)}, u32[]{:S(2)}, u32[]{:S(2)}) collective-permute-start(f32[1,8,128]{2,1,0:T(8,128)S(1)} %slice.3), channel_id=1, source_target_pairs={{0,240},{16,0},{32,16},{48,32},{64,48},{80,64},{96,80},{112,96},{1... | collective-permute-start | bytes 12296 | tf_op jit(solution)/shard_map/ppermute | solution.py:474
  35.2 3.0 %collective-permute-start.6 = (f32[1,8,128]{2,1,0:T(8,128)S(1)}, f32[1,8,128]{2,1,0:T(8,128)S(1)}, u32[]{:S(2)}, u32[]{:S(2)}) collective-permute-start(f32[1,8,128]{2,1,0:T(8,128)S(1)} %slice.3), channel_id=1, source_target_pairs={{0,16},{16,32},{32,48},{48,64},{64,80},{80,96},{96,112},{112,128},... | collective-permute-start | bytes 12296 | tf_op jit(solution)/shard_map/ppermute | solution.py:474
  38.3 7.4 %collective-permute-start.9 = (f32[11,8,128]{2,1,0:T(8,128)S(1)}, f32[11,8,128]{2,1,0:T(8,128)S(1)}, u32[]{:S(2)}, u32[]{:S(2)}) collective-permute-start(f32[11,8,128]{2,1,0:T(8,128)S(1)} %constant_dynamic-update-slice_fusion.2), channel_id=1, source_target_pairs={{0,1},{1,2},{2,3},{3,4},{4,5},{5,6},{6,7},{7,8},{8,9},{9,10},{10,1... | collective-permute-start | bytes 135176 | tf_op jit(solution)/shard_map/ppermute | solution.py:474
  38.3 7.4 %collective-permute-start.8 = (f32[11,8,128]{2,1,0:T(8,128)S(1)}, f32[11,8,128]{2,1,0:T(8,128)S(1)}, u32[]{:S(2)}, u32[]{:S(2)}) collective-permute-start(f32[11,8,128]{2,1,0:T(8,128)S(1)} %constant_dynamic-update-slice_fusion.2), channel_id=1, source_target_pairs={{0,15},{1,0},{2,1},{3,2},{4,3},{5,4},{6,5},{7,6},{8,7},{9,8},{10,9... | collective-permute-start | bytes 135176 | tf_op jit(solution)/shard_map/ppermute | solution.py:474
  46.7 3.3 %collective-permute-start.12 = (f32[16,128]{1,0:T(8,128)S(1)}, f32[16,128]{1,0:T(8,128)S(1)}, u32[]{:S(2)}, u32[]{:S(2)}) collective-permute-start(f32[16,128]{1,0:T(8,128)S(1)} %get-tuple-element.19), channel_id=1, source_target_pairs={{0,48},{16,32},{32,16},{48,0},{64,112},{80,96},{96,80},{112,64},{1... | collective-permute-start | bytes 24584 | tf_op jit(solution)/shard_map/ppermute | solution.py:483
  48.6 3.7 %collective-permute-start.11 = (f32[16,128]{1,0:T(8,128)S(1)}, f32[16,128]{1,0:T(8,128)S(1)}, u32[]{:S(2)}, u32[]{:S(2)}) collective-permute-start(f32[16,128]{1,0:T(8,128)S(1)} %get-tuple-element.19), channel_id=1, source_target_pairs={{0,32},{16,48},{32,0},{48,16},{64,96},{80,112},{96,64},{112,80},{1... | collective-permute-start | bytes 24584 | tf_op jit(solution)/shard_map/ppermute | solution.py:483
  48.9 3.4 %collective-permute-start.10 = (f32[16,128]{1,0:T(8,128)S(1)}, f32[16,128]{1,0:T(8,128)S(1)}, u32[]{:S(2)}, u32[]{:S(2)}) collective-permute-start(f32[16,128]{1,0:T(8,128)S(1)} %get-tuple-element.19), channel_id=1, source_target_pairs={{0,16},{16,0},{32,48},{48,32},{64,80},{80,64},{96,112},{112,96},{1... | collective-permute-start | bytes 24584 | tf_op jit(solution)/shard_map/ppermute | solution.py:483
  52.3 6.9 %collective-permute-start.15 = (f32[16,128]{1,0:T(8,128)S(1)}, f32[16,128]{1,0:T(8,128)S(1)}, u32[]{:S(2)}, u32[]{:S(2)}) collective-permute-start(f32[16,128]{1,0:T(8,128)S(1)} %add_add_fusion.3), channel_id=1, source_target_pairs={{0,192},{16,208},{32,224},{48,240},{64,128},{80,144},{96,160},{112... | collective-permute-start | bytes 24584 | tf_op jit(solution)/shard_map/ppermute | solution.py:483
  56.3 7.6 %collective-permute-start.14 = (f32[16,128]{1,0:T(8,128)S(1)}, f32[16,128]{1,0:T(8,128)S(1)}, u32[]{:S(2)}, u32[]{:S(2)}) collective-permute-start(f32[16,128]{1,0:T(8,128)S(1)} %add_add_fusion.3), channel_id=1, source_target_pairs={{0,128},{16,144},{32,160},{48,176},{64,192},{80,208},{96,224},{112... | collective-permute-start | bytes 24584 | tf_op jit(solution)/shard_map/ppermute | solution.py:483
  59.2 4.7 %collective-permute-start.13 = (f32[16,128]{1,0:T(8,128)S(1)}, f32[16,128]{1,0:T(8,128)S(1)}, u32[]{:S(2)}, u32[]{:S(2)}) collective-permute-start(f32[16,128]{1,0:T(8,128)S(1)} %add_add_fusion.3), channel_id=1, source_target_pairs={{0,64},{16,80},{32,96},{48,112},{64,0},{80,16},{96,32},{112,48},{1... | collective-permute-start | bytes 24584 | tf_op jit(solution)/shard_map/ppermute | solution.py:483
  63.9 4.9 %collective-permute-start.18 = (f32[16,128]{1,0:T(8,128)S(1)}, f32[16,128]{1,0:T(8,128)S(1)}, u32[]{:S(2)}, u32[]{:S(2)}) collective-permute-start(f32[16,128]{1,0:T(8,128)S(1)} %add_add_fusion.2), channel_id=1, source_target_pairs={{0,3},{1,2},{2,1},{3,0},{4,7},{5,6},{6,5},{7,4},{8,11},{9,10},{10,... | collective-permute-start | bytes 24584 | tf_op jit(solution)/shard_map/ppermute | solution.py:483
  64.0 5.2 %collective-permute-start.17 = (f32[16,128]{1,0:T(8,128)S(1)}, f32[16,128]{1,0:T(8,128)S(1)}, u32[]{:S(2)}, u32[]{:S(2)}) collective-permute-start(f32[16,128]{1,0:T(8,128)S(1)} %add_add_fusion.2), channel_id=1, source_target_pairs={{0,2},{1,3},{2,0},{3,1},{4,6},{5,7},{6,4},{7,5},{8,10},{9,11},{10,... | collective-permute-start | bytes 24584 | tf_op jit(solution)/shard_map/ppermute | solution.py:483
  64.1 5.7 %collective-permute-start.16 = (f32[16,128]{1,0:T(8,128)S(1)}, f32[16,128]{1,0:T(8,128)S(1)}, u32[]{:S(2)}, u32[]{:S(2)}) collective-permute-start(f32[16,128]{1,0:T(8,128)S(1)} %add_add_fusion.2), channel_id=1, source_target_pairs={{0,1},{1,0},{2,3},{3,2},{4,5},{5,4},{6,7},{7,6},{8,9},{9,8},{10,11... | collective-permute-start | bytes 24584 | tf_op jit(solution)/shard_map/ppermute | solution.py:483
  69.8 7.0 %collective-permute-start.21 = (f32[16,128]{1,0:T(8,128)S(1)}, f32[16,128]{1,0:T(8,128)S(1)}, u32[]{:S(2)}, u32[]{:S(2)}) collective-permute-start(f32[16,128]{1,0:T(8,128)S(1)} %add_add_fusion.1), channel_id=1, source_target_pairs={{0,12},{1,13},{2,14},{3,15},{4,8},{5,9},{6,10},{7,11},{8,4},{9,5},... | collective-permute-start | bytes 24584 | tf_op jit(solution)/shard_map/ppermute | solution.py:483
  75.1 5.2 %collective-permute-start.20 = (f32[16,128]{1,0:T(8,128)S(1)}, f32[16,128]{1,0:T(8,128)S(1)}, u32[]{:S(2)}, u32[]{:S(2)}) collective-permute-start(f32[16,128]{1,0:T(8,128)S(1)} %add_add_fusion.1), channel_id=1, source_target_pairs={{0,8},{1,9},{2,10},{3,11},{4,12},{5,13},{6,14},{7,15},{8,0},{9,1},... | collective-permute-start | bytes 24584 | tf_op jit(solution)/shard_map/ppermute | solution.py:483
  75.1 5.2 %collective-permute-start.19 = (f32[16,128]{1,0:T(8,128)S(1)}, f32[16,128]{1,0:T(8,128)S(1)}, u32[]{:S(2)}, u32[]{:S(2)}) collective-permute-start(f32[16,128]{1,0:T(8,128)S(1)} %add_add_fusion.1), channel_id=1, source_target_pairs={{0,4},{1,5},{2,6},{3,7},{4,0},{5,1},{6,2},{7,3},{8,12},{9,13},{10,... | collective-permute-start | bytes 24584 | tf_op jit(solution)/shard_map/ppermute | solution.py:483

commit v2 on v1

--- a/solution.py
+++ b/solution.py
@@ -67,9 +67,19 @@
     return (lane >= start) & (lane < start + width)
 
 
-def pack_kernel(pop, conc, pot, solid, x_left, x_right, y_down, y_up):
+def pack_kernel(*refs):
+    sources, copies = refs[:5], refs[5:10]
+    x_left, x_right, y_down, y_up, sems = refs[10:]
+    moves = [
+        pltpu.make_async_copy(sources[i], copies[i], sems.at[i]) for i in (0, 1, 2, 3, 4)
+    ]
+    for move in moves:
+        move.start()
+    pop, conc, pot, solid = copies[:4]
     lane, row = lane_id(), row_id()
     top = row < 4
+    for move in moves:
+        move.wait()
 
     def tile(k, z):
         if k < F_CONC:
@@ -106,16 +116,44 @@
             y_up[4 * k + pair] = high
 
 
+def y_shift(a, b, cy, halves=(0, 1)):
+    if cy == 0:
+        return a, b
+    edge = row_id() == (0 if cy > 0 else 7)
+    ra, rb = rs(a, cy), rs(b, cy)
+    return tuple(jnp.where(edge, rb, ra) if h == 0 else jnp.where(edge, ra, rb) for h in halves)
+
+
+def x_shift(v, side, z, cx):
+    if cx > 0:
+        return jnp.where(lane_id() == 0, rl(side, -(16 * z + 3)), rl(v, 1))
+    return jnp.where(lane_id() == 127, rl(side, 127 - (16 * z + 12)), rl(v, -1))
+
+
+def shifted(get, offset, own=False):
+    cz, cy, cx = offset
+    halves = (0,) if own else (0, 1)
+    side = y_shift(get(16), get(17), cy, halves) if cx or not own else None
+    out = []
+    for z in range(8):
+        source = (z - cz) % 8
+        v = y_shift(get(2 * source), get(2 * source + 1), cy, halves)
+        if cx:
+            v = tuple(x_shift(v[h], side[h], source, cx) for h in halves)
+        out.append(v)
+    if not own:
+        out.append(tuple(rl(side[h], 16 * cz + cx) for h in halves))
+    return out
+
+
 def step_kernel(
     pop, conc, pot, solid, sign, up, down, from_right, from_left, corner_up, corner_down,
-    pop_out, conc_out, edge_out,
-    f, g, vel, cc, fluid, pt, mask, dpot, field,
+    g, mask, conc_out, edge_out,
+    f, vel, cc, fluid, pt, dpot, field, speed_up, flux,
 ):
     lane, row = lane_id(), row_id()
     top = row < 4
     slot = lane % 16
-    first_row, last_row = row == 0, row == 7
-    first_lane, last_lane = lane == 0, lane == 127
 
     def halves(k, z):
         u, d = up[4 * k + z // 2], down[4 * k + z // 2]
@@ -155,31 +193,6 @@
         load(F_CONC + k, lambda z, k=k: conc[k, z], putter(cc, 0, k))
     load(F_FLUID, lambda z: 1.0 - solid[z].astype(jnp.float32), putter(fluid))
     load(F_POT, lambda z: pot[z], putter(pt))
-
-    def y_shift(a, b, cy):
-        if cy == 0:
-            return a, b
-        edge = first_row if cy > 0 else last_row
-        ra, rb = rs(a, cy), rs(b, cy)
-        return jnp.where(edge, rb, ra), jnp.where(edge, ra, rb)
-
-    def x_shift(v, side, z, cx):
-        if cx > 0:
-            return jnp.where(first_lane, rl(side, -(16 * z + 3)), rl(v, 1))
-        return jnp.where(last_lane, rl(side, 127 - (16 * z + 12)), rl(v, -1))
-
-    def shifted(get, offset):
-        cz, cy, cx = offset
-        side = y_shift(get(16), get(17), cy)
-        out = []
-        for z in range(8):
-            source = (z - cz) % 8
-            v = y_shift(get(2 * source), get(2 * source + 1), cy)
-            if cx:
-                v = tuple(x_shift(v[h], side[h], source, cx) for h in range(2))
-            out.append(v)
-        out.append(tuple(rl(side[h], 16 * cz + cx) for h in range(2)))
-        return out
 
     for i in range(1, 19):
         moved = shifted(lambda s: fluid[s], lattice_velocity[i])
@@ -209,6 +222,8 @@
                 if axis == 2 and s == 8:
                     lo = jnp.where(slot == 0, rl(edge_low[h], -4 * q2 - 3), lo)
                     hi = jnp.where(slot == 15, rl(edge_high[h], 15 - 4 * q2), hi)
+                    for z in range(8):
+                        hi = jnp.where(lane == 16 * z + 7, rl(pt[2 * z + h], 16 * z + 3), hi)
                 here = pt[2 * s + h]
                 dpot[2 * axis, 2 * s + h] = here - lo
                 dpot[2 * axis + 1, 2 * s + h] = hi - here
@@ -271,16 +286,15 @@
             g[a, s] = jnp.where(is_open, keep * v[a] + w * (middle + side), v[b])
             g[b, s] = jnp.where(is_open, keep * v[b] + w * (middle - side), v[a])
 
-    def one_step(step, carry):
-        now = lax.rem(step, 2)
-        after = 1 - now
-
+    def collide_all(now):
         def both(s, c):
             collide(2 * s, now)
             collide(2 * s + 1, now)
             return c
 
         lax.fori_loop(0, SLABS, both, 0)
+
+    def stream():
         for s in range(2 * SLABS):
             f[0, s] = g[0, s]
         for i in range(1, 19):
@@ -289,40 +303,50 @@
                 for h in range(2):
                     n = 2 * s + h
                     f[i, n] = jnp.where(mask[i - 1, n] > 0.5, moved[s][h], g[opposite[i], n])
-        for k in range(3):
-            for s in range(2 * SLABS):
-                cc[after, k, s] = cc[now, k, s]
+
+    def ions(now, after, own=False):
         for axis in range(3):
             plus = tuple(1 if d == axis else 0 for d in range(3))
             minus = tuple(-p for p in plus)
-            lower = 2 * (2 - axis)
-            v_low = shifted(lambda s: vel[axis, s], plus)
+            upper = 2 * (2 - axis) + 1
             v_high = shifted(lambda s: vel[axis, s], minus)
+            for s in range(SLABS):
+                for h in range(2):
+                    n = 2 * s + h
+                    speed_up[n] = 0.25 * (vel[axis, n] + v_high[s][h])
             for k in range(3):
-                c_low = shifted(lambda s: cc[now, k, s], plus)
                 c_high = shifted(lambda s: cc[now, k, s], minus)
                 rate = diffusivity[k]
                 drift = 0.5 * rate * valences[k]
                 for s in range(SLABS):
                     for h in range(2):
                         n = 2 * s + h
-                        here, v_here = cc[now, k, n], vel[axis, n]
-                        lo, hi = c_low[s][h], c_high[s][h]
-                        carry_low = 0.25 * (v_low[s][h] + v_here) - drift * dpot[2 * axis, n]
-                        carry_high = 0.25 * (v_here + v_high[s][h]) - drift * dpot[2 * axis + 1, n]
-                        flux_low = mask[lower, n] * (rate * (lo - here) + (lo + here) * carry_low)
-                        flux_high = mask[lower + 1, n] * (rate * (here - hi) + (here + hi) * carry_high)
-                        cc[after, k, n] = cc[after, k, n] - (flux_high - flux_low)
+                        here, hi = cc[now, k, n], c_high[s][h]
+                        pull = speed_up[n] - drift * dpot[2 * axis + 1, n]
+                        flux[k, n] = mask[upper, n] * (rate * (here - hi) + (here + hi) * pull)
+                low = shifted(lambda s: flux[k, s], plus, own)
+                for s in range(8 if own else SLABS):
+                    for h in range(1 if own else 2):
+                        n = 2 * s + h
+                        before = cc[now if axis == 0 else after, k, n]
+                        cc[after, k, n] = before - (flux[k, n] - low[s][h])
+
+    def one_step(step, carry):
+        now = lax.rem(step, 2)
+        collide_all(now)
+        stream()
+        ions(now, 1 - now)
         return carry
 
-    lax.fori_loop(0, STEPS, one_step, 0)
+    lax.fori_loop(0, STEPS - 1, one_step, 0)
+    final = (STEPS - 1) % 2
+    collide_all(final)
+    ions(final, 1 - final, own=True)
 
     last = STEPS % 2
     edge = jnp.zeros(TILE, jnp.float32)
     for z in range(8):
         n = 2 * z
-        for i in range(19):
-            pop_out[i, z] = f[i, n]
         c = [cc[last, k, n] for k in range(3)]
         for k in range(3):
             conc_out[k, z] = c[k]
@@ -340,7 +364,16 @@
     edge_out[8] = edge
 
 
-def levels_kernel(own, left, right, up, down, level_out, moment_out, lv):
+def finish_kernel(g, mask, pop_out):
+    for z in range(8):
+        pop_out[0, z] = g[0, 2 * z]
+    for i in range(1, 19):
+        moved = shifted(lambda s, i=i: g[i, s], lattice_velocity[i], own=True)
+        for z in range(8):
+            pop_out[i, z] = jnp.where(mask[i - 1, 2 * z] > 0.5, moved[z][0], g[opposite[i], 2 * z])
+
+
+def levels_kernel(own, left, right, up, down, level_out, row_out, lv, part):
     lane, row = lane_id(), row_id()
     slot = lane % 16
     first_row, last_row = row == 0, row == 7
@@ -387,12 +420,22 @@
                     level_out[j, s] = here
                     squares = squares + here * here
                     products = products + here * fresh
-        moment_out[j : j + 1, :] = jnp.sum(squares, axis=0, keepdims=True)
-        moment_out[8 + j : 9 + j, :] = jnp.sum(products, axis=0, keepdims=True)
-
-
-def combine_kernel(moments, levels, pot, out):
-    sums = jnp.sum(moments[...], axis=1, keepdims=True)
+        part[j : j + 1, :] = jnp.sum(squares, axis=0, keepdims=True)
+        part[8 + j : 9 + j, :] = jnp.sum(products, axis=0, keepdims=True)
+    sums = jnp.sum(part[...], axis=1, keepdims=True)
+    diagonal = lax.broadcasted_iota(jnp.int32, (16, 128), 0) == lax.broadcasted_iota(
+        jnp.int32, (16, 128), 1
+    )
+    one_row = jnp.sum(jnp.where(diagonal, sums, 0.0), axis=0, keepdims=True)
+    row_out[...] = jnp.broadcast_to(one_row, row_out.shape)
+
+
+def combine_kernel(rows, levels, pot, out):
+    total = jnp.broadcast_to(jnp.sum(rows[...], axis=0, keepdims=True), (16, 128))
+    diagonal = lax.broadcasted_iota(jnp.int32, (16, 128), 0) == lax.broadcasted_iota(
+        jnp.int32, (16, 128), 1
+    )
+    sums = jnp.sum(jnp.where(diagonal, total, 0.0), axis=1, keepdims=True)
 
     def entry(i):
         return jnp.broadcast_to(sums[i : i + 1, :], TILE)
@@ -457,14 +500,17 @@
     return jax.ShapeDtypeStruct(shape, jnp.float32)
 
 
-def call(kernel, name, outs, scratch, *args):
+def call(kernel, name, outs, scratch, *args, in_specs=None):
     return pl.pallas_call(
         kernel,
         name=name,
         out_shape=outs,
-        in_specs=in_vmem(len(args)),
+        in_specs=in_specs or in_vmem(len(args)),
         out_specs=in_vmem(len(outs)),
-        scratch_shapes=[pltpu.VMEM(shape, jnp.float32) for shape in scratch],
+        scratch_shapes=[
+            pltpu.VMEM(shape, jnp.float32) if isinstance(shape, tuple) else shape
+            for shape in scratch
+        ],
         compiler_params=pltpu.CompilerParams(vmem_limit_bytes=48 << 20),
     )(*args)
 
@@ -474,34 +520,18 @@
     return lax.ppermute(block, axis, [(i, (i + step) % count) for i in range(count)])
 
 
-def total_over(block, axis):
-    count = lax.axis_size(axis)
-    step = 1
-    while step < count:
-        if step * 4 <= count:
-            parts = [
-                lax.ppermute(block, axis, [(i, i ^ (k * step)) for i in range(count)])
-                for k in (1, 2, 3)
-            ]
-            block = (block + parts[0]) + (parts[1] + parts[2])
-            step *= 4
-        else:
-            block = block + lax.ppermute(block, axis, [(i, i ^ step) for i in range(count)])
-            step *= 2
-    return block
-
-
 def local(populations, concentrations, potential, solid_mask, surface_sign):
-    x_left, x_right, y_down, y_up = call(
+    inputs = (populations, concentrations, potential, solid_mask, surface_sign)
+    packed = call(
         pack_kernel,
         "pack",
-        (f32(XT, 8, 128), f32(XT, 8, 128), f32(4 * FIELDS, 8, 128), f32(4 * FIELDS, 8, 128)),
-        [],
-        populations,
-        concentrations,
-        potential,
-        solid_mask,
-    )
+        tuple(jax.ShapeDtypeStruct(a.shape, a.dtype) for a in inputs)
+        + (f32(XT, 8, 128), f32(XT, 8, 128), f32(4 * FIELDS, 8, 128), f32(4 * FIELDS, 8, 128)),
+        [pltpu.SemaphoreType.DMA((5,))],
+        *inputs,
+        in_specs=[pl.BlockSpec(memory_space=pltpu.HBM)] * 5,
+    )
+    kept, (x_left, x_right, y_down, y_up) = packed[:5], packed[5:]
     up = send(y_down, "gy", -1)
     down = send(y_up, "gy", 1)
     from_right = send(x_left, "gx", -1)
@@ -510,26 +540,22 @@
     corner_up = send(corner, "gy", -1)
     corner_down = send(corner, "gy", 1)
     n = 2 * SLABS
-    pop_new, conc_new, edge = call(
+    relaxed, mask, conc_new, edge = call(
         step_kernel,
         "steps",
-        (f32(19, 8, 8, 128), f32(3, 8, 8, 128), f32(9, 8, 128)),
+        (f32(19, n, 8, 128), f32(18, n, 8, 128), f32(3, 8, 8, 128), f32(9, 8, 128)),
         [
-            (19, n, 8, 128),
             (19, n, 8, 128),
             (3, n, 8, 128),
             (2, 3, n, 8, 128),
             (n, 8, 128),
             (n, 8, 128),
-            (18, n, 8, 128),
             (6, n, 8, 128),
             (3, n, 8, 128),
+            (n, 8, 128),
+            (3, n, 8, 128),
         ],
-        populations,
-        concentrations,
-        potential,
-        solid_mask,
-        surface_sign,
+        *kept,
         up,
         down,
         from_right,
@@ -540,22 +566,24 @@
     strip = edge[8:]
     left = send(strip, "gx", 1)
     right = send(strip, "gx", -1)
+    (pop_new,) = call(finish_kernel, "finish", (f32(19, 8, 8, 128),), [], relaxed, mask)
     wide = jnp.concatenate([edge, left, right])
     above = send(wide, "gy", -1)
     below = send(wide, "gy", 1)
-    levels, moments = call(
+    devices = lax.axis_size("gx") * lax.axis_size("gy")
+    levels, rows = call(
         levels_kernel,
         "levels",
-        (f32(ITERS, 8, 8, 128), f32(16, 128)),
-        [(ITERS, 3, 10, 8, 128)],
+        (f32(ITERS, 8, 8, 128), f32(devices, 128)),
+        [(ITERS, 3, 10, 8, 128), (16, 128)],
         edge,
         left,
         right,
         above,
         below,
     )
-    moments = total_over(total_over(moments, "gx"), "gy")
-    (pot_new,) = call(combine_kernel, "combine", (f32(8, 8, 128),), [], moments, levels, potential)
+    rows = lax.all_to_all(rows, ("gx", "gy"), 0, 0, tiled=True)
+    (pot_new,) = call(combine_kernel, "combine", (f32(8, 8, 128),), [], rows, levels, kept[2])
     return (pop_new, conc_new, pot_new)
 
 

time: 81.7 us -> 78.8 us (0.965)
  the two profiles are of different devices: /device:TPU:64 before, /device:TPU:1 now
where the time goes in v2:
time: 78.8 us; the launch traced here: 78.4 us
  starting transfers between devices  35.9 us (46%)
  waiting for transfers between devices  23.9 us (30%)
  Pallas kernels  13.7 us (17%)
  local copies, waits for them, and re-layouts  4.25 us (5%)
    ppermute x10, starting transfers between devices, send(): lax.ppermute(block, axis, [(i, (i + step) % count) for i in range(count)])  21.4 us
    all_to_all x1, starting transfers between devices, local(): rows = lax.all_to_all(rows, ('gx', 'gy'), 0, 0, tiled=True)  14.5 us
    pallas_call x5, Pallas kernels, call(): pl.pallas_call(kernel, name=name, out_shape=outs, in_specs=in_specs or in...  13.7 us
    all_to_all x1, waiting for transfers between devices, local(): rows = lax.all_to_all(rows, ('gx', 'gy'), 0, 0, tiled=True)  12 us
    ppermute x10, waiting for transfers between devices, send(): lax.ppermute(block, axis, [(i, (i + step) % count) for i in range(count)])  11.9 us
    unnamed x13, local copies, waits for them, and re-layouts  4.24 us
  transfers between devices with their start and end apart: 11, of which 6 were waited for; matrix products, arithmetic and copies ran while one was open for 0% of the time, Pallas kernels for 1%

profile of v2, /device:TPU:1, one launch (start us, length us, event | category | flops | bytes accessed | tf_op | source)
XLA Modules:
  0.0 78.4 jit_solution(932412842976815963)
XLA Ops:
  0.6 0.0 copy-start
  0.6 1.1 %copy-done = f32[19,8,8,128]{3,2,1,0:T(8,128)S(1)} copy-done((f32[19,8,8,128]{3,2,1,0:T(8,128)S(1)}, f32[19,8,8,128]{3,2,1,0:T(8,128)}, u32[]{:S(2)}) %copy-start) | copy-done | bytes 622616
  1.7 0.0 copy-start.1
  1.7 0.9 %copy-done.1 = f32[3,8,8,128]{3,2,1,0:T(8,128)S(1)} copy-done((f32[3,8,8,128]{3,2,1,0:T(8,128)S(1)}, f32[3,8,8,128]{3,2,1,0:T(8,128)}, u32[]{:S(2)}) %copy-start.1) | copy-done | bytes 98328
  2.6 0.0 copy-start.2
  2.6 0.8 copy-done.2
  3.4 0.0 copy-start.3
  3.4 0.8 copy-done.3
  4.1 0.0 copy-start.4
  4.1 0.8 copy-done.4
  4.9 1.0 %pack.1 = (f32[19,8,8,128]{3,2,1,0:T(8,128)S(1)}, f32[3,8,8,128]{3,2,1,0:T(8,128)S(1)}, f32[8,8,128]{2,1,0:T(8,128)S(1)}, s32[8,8,128]{2,1,0:T(8,128)S(1)}, s32[...) custom-call(f32[19,8,8,128]{3,2,1,0:T(8,128)S(1)} %copy-done, ...), custom_call_target="tpu_custom_call" | custom-call | tf_op jit(solution)/shard_map/pack/pallas_call | solution.py:504
  5.9 5.8 %collective-permute-start = (f32[100,8,128]{2,1,0:T(8,128)S(1)}, f32[100,8,128]{2,1,0:T(8,128)S(1)}, u32[]{:S(2)}, u32[]{:S(2)}) collective-permute-start(f32[100,8,128]{2,1,0:T(8,128)S(1)} %get-tuple-element.23), channel_id=1, source_target_pairs={{0,15},{1,0},{2,1},{3,2},{4,3},{5,4},{6,5},{7,6},{8,7},{9,8},{10,9... | collective-permute-start | bytes 1228808 | tf_op jit(solution)/shard_map/ppermute | solution.py:520
  11.7 0.0 collective-permute-start.1
  11.7 1.0 %collective-permute-start.2 = (f32[7,8,128]{2,1,0:T(8,128)S(1)}, f32[7,8,128]{2,1,0:T(8,128)S(1)}, u32[]{:S(2)}, u32[]{:S(2)}) collective-permute-start(f32[7,8,128]{2,1,0:T(8,128)S(1)} %get-tuple-element.25), channel_id=1, source_target_pairs={{0,240},{16,0},{32,16},{48,32},{64,48},{80,64},{96,80},{112,96},{1... | collective-permute-start | bytes 86024 | tf_op jit(solution)/shard_map/ppermute | solution.py:520
  12.7 1.5 %collective-permute-start.3 = (f32[7,8,128]{2,1,0:T(8,128)S(1)}, f32[7,8,128]{2,1,0:T(8,128)S(1)}, u32[]{:S(2)}, u32[]{:S(2)}) collective-permute-start(f32[7,8,128]{2,1,0:T(8,128)S(1)} %get-tuple-element.26), channel_id=1, source_target_pairs={{0,16},{16,32},{32,48},{48,64},{64,80},{80,96},{96,112},{112,128},... | collective-permute-start | bytes 86024 | tf_op jit(solution)/shard_map/ppermute | solution.py:520
  14.2 1.8 %collective-permute-done.2.from_right = f32[7,8,128]{2,1,0:T(8,128)S(1)} collective-permute-done((f32[7,8,128]{2,1,0:T(8,128)S(1)}, f32[7,8,128]{2,1,0:T(8,128)S(1)}, u32[]{:S(2)}, u32[]{:S(2)}) %collective-permute-start.2) | collective-permute-done | bytes 28704 | tf_op jit(solution)/shard_map/ppermute | solution.py:520
  16.0 2.3 %collective-permute-done.3.from_left = f32[7,8,128]{2,1,0:T(8,128)S(1)} collective-permute-done((f32[7,8,128]{2,1,0:T(8,128)S(1)}, f32[7,8,128]{2,1,0:T(8,128)S(1)}, u32[]{:S(2)}, u32[]{:S(2)}) %collective-permute-start.3) | collective-permute-done | bytes 28704 | tf_op jit(solution)/shard_map/ppermute | solution.py:520
  18.4 0.0 collective-permute-start.5
  18.4 4.8 %collective-permute-start.4 = (f32[14,8,128]{2,1,0:T(8,128)S(1)}, f32[14,8,128]{2,1,0:T(8,128)S(1)}, u32[]{:S(2)}, u32[]{:S(2)}) collective-permute-start(f32[14,8,128]{2,1,0:T(8,128)S(1)} %constant_dynamic-update-slice_fusion), channel_id=1, source_target_pairs={{0,15},{1,0},{2,1},{3,2},{4,3},{5,4},{6,5},{7,6},{8,7},{9,8},{10,9... | collective-permute-start | bytes 172040 | tf_op jit(solution)/shard_map/ppermute | solution.py:520
  23.2 3.1 %collective-permute-done.5.corner_down = f32[14,8,128]{2,1,0:T(8,128)S(1)} collective-permute-done((f32[14,8,128]{2,1,0:T(8,128)S(1)}, f32[14,8,128]{2,1,0:T(8,128)S(1)}, u32[]{:S(2)}, u32[]{:S(2)}) %collective-permute-start.5) | collective-permute-done | bytes 57376 | tf_op jit(solution)/shard_map/ppermute | solution.py:520
  26.3 0.0 collective-permute-done.4.corner_up
  26.3 0.0 collective-permute-done.up
  26.3 0.0 collective-permute-done.1.down
  26.3 8.8 %steps.1 = (f32[19,18,8,128]{3,2,1,0:T(8,128)S(1)}, f32[18,18,8,128]{3,2,1,0:T(8,128)S(1)}, f32[3,8,8,128]{3,2,1,0:T(8,128)}, f32[9,8,128]{2,1,0:T(8,128)S(1)}) custom-call(f32[19,8,8,128]{3,2,1,0:T(8,128)S(1)} %get-tuple-element.18.pop, f32[3,8,8,128]{3,2,1,0:T(8,128)S(1)} %get-tuple-element.19.conc, f32[8,8,128]{2,1,0:T(8,128)S(1)} %get-tuple-element.20.pot, ...), custom_call_target="tpu_custom_call" | custom-call | tf_op jit(solution)/shard_map/steps/pallas_call | solution.py:504
  35.1 3.4 %collective-permute-start.7 = (f32[1,8,128]{2,1,0:T(8,128)S(1)}, f32[1,8,128]{2,1,0:T(8,128)S(1)}, u32[]{:S(2)}, u32[]{:S(2)}) collective-permute-start(f32[1,8,128]{2,1,0:T(8,128)S(1)} %slice.3), channel_id=1, source_target_pairs={{0,240},{16,0},{32,16},{48,32},{64,48},{80,64},{96,80},{112,96},{1... | collective-permute-start | bytes 12296 | tf_op jit(solution)/shard_map/ppermute | solution.py:520
  38.5 0.0 collective-permute-start.6
  38.5 3.2 %collective-permute-done.6.left = f32[1,8,128]{2,1,0:T(8,128)S(1)} collective-permute-done((f32[1,8,128]{2,1,0:T(8,128)S(1)}, f32[1,8,128]{2,1,0:T(8,128)S(1)}, u32[]{:S(2)}, u32[]{:S(2)}) %collective-permute-start.6) | collective-permute-done | bytes 4128 | tf_op jit(solution)/shard_map/ppermute | solution.py:520
  41.7 0.0 collective-permute-done.7.right
  41.7 0.1 collective-permute-start.9
  41.8 4.8 %collective-permute-start.8 = (f32[11,8,128]{2,1,0:T(8,128)S(1)}, f32[11,8,128]{2,1,0:T(8,128)S(1)}, u32[]{:S(2)}, u32[]{:S(2)}) collective-permute-start(f32[11,8,128]{2,1,0:T(8,128)S(1)} %constant_dynamic-update-slice_fusion.2), channel_id=1, source_target_pairs={{0,15},{1,0},{2,1},{3,2},{4,3},{5,4},{6,5},{7,6},{8,7},{9,8},{10,9... | collective-permute-start | bytes 135176 | tf_op jit(solution)/shard_map/ppermute | solution.py:520
  46.6 1.4 %collective-permute-done.9.down = f32[11,8,128]{2,1,0:T(8,128)S(1)} collective-permute-done((f32[11,8,128]{2,1,0:T(8,128)S(1)}, f32[11,8,128]{2,1,0:T(8,128)S(1)}, u32[]{:S(2)}, u32[]{:S(2)}) %collective-permute-start.9) | collective-permute-done | bytes 45088 | tf_op jit(solution)/shard_map/ppermute | solution.py:520
  48.0 0.0 collective-permute-done.8.up
  48.0 1.8 %levels.1 = (f32[8,8,8,128]{3,2,1,0:T(8,128)S(1)}, f32[256,128]{1,0:T(8,128)}) custom-call(f32[9,8,128]{2,1,0:T(8,128)S(1)} %get-tuple-element.30.own, f32[1,8,128]{2,1,0:T(8,128)S(1)} %collective-permute-done.6.left, f32[1,8,128]{2,1,0:T(8,128)S(1)} %collective-permute-done.7.right, f32[11,8,128]{2,1,0:T(8,128)S(1)} %collective-permute-done.8.up, ...), custom_call_target="tpu_custom_call" | custom-call | tf_op jit(solution)/shard_map/levels/pallas_call | solution.py:504
  49.8 14.5 %all-to-all-start = ((f32[256,1,128]{2,1,0:T(1,128)}), f32[256,1,128]{2,1,0:T(1,128)S(1)}, u32[]{:S(2)}, u32[]{:S(2)}) async-start(f32[256,1,128]{2,1,0:T(1,128)} %bitcast.1), calls=%async_computation | async-start | bytes 262144 | tf_op jit(solution)/shard_map/all_to_all | solution.py:585
  64.2 1.1 %finish.1 = f32[19,8,8,128]{3,2,1,0:T(8,128)} custom-call(f32[19,18,8,128]{3,2,1,0:T(8,128)S(1)} %get-tuple-element.27.g, f32[18,18,8,128]{3,2,1,0:T(8,128)S(1)} %get-tuple-element.28.mask), custom_call_target="tpu_custom_call" | custom-call | tf_op jit(solution)/shard_map/finish/pallas_call | solution.py:504
  65.3 12.0 %all-to-all-done = f32[256,1,128]{2,1,0:T(1,128)S(1)} async-done(((f32[256,1,128]{2,1,0:T(1,128)}), f32[256,1,128]{2,1,0:T(1,128)S(1)}, u32[]{:S(2)}, u32[]{:S(2)}) %all-to-all-start) | async-done | bytes 131104 | tf_op jit(solution)/shard_map/all_to_all | solution.py:585
  77.3 1.1 %combine.1 = f32[8,8,128]{2,1,0:T(8,128)} custom-call(f32[256,128]{1,0:T(8,128)S(1)} %bitcast.4, f32[8,8,8,128]{3,2,1,0:T(8,128)S(1)} %get-tuple-element.32.levels, f32[8,8,128]{2,1,0:T(8,128)S(1)} %get-tuple-element.20.pot), custom_call_target="tpu_custom_call" | custom-call | tf_op jit(solution)/shard_map/combine/pallas_call | solution.py:504
  (6 shorter events, 0.0 us)
Async XLA Ops:
  0.6 1.1 %copy-start = (f32[19,8,8,128]{3,2,1,0:T(8,128)S(1)}, f32[19,8,8,128]{3,2,1,0:T(8,128)}, u32[]{:S(2)}) copy-start(f32[19,8,8,128]{3,2,1,0:T(8,128)} %refs_0_.1) | copy-start | bytes 1867780
  1.7 0.9 %copy-start.1 = (f32[3,8,8,128]{3,2,1,0:T(8,128)S(1)}, f32[3,8,8,128]{3,2,1,0:T(8,128)}, u32[]{:S(2)}) copy-start(f32[3,8,8,128]{3,2,1,0:T(8,128)} %refs_1_.1) | copy-start | bytes 294916
  2.6 0.8 copy-start.2
  3.4 0.8 copy-start.3
  4.1 0.8 copy-start.4
  5.9 20.4 %collective-permute-start = (f32[100,8,128]{2,1,0:T(8,128)S(1)}, f32[100,8,128]{2,1,0:T(8,128)S(1)}, u32[]{:S(2)}, u32[]{:S(2)}) collective-permute-start(f32[100,8,128]{2,1,0:T(8,128)S(1)} %get-tuple-element.23), channel_id=1, source_target_pairs={{0,15},{1,0},{2,1},{3,2},{4,3},{5,4},{6,5},{7,6},{8,7},{9,8},{10,9... | collective-permute-start | bytes 1228808 | tf_op jit(solution)/shard_map/ppermute | solution.py:520
  11.7 14.6 %collective-permute-start.1 = (f32[100,8,128]{2,1,0:T(8,128)S(1)}, f32[100,8,128]{2,1,0:T(8,128)S(1)}, u32[]{:S(2)}, u32[]{:S(2)}) collective-permute-start(f32[100,8,128]{2,1,0:T(8,128)S(1)} %get-tuple-element.24), channel_id=1, source_target_pairs={{0,1},{1,2},{2,3},{3,4},{4,5},{5,6},{6,7},{7,8},{8,9},{9,10},{10,1... | collective-permute-start | bytes 1228808 | tf_op jit(solution)/shard_map/ppermute | solution.py:520
  11.7 4.3 %collective-permute-start.2 = (f32[7,8,128]{2,1,0:T(8,128)S(1)}, f32[7,8,128]{2,1,0:T(8,128)S(1)}, u32[]{:S(2)}, u32[]{:S(2)}) collective-permute-start(f32[7,8,128]{2,1,0:T(8,128)S(1)} %get-tuple-element.25), channel_id=1, source_target_pairs={{0,240},{16,0},{32,16},{48,32},{64,48},{80,64},{96,80},{112,96},{1... | collective-permute-start | bytes 86024 | tf_op jit(solution)/shard_map/ppermute | solution.py:520
  12.7 5.7 %collective-permute-start.3 = (f32[7,8,128]{2,1,0:T(8,128)S(1)}, f32[7,8,128]{2,1,0:T(8,128)S(1)}, u32[]{:S(2)}, u32[]{:S(2)}) collective-permute-start(f32[7,8,128]{2,1,0:T(8,128)S(1)} %get-tuple-element.26), channel_id=1, source_target_pairs={{0,16},{16,32},{32,48},{48,64},{64,80},{80,96},{96,112},{112,128},... | collective-permute-start | bytes 86024 | tf_op jit(solution)/shard_map/ppermute | solution.py:520
  18.4 7.9 %collective-permute-start.5 = (f32[14,8,128]{2,1,0:T(8,128)S(1)}, f32[14,8,128]{2,1,0:T(8,128)S(1)}, u32[]{:S(2)}, u32[]{:S(2)}) collective-permute-start(f32[14,8,128]{2,1,0:T(8,128)S(1)} %constant_dynamic-update-slice_fusion), channel_id=1, source_target_pairs={{0,1},{1,2},{2,3},{3,4},{4,5},{5,6},{6,7},{7,8},{8,9},{9,10},{10,1... | collective-permute-start | bytes 172040 | tf_op jit(solution)/shard_map/ppermute | solution.py:520
  18.4 7.9 %collective-permute-start.4 = (f32[14,8,128]{2,1,0:T(8,128)S(1)}, f32[14,8,128]{2,1,0:T(8,128)S(1)}, u32[]{:S(2)}, u32[]{:S(2)}) collective-permute-start(f32[14,8,128]{2,1,0:T(8,128)S(1)} %constant_dynamic-update-slice_fusion), channel_id=1, source_target_pairs={{0,15},{1,0},{2,1},{3,2},{4,3},{5,4},{6,5},{7,6},{8,7},{9,8},{10,9... | collective-permute-start | bytes 172040 | tf_op jit(solution)/shard_map/ppermute | solution.py:520
  35.1 6.6 %collective-permute-start.7 = (f32[1,8,128]{2,1,0:T(8,128)S(1)}, f32[1,8,128]{2,1,0:T(8,128)S(1)}, u32[]{:S(2)}, u32[]{:S(2)}) collective-permute-start(f32[1,8,128]{2,1,0:T(8,128)S(1)} %slice.3), channel_id=1, source_target_pairs={{0,240},{16,0},{32,16},{48,32},{64,48},{80,64},{96,80},{112,96},{1... | collective-permute-start | bytes 12296 | tf_op jit(solution)/shard_map/ppermute | solution.py:520
  38.5 3.2 %collective-permute-start.6 = (f32[1,8,128]{2,1,0:T(8,128)S(1)}, f32[1,8,128]{2,1,0:T(8,128)S(1)}, u32[]{:S(2)}, u32[]{:S(2)}) collective-permute-start(f32[1,8,128]{2,1,0:T(8,128)S(1)} %slice.3), channel_id=1, source_target_pairs={{0,16},{16,32},{32,48},{48,64},{64,80},{80,96},{96,112},{112,128},... | collective-permute-start | bytes 12296 | tf_op jit(solution)/shard_map/ppermute | solution.py:520
  41.7 6.3 %collective-permute-start.9 = (f32[11,8,128]{2,1,0:T(8,128)S(1)}, f32[11,8,128]{2,1,0:T(8,128)S(1)}, u32[]{:S(2)}, u32[]{:S(2)}) collective-permute-start(f32[11,8,128]{2,1,0:T(8,128)S(1)} %constant_dynamic-update-slice_fusion.2), channel_id=1, source_target_pairs={{0,1},{1,2},{2,3},{3,4},{4,5},{5,6},{6,7},{7,8},{8,9},{9,10},{10,1... | collective-permute-start | bytes 135176 | tf_op jit(solution)/shard_map/ppermute | solution.py:520
  41.8 6.2 %collective-permute-start.8 = (f32[11,8,128]{2,1,0:T(8,128)S(1)}, f32[11,8,128]{2,1,0:T(8,128)S(1)}, u32[]{:S(2)}, u32[]{:S(2)}) collective-permute-start(f32[11,8,128]{2,1,0:T(8,128)S(1)} %constant_dynamic-update-slice_fusion.2), channel_id=1, source_target_pairs={{0,15},{1,0},{2,1},{3,2},{4,3},{5,4},{6,5},{7,6},{8,7},{9,8},{10,9... | collective-permute-start | bytes 135176 | tf_op jit(solution)/shard_map/ppermute | solution.py:520
  49.8 27.5 %all-to-all-start = ((f32[256,1,128]{2,1,0:T(1,128)}), f32[256,1,128]{2,1,0:T(1,128)S(1)}, u32[]{:S(2)}, u32[]{:S(2)}) async-start(f32[256,1,128]{2,1,0:T(1,128)} %bitcast.1), calls=%async_computation | async-start | bytes 262144 | tf_op jit(solution)/shard_map/all_to_all | solution.py:585

commit v3 on v2

--- a/solution.py
+++ b/solution.py
@@ -521,7 +521,10 @@
 
 
 def local(populations, concentrations, potential, solid_mask, surface_sign):
-    inputs = (populations, concentrations, potential, solid_mask, surface_sign)
+    inputs = tuple(
+        pltpu.with_memory_space_constraint(a, pltpu.HBM)
+        for a in (populations, concentrations, potential, solid_mask, surface_sign)
+    )
     packed = call(
         pack_kernel,
         "pack",
@@ -567,6 +570,7 @@
     left = send(strip, "gx", 1)
     right = send(strip, "gx", -1)
     (pop_new,) = call(finish_kernel, "finish", (f32(19, 8, 8, 128),), [], relaxed, mask)
+    left, right, pop_new = lax.optimization_barrier((left, right, pop_new))
     wide = jnp.concatenate([edge, left, right])
     above = send(wide, "gy", -1)
     below = send(wide, "gy", 1)

time: 78.8 us -> 74 us (0.939)
  blocking collectives: 0 us -> 27.4 us
  starting transfers between devices: 35.9 us -> 21.3 us
  waiting for transfers between devices: 23.9 us -> 10.9 us
  local copies, waits for them, and re-layouts: 4.25 us -> 0.01 us
    all_to_all x0 -> x1, blocking collectives: none -> 27.4 us  [local(): rows = lax.all_to_all(rows, ('gx', 'gy'), 0, 0, tiled=True)]
    all_to_all x1 -> x0, starting transfers between devices: 14.5 us -> none  [local(): rows = lax.all_to_all(rows, ('gx', 'gy'), 0, 0, tiled=True)]
    all_to_all x1 -> x0, waiting for transfers between devices: 12 us -> none  [local(): rows = lax.all_to_all(rows, ('gx', 'gy'), 0, 0, tiled=True)]
    unnamed x13 -> x3, local copies, waits for them, and re-layouts: 4.24 us -> 0.01 us
    ppermute x10, waiting for transfers between devices: 11.9 us -> 10.9 us  [send(): lax.ppermute(block, axis, [(i, (i + step) % count) for i in range(count)])]
  transfers between devices with their start and end apart: 11 -> 10, of which waited for: 6 -> 6; matrix products, arithmetic and copies ran while one was open for 0% -> 0% of each run, Pallas kernels for 1% -> 1%
where the time goes in v3:
time: 74 us; the launch traced here: 73.9 us
  blocking collectives  27.4 us (37%)
  starting transfers between devices  21.3 us (29%)
  Pallas kernels  13.7 us (19%)
  waiting for transfers between devices  10.9 us (15%)
    all_to_all x1, blocking collectives, local(): rows = lax.all_to_all(rows, ('gx', 'gy'), 0, 0, tiled=True)  27.4 us
    ppermute x10, starting transfers between devices, send(): lax.ppermute(block, axis, [(i, (i + step) % count) for i in range(count)])  21.3 us
    pallas_call x5, Pallas kernels, call(): pl.pallas_call(kernel, name=name, out_shape=outs, in_specs=in_specs or in...  13.7 us
    ppermute x10, waiting for transfers between devices, send(): lax.ppermute(block, axis, [(i, (i + step) % count) for i in range(count)])  10.9 us
  transfers between devices with their start and end apart: 10, of which 6 were waited for; matrix products, arithmetic and copies ran while one was open for 0% of the time, Pallas kernels for 1%

profile of v3, /device:TPU:1, one launch (start us, length us, event | category | flops | bytes accessed | tf_op | source)
XLA Modules:
  0.0 73.9 jit_solution(3034114036967477929)
XLA Ops:
  0.6 1.6 %pack.1 = (f32[19,8,8,128]{3,2,1,0:T(8,128)S(1)}, f32[3,8,8,128]{3,2,1,0:T(8,128)S(1)}, f32[8,8,128]{2,1,0:T(8,128)S(1)}, s32[8,8,128]{2,1,0:T(8,128)S(1)}, s32[...) custom-call(f32[19,8,8,128]{3,2,1,0:T(8,128)} %refs_0_.1, ...), custom_call_target="tpu_custom_call" | custom-call | tf_op jit(solution)/shard_map/pack/pallas_call | solution.py:504
  2.3 5.8 %collective-permute-start = (f32[100,8,128]{2,1,0:T(8,128)S(1)}, f32[100,8,128]{2,1,0:T(8,128)S(1)}, u32[]{:S(2)}, u32[]{:S(2)}) collective-permute-start(f32[100,8,128]{2,1,0:T(8,128)S(1)} %get-tuple-element.26), channel_id=1, source_target_pairs={{0,15},{1,0},{2,1},{3,2},{4,3},{5,4},{6,5},{7,6},{8,7},{9,8},{10,9... | collective-permute-start | bytes 1228808 | tf_op jit(solution)/shard_map/ppermute | solution.py:520
  8.1 0.0 collective-permute-start.1
  8.1 1.0 %collective-permute-start.2 = (f32[7,8,128]{2,1,0:T(8,128)S(1)}, f32[7,8,128]{2,1,0:T(8,128)S(1)}, u32[]{:S(2)}, u32[]{:S(2)}) collective-permute-start(f32[7,8,128]{2,1,0:T(8,128)S(1)} %get-tuple-element.28), channel_id=1, source_target_pairs={{0,240},{16,0},{32,16},{48,32},{64,48},{80,64},{96,80},{112,96},{1... | collective-permute-start | bytes 86024 | tf_op jit(solution)/shard_map/ppermute | solution.py:520
  9.1 1.5 %collective-permute-start.3 = (f32[7,8,128]{2,1,0:T(8,128)S(1)}, f32[7,8,128]{2,1,0:T(8,128)S(1)}, u32[]{:S(2)}, u32[]{:S(2)}) collective-permute-start(f32[7,8,128]{2,1,0:T(8,128)S(1)} %get-tuple-element.29), channel_id=1, source_target_pairs={{0,16},{16,32},{32,48},{48,64},{64,80},{80,96},{96,112},{112,128},... | collective-permute-start | bytes 86024 | tf_op jit(solution)/shard_map/ppermute | solution.py:520
  10.6 1.8 %collective-permute-done.2.from_right = f32[7,8,128]{2,1,0:T(8,128)S(1)} collective-permute-done((f32[7,8,128]{2,1,0:T(8,128)S(1)}, f32[7,8,128]{2,1,0:T(8,128)S(1)}, u32[]{:S(2)}, u32[]{:S(2)}) %collective-permute-start.2) | collective-permute-done | bytes 28704 | tf_op jit(solution)/shard_map/ppermute | solution.py:520
  12.5 2.3 %collective-permute-done.3.from_left = f32[7,8,128]{2,1,0:T(8,128)S(1)} collective-permute-done((f32[7,8,128]{2,1,0:T(8,128)S(1)}, f32[7,8,128]{2,1,0:T(8,128)S(1)}, u32[]{:S(2)}, u32[]{:S(2)}) %collective-permute-start.3) | collective-permute-done | bytes 28704 | tf_op jit(solution)/shard_map/ppermute | solution.py:520
  14.8 0.0 collective-permute-start.5
  14.8 4.8 %collective-permute-start.4 = (f32[14,8,128]{2,1,0:T(8,128)S(1)}, f32[14,8,128]{2,1,0:T(8,128)S(1)}, u32[]{:S(2)}, u32[]{:S(2)}) collective-permute-start(f32[14,8,128]{2,1,0:T(8,128)S(1)} %constant_dynamic-update-slice_fusion), channel_id=1, source_target_pairs={{0,15},{1,0},{2,1},{3,2},{4,3},{5,4},{6,5},{7,6},{8,7},{9,8},{10,9... | collective-permute-start | bytes 172040 | tf_op jit(solution)/shard_map/ppermute | solution.py:520
  19.6 3.1 %collective-permute-done.5.corner_down = f32[14,8,128]{2,1,0:T(8,128)S(1)} collective-permute-done((f32[14,8,128]{2,1,0:T(8,128)S(1)}, f32[14,8,128]{2,1,0:T(8,128)S(1)}, u32[]{:S(2)}, u32[]{:S(2)}) %collective-permute-start.5) | collective-permute-done | bytes 57376 | tf_op jit(solution)/shard_map/ppermute | solution.py:520
  22.7 0.0 collective-permute-done.4.corner_up
  22.7 0.0 collective-permute-done.up
  22.7 0.0 collective-permute-done.1.down
  22.7 8.8 %steps.1 = (f32[19,18,8,128]{3,2,1,0:T(8,128)S(1)}, f32[18,18,8,128]{3,2,1,0:T(8,128)S(1)}, f32[3,8,8,128]{3,2,1,0:T(8,128)}, f32[9,8,128]{2,1,0:T(8,128)S(1)}) custom-call(f32[19,8,8,128]{3,2,1,0:T(8,128)S(1)} %get-tuple-element.21.pop, f32[3,8,8,128]{3,2,1,0:T(8,128)S(1)} %get-tuple-element.22.conc, f32[8,8,128]{2,1,0:T(8,128)S(1)} %get-tuple-element.23.pot, ...), custom_call_target="tpu_custom_call" | custom-call | tf_op jit(solution)/shard_map/steps/pallas_call | solution.py:504
  31.5 3.4 %collective-permute-start.7 = (f32[1,8,128]{2,1,0:T(8,128)S(1)}, f32[1,8,128]{2,1,0:T(8,128)S(1)}, u32[]{:S(2)}, u32[]{:S(2)}) collective-permute-start(f32[1,8,128]{2,1,0:T(8,128)S(1)} %slice.3), channel_id=1, source_target_pairs={{0,240},{16,0},{32,16},{48,32},{64,48},{80,64},{96,80},{112,96},{1... | collective-permute-start | bytes 12296 | tf_op jit(solution)/shard_map/ppermute | solution.py:520
  34.9 0.0 collective-permute-start.6
  34.9 1.1 %finish.1 = f32[19,8,8,128]{3,2,1,0:T(8,128)} custom-call(f32[19,18,8,128]{3,2,1,0:T(8,128)S(1)} %get-tuple-element.31.g, f32[18,18,8,128]{3,2,1,0:T(8,128)S(1)} %get-tuple-element.32.mask), custom_call_target="tpu_custom_call" | custom-call | tf_op jit(solution)/shard_map/finish/pallas_call | solution.py:504
  36.0 0.2 collective-permute-done.7.right
  36.2 2.0 %collective-permute-done.6.left = f32[1,8,128]{2,1,0:T(8,128)S(1)} collective-permute-done((f32[1,8,128]{2,1,0:T(8,128)S(1)}, f32[1,8,128]{2,1,0:T(8,128)S(1)}, u32[]{:S(2)}, u32[]{:S(2)}) %collective-permute-start.6) | collective-permute-done | bytes 4128 | tf_op jit(solution)/shard_map/ppermute | solution.py:520
  38.1 0.0 collective-permute-start.9
  38.1 4.8 %collective-permute-start.8 = (f32[11,8,128]{2,1,0:T(8,128)S(1)}, f32[11,8,128]{2,1,0:T(8,128)S(1)}, u32[]{:S(2)}, u32[]{:S(2)}) collective-permute-start(f32[11,8,128]{2,1,0:T(8,128)S(1)} %constant_dynamic-update-slice_fusion.2), channel_id=1, source_target_pairs={{0,15},{1,0},{2,1},{3,2},{4,3},{5,4},{6,5},{7,6},{8,7},{9,8},{10,9... | collective-permute-start | bytes 135176 | tf_op jit(solution)/shard_map/ppermute | solution.py:520
  42.9 1.4 %collective-permute-done.9.down = f32[11,8,128]{2,1,0:T(8,128)S(1)} collective-permute-done((f32[11,8,128]{2,1,0:T(8,128)S(1)}, f32[11,8,128]{2,1,0:T(8,128)S(1)}, u32[]{:S(2)}, u32[]{:S(2)}) %collective-permute-start.9) | collective-permute-done | bytes 45088 | tf_op jit(solution)/shard_map/ppermute | solution.py:520
  44.3 0.0 collective-permute-done.8.up
  44.3 1.1 %levels.1 = (f32[8,8,8,128]{3,2,1,0:T(8,128)S(1)}, f32[256,128]{1,0:T(8,128)S(1)}) custom-call(f32[9,8,128]{2,1,0:T(8,128)S(1)} %get-tuple-element.30.own, f32[1,8,128]{2,1,0:T(8,128)S(1)} %collective-permute-done.6.left, f32[1,8,128]{2,1,0:T(8,128)S(1)} %collective-permute-done.7.right, f32[11,8,128]{2,1,0:T(8,128)S(1)} %collective-permute-done.8.up, ...), custom_call_target="tpu_custom_call" | custom-call | tf_op jit(solution)/shard_map/levels/pallas_call | solution.py:504
  45.4 27.4 %all_to_all.11 = f32[256,1,128]{2,1,0:T(1,128)S(1)} all-to-all(f32[256,1,128]{2,1,0:T(1,128)S(1)} %bitcast.5), channel_id=1, replica_groups=mesh['gx'=16,'gy'=16] {'gx','gy'}, dimensions={0} | all-to-all | bytes 262144 | tf_op jit(solution)/shard_map/all_to_all | solution.py:589
  72.8 1.1 %combine.1 = f32[8,8,128]{2,1,0:T(8,128)} custom-call(f32[256,128]{1,0:T(8,128)S(1)} %bitcast.4, f32[8,8,8,128]{3,2,1,0:T(8,128)S(1)} %get-tuple-element.38.levels, f32[8,8,128]{2,1,0:T(8,128)S(1)} %get-tuple-element.23.pot), custom_call_target="tpu_custom_call" | custom-call | tf_op jit(solution)/shard_map/combine/pallas_call | solution.py:504
  (6 shorter events, 0.0 us)
Async XLA Ops:
  2.3 20.4 %collective-permute-start = (f32[100,8,128]{2,1,0:T(8,128)S(1)}, f32[100,8,128]{2,1,0:T(8,128)S(1)}, u32[]{:S(2)}, u32[]{:S(2)}) collective-permute-start(f32[100,8,128]{2,1,0:T(8,128)S(1)} %get-tuple-element.26), channel_id=1, source_target_pairs={{0,15},{1,0},{2,1},{3,2},{4,3},{5,4},{6,5},{7,6},{8,7},{9,8},{10,9... | collective-permute-start | bytes 1228808 | tf_op jit(solution)/shard_map/ppermute | solution.py:520
  8.1 14.6 %collective-permute-start.1 = (f32[100,8,128]{2,1,0:T(8,128)S(1)}, f32[100,8,128]{2,1,0:T(8,128)S(1)}, u32[]{:S(2)}, u32[]{:S(2)}) collective-permute-start(f32[100,8,128]{2,1,0:T(8,128)S(1)} %get-tuple-element.27), channel_id=1, source_target_pairs={{0,1},{1,2},{2,3},{3,4},{4,5},{5,6},{6,7},{7,8},{8,9},{9,10},{10,1... | collective-permute-start | bytes 1228808 | tf_op jit(solution)/shard_map/ppermute | solution.py:520
  8.1 4.3 %collective-permute-start.2 = (f32[7,8,128]{2,1,0:T(8,128)S(1)}, f32[7,8,128]{2,1,0:T(8,128)S(1)}, u32[]{:S(2)}, u32[]{:S(2)}) collective-permute-start(f32[7,8,128]{2,1,0:T(8,128)S(1)} %get-tuple-element.28), channel_id=1, source_target_pairs={{0,240},{16,0},{32,16},{48,32},{64,48},{80,64},{96,80},{112,96},{1... | collective-permute-start | bytes 86024 | tf_op jit(solution)/shard_map/ppermute | solution.py:520
  9.1 5.7 %collective-permute-start.3 = (f32[7,8,128]{2,1,0:T(8,128)S(1)}, f32[7,8,128]{2,1,0:T(8,128)S(1)}, u32[]{:S(2)}, u32[]{:S(2)}) collective-permute-start(f32[7,8,128]{2,1,0:T(8,128)S(1)} %get-tuple-element.29), channel_id=1, source_target_pairs={{0,16},{16,32},{32,48},{48,64},{64,80},{80,96},{96,112},{112,128},... | collective-permute-start | bytes 86024 | tf_op jit(solution)/shard_map/ppermute | solution.py:520
  14.8 7.9 %collective-permute-start.5 = (f32[14,8,128]{2,1,0:T(8,128)S(1)}, f32[14,8,128]{2,1,0:T(8,128)S(1)}, u32[]{:S(2)}, u32[]{:S(2)}) collective-permute-start(f32[14,8,128]{2,1,0:T(8,128)S(1)} %constant_dynamic-update-slice_fusion), channel_id=1, source_target_pairs={{0,1},{1,2},{2,3},{3,4},{4,5},{5,6},{6,7},{7,8},{8,9},{9,10},{10,1... | collective-permute-start | bytes 172040 | tf_op jit(solution)/shard_map/ppermute | solution.py:520
  14.8 7.9 %collective-permute-start.4 = (f32[14,8,128]{2,1,0:T(8,128)S(1)}, f32[14,8,128]{2,1,0:T(8,128)S(1)}, u32[]{:S(2)}, u32[]{:S(2)}) collective-permute-start(f32[14,8,128]{2,1,0:T(8,128)S(1)} %constant_dynamic-update-slice_fusion), channel_id=1, source_target_pairs={{0,15},{1,0},{2,1},{3,2},{4,3},{5,4},{6,5},{7,6},{8,7},{9,8},{10,9... | collective-permute-start | bytes 172040 | tf_op jit(solution)/shard_map/ppermute | solution.py:520
  31.5 4.7 %collective-permute-start.7 = (f32[1,8,128]{2,1,0:T(8,128)S(1)}, f32[1,8,128]{2,1,0:T(8,128)S(1)}, u32[]{:S(2)}, u32[]{:S(2)}) collective-permute-start(f32[1,8,128]{2,1,0:T(8,128)S(1)} %slice.3), channel_id=1, source_target_pairs={{0,240},{16,0},{32,16},{48,32},{64,48},{80,64},{96,80},{112,96},{1... | collective-permute-start | bytes 12296 | tf_op jit(solution)/shard_map/ppermute | solution.py:520
  34.9 3.2 %collective-permute-start.6 = (f32[1,8,128]{2,1,0:T(8,128)S(1)}, f32[1,8,128]{2,1,0:T(8,128)S(1)}, u32[]{:S(2)}, u32[]{:S(2)}) collective-permute-start(f32[1,8,128]{2,1,0:T(8,128)S(1)} %slice.3), channel_id=1, source_target_pairs={{0,16},{16,32},{32,48},{48,64},{64,80},{80,96},{96,112},{112,128},... | collective-permute-start | bytes 12296 | tf_op jit(solution)/shard_map/ppermute | solution.py:520
  38.1 6.2 %collective-permute-start.9 = (f32[11,8,128]{2,1,0:T(8,128)S(1)}, f32[11,8,128]{2,1,0:T(8,128)S(1)}, u32[]{:S(2)}, u32[]{:S(2)}) collective-permute-start(f32[11,8,128]{2,1,0:T(8,128)S(1)} %constant_dynamic-update-slice_fusion.2), channel_id=1, source_target_pairs={{0,1},{1,2},{2,3},{3,4},{4,5},{5,6},{6,7},{7,8},{8,9},{9,10},{10,1... | collective-permute-start | bytes 135176 | tf_op jit(solution)/shard_map/ppermute | solution.py:520
  38.1 6.2 %collective-permute-start.8 = (f32[11,8,128]{2,1,0:T(8,128)S(1)}, f32[11,8,128]{2,1,0:T(8,128)S(1)}, u32[]{:S(2)}, u32[]{:S(2)}) collective-permute-start(f32[11,8,128]{2,1,0:T(8,128)S(1)} %constant_dynamic-update-slice_fusion.2), channel_id=1, source_target_pairs={{0,15},{1,0},{2,1},{3,2},{4,3},{5,4},{6,5},{7,6},{8,7},{9,8},{10,9... | collective-permute-start | bytes 135176 | tf_op jit(solution)/shard_map/ppermute | solution.py:520

commit v4 on v3

--- a/solution.py
+++ b/solution.py
@@ -146,10 +146,23 @@
     return out
 
 
+def shifted_slab(get, offset, s):
+    cz, cy, cx = offset
+    if s == 8:
+        v = y_shift(get(16), get(17), cy)
+        return tuple(rl(x, 16 * cz + cx) for x in v)
+    source = (s - cz) % 8
+    v = y_shift(get(2 * source), get(2 * source + 1), cy)
+    if cx:
+        side = y_shift(get(16), get(17), cy)
+        v = tuple(x_shift(v[h], side[h], source, cx) for h in range(2))
+    return v
+
+
 def step_kernel(
-    pop, conc, pot, solid, sign, up, down, from_right, from_left, corner_up, corner_down,
-    g, mask, conc_out, edge_out,
-    f, vel, cc, fluid, pt, dpot, field, speed_up, flux,
+    pop, conc, pot, solid, sign, x_left, x_right, up, down, from_right, from_left, corner_up,
+    corner_down, g, mask, conc_out, edge_out,
+    f, below_rows, vel, cc, cn, fluid, pt, dpot, field, flux,
 ):
     lane, row = lane_id(), row_id()
     top = row < 4
@@ -169,17 +182,27 @@
             out = jnp.where(in_lanes(lane, 16 * z + 8, 4), rl(tiles[z], 16 * z + 8 - 124), out)
         return out
 
+    def strips(k, b):
+        t = k // 4
+        low = jnp.where(top, corner_up[XT + t], corner_down[XT + t])
+        high = jnp.where(top, corner_up[t], corner_down[t])
+        q = k % 4
+        mine = jnp.where(
+            slot < 8,
+            jnp.where(slot < 4, rl(from_left[t], -4 * q), rl(x_left[t], 4 - 4 * q)),
+            jnp.where(slot < 12, rl(x_right[t], 8 - 4 * q), rl(from_right[t], 12 - 4 * q)),
+        )
+        return mine, strip(k, b, low, high)
+
     def load(k, own, put):
-        t = k // 4
         a = [own(z) for z in range(8)]
         b = [halves(k, z) for z in range(8)]
         for z in range(8):
             put(2 * z, a[z])
             put(2 * z + 1, b[z])
-        put(16, strip(k, a, from_left[t], from_right[t]))
-        low = jnp.where(top, corner_up[XT + t], corner_down[XT + t])
-        high = jnp.where(top, corner_up[t], corner_down[t])
-        put(17, strip(k, b, low, high))
+        sa, sb = strips(k, b)
+        put(16, sa)
+        put(17, sb)
 
     def putter(ref, *index):
         def put(i, v):
@@ -187,10 +210,8 @@
 
         return put
 
-    for k in range(19):
-        load(k, lambda z, k=k: pop[k, z], putter(f, k))
     for k in range(3):
-        load(F_CONC + k, lambda z, k=k: conc[k, z], putter(cc, 0, k))
+        load(F_CONC + k, lambda z, k=k: conc[k, z], putter(cc, k))
     load(F_FLUID, lambda z: 1.0 - solid[z].astype(jnp.float32), putter(fluid))
     load(F_POT, lambda z: pot[z], putter(pt))
 
@@ -225,14 +246,24 @@
                     for z in range(8):
                         hi = jnp.where(lane == 16 * z + 7, rl(pt[2 * z + h], 16 * z + 3), hi)
                 here = pt[2 * s + h]
-                dpot[2 * axis, 2 * s + h] = here - lo
-                dpot[2 * axis + 1, 2 * s + h] = hi - here
+                if h == 0 and s < 8:
+                    dpot[3 + axis, 2 * s] = here - lo
+                dpot[axis, 2 * s + h] = hi - here
                 field[axis, 2 * s + h] = (0.5 * force_scale) * (lo - hi)
 
     pairs = [(i, i + 1) for i in range(1, 19, 2)]
 
-    def collide(s, now):
-        v = [f[i, s] for i in range(19)]
+    def along(c, vector):
+        running = None
+        for d in range(3):
+            if c[d] != 0:
+                if running is None:
+                    running = vector[d] if c[d] > 0 else -vector[d]
+                else:
+                    running = running + vector[d] if c[d] > 0 else running - vector[d]
+        return running
+
+    def collide(s, v):
         total = {}
         delta = {}
         for a, b in pairs:
@@ -250,7 +281,7 @@
         )
         open_cell = fluid[s]
         charge = open_cell * (
-            valences[0] * cc[now, 0, s] + valences[1] * cc[now, 1, s] + valences[2] * cc[now, 2, s]
+            valences[0] * cc[0, s] + valences[1] * cc[1, s] + valences[2] * cc[2, s]
         )
         force = [charge * field[d, s] for d in range(3)]
         inverse = 1.0 / density
@@ -268,17 +299,6 @@
         even = [(4.5 * gain) * flow[d] + (9.0 * push) * force[d] for d in range(3)]
         is_open = open_cell > 0.5
         g[0, s] = jnp.where(is_open, keep * v[0] + lattice_weight[0] * base, v[0])
-
-        def along(c, vector):
-            running = None
-            for d in range(3):
-                if c[d] != 0:
-                    if running is None:
-                        running = vector[d] if c[d] > 0 else -vector[d]
-                    else:
-                        running = running + vector[d] if c[d] > 0 else running - vector[d]
-            return running
-
         for a, b in pairs:
             c, w = lattice_velocity[a], lattice_weight[a]
             middle = base + along(c, u) * along(c, even)
@@ -286,68 +306,77 @@
             g[a, s] = jnp.where(is_open, keep * v[a] + w * (middle + side), v[b])
             g[b, s] = jnp.where(is_open, keep * v[b] + w * (middle - side), v[a])
 
-    def collide_all(now):
-        def both(s, c):
-            collide(2 * s, now)
-            collide(2 * s + 1, now)
-            return c
-
-        lax.fori_loop(0, SLABS, both, 0)
+    for z in range(8):
+        collide(2 * z, [pop[k, z] for k in range(19)])
+    for z in range(8):
+        v = [halves(k, z) for k in range(19)]
+        for k in range(19):
+            below_rows[k, z] = v[k]
+        collide(2 * z + 1, v)
+    both = [
+        strips(k, [below_rows[k, z] for z in range(8)])
+        for k in range(19)
+    ]
+    for h in range(2):
+        collide(16 + h, [both[k][h] for k in range(19)])
 
     def stream():
         for s in range(2 * SLABS):
             f[0, s] = g[0, s]
-        for i in range(1, 19):
-            moved = shifted(lambda s, i=i: g[i, s], lattice_velocity[i])
-            for s in range(SLABS):
+        for s in range(SLABS):
+            for i in range(1, 19):
+                moved = shifted_slab(lambda n, i=i: g[i, n], lattice_velocity[i], s)
                 for h in range(2):
                     n = 2 * s + h
-                    f[i, n] = jnp.where(mask[i - 1, n] > 0.5, moved[s][h], g[opposite[i], n])
-
-    def ions(now, after, own=False):
+                    f[i, n] = jnp.where(mask[i - 1, n] > 0.5, moved[h], g[opposite[i], n])
+        for s in range(2 * SLABS):
+            collide(s, [f[i, s] for i in range(19)])
+
+    def ions(own=False):
         for axis in range(3):
             plus = tuple(1 if d == axis else 0 for d in range(3))
             minus = tuple(-p for p in plus)
             upper = 2 * (2 - axis) + 1
-            v_high = shifted(lambda s: vel[axis, s], minus)
-            for s in range(SLABS):
+            for s in [8] + list(range(8)):
+                v_high = shifted_slab(lambda n: vel[axis, n], minus, s)
+                c_high = [shifted_slab(lambda n, k=k: cc[k, n], minus, s) for k in range(3)]
                 for h in range(2):
                     n = 2 * s + h
-                    speed_up[n] = 0.25 * (vel[axis, n] + v_high[s][h])
-            for k in range(3):
-                c_high = shifted(lambda s: cc[now, k, s], minus)
-                rate = diffusivity[k]
-                drift = 0.5 * rate * valences[k]
-                for s in range(SLABS):
-                    for h in range(2):
-                        n = 2 * s + h
-                        here, hi = cc[now, k, n], c_high[s][h]
-                        pull = speed_up[n] - drift * dpot[2 * axis + 1, n]
-                        flux[k, n] = mask[upper, n] * (rate * (here - hi) + (here + hi) * pull)
-                low = shifted(lambda s: flux[k, s], plus, own)
-                for s in range(8 if own else SLABS):
-                    for h in range(1 if own else 2):
-                        n = 2 * s + h
-                        before = cc[now if axis == 0 else after, k, n]
-                        cc[after, k, n] = before - (flux[k, n] - low[s][h])
+                    speed = 0.25 * (vel[axis, n] + v_high[h])
+                    step, is_open = dpot[axis, n], mask[upper, n]
+                    for k in range(3):
+                        rate = diffusivity[k]
+                        here, hi = cc[k, n], c_high[k][h]
+                        pull = speed - (0.5 * rate * valences[k]) * step
+                        flux[axis, k, n] = is_open * (rate * (here - hi) + (here + hi) * pull)
+        for k in range(3):
+            for s in range(8 if own else SLABS):
+                low = [
+                    shifted_slab(
+                        lambda n, d=d: flux[d, k, n], tuple(1 if e == d else 0 for e in range(3)), s
+                    )
+                    for d in range(3)
+                ]
+                for h in range(1 if own else 2):
+                    n = 2 * s + h
+                    net = [flux[d, k, n] - low[d][h] for d in range(3)]
+                    cn[k, n] = cc[k, n] - ((net[0] + net[1]) + net[2])
 
     def one_step(step, carry):
-        now = lax.rem(step, 2)
-        collide_all(now)
+        ions()
+        for k in range(3):
+            for n in range(2 * SLABS):
+                cc[k, n] = cn[k, n]
         stream()
-        ions(now, 1 - now)
         return carry
 
     lax.fori_loop(0, STEPS - 1, one_step, 0)
-    final = (STEPS - 1) % 2
-    collide_all(final)
-    ions(final, 1 - final, own=True)
-
-    last = STEPS % 2
+    ions(own=True)
+
     edge = jnp.zeros(TILE, jnp.float32)
     for z in range(8):
         n = 2 * z
-        c = [cc[last, k, n] for k in range(3)]
+        c = [cn[k, n] for k in range(3)]
         for k in range(3):
             conc_out[k, z] = c[k]
         open_cell = fluid[n]
@@ -355,7 +384,7 @@
             valences[0] * c[0] + valences[1] * c[1] + valences[2] * c[2]
         ) + surface_scale * sign[z].astype(jnp.float32) * (1.0 - open_cell)
         spread = (
-            (dpot[1, n] - dpot[0, n]) + (dpot[3, n] - dpot[2, n]) + (dpot[5, n] - dpot[4, n])
+            (dpot[0, n] - dpot[3, n]) + (dpot[1, n] - dpot[4, n]) + (dpot[2, n] - dpot[5, n])
         )
         residual = target - ((diag_coef - 6.0) * pt[n] - spread)
         edge_out[z] = residual
@@ -364,13 +393,37 @@
     edge_out[8] = edge
 
 
+STEP_SHAPES = (
+    (
+        (19, 2 * SLABS, 8, 128),
+        (18, 2 * SLABS, 8, 128),
+        (3, 8, 8, 128),
+        (9, 8, 128),
+    ),
+    (
+        (19, 2 * SLABS, 8, 128),
+        (19, 8, 8, 128),
+        (3, 2 * SLABS, 8, 128),
+        (3, 2 * SLABS, 8, 128),
+        (3, 2 * SLABS, 8, 128),
+        (2 * SLABS, 8, 128),
+        (2 * SLABS, 8, 128),
+        (6, 2 * SLABS, 8, 128),
+        (3, 2 * SLABS, 8, 128),
+        (3, 3, 2 * SLABS, 8, 128),
+    ),
+)
+
+
 def finish_kernel(g, mask, pop_out):
     for z in range(8):
         pop_out[0, z] = g[0, 2 * z]
     for i in range(1, 19):
         moved = shifted(lambda s, i=i: g[i, s], lattice_velocity[i], own=True)
         for z in range(8):
-            pop_out[i, z] = jnp.where(mask[i - 1, 2 * z] > 0.5, moved[z][0], g[opposite[i], 2 * z])
+            pop_out[i, z] = jnp.where(
+                mask[i - 1, 2 * z] > 0.5, moved[z][0], g[opposite[i], 2 * z]
+            )
 
 
 def levels_kernel(own, left, right, up, down, level_out, row_out, lv, part):
@@ -542,23 +595,14 @@
     corner = jnp.concatenate([from_right, from_left])
     corner_up = send(corner, "gy", -1)
     corner_down = send(corner, "gy", 1)
-    n = 2 * SLABS
     relaxed, mask, conc_new, edge = call(
         step_kernel,
         "steps",
-        (f32(19, n, 8, 128), f32(18, n, 8, 128), f32(3, 8, 8, 128), f32(9, 8, 128)),
-        [
-            (19, n, 8, 128),
-            (3, n, 8, 128),
-            (2, 3, n, 8, 128),
-            (n, 8, 128),
-            (n, 8, 128),
-            (6, n, 8, 128),
-            (3, n, 8, 128),
-            (n, 8, 128),
-            (3, n, 8, 128),
-        ],
+        tuple(f32(*shape) for shape in STEP_SHAPES[0]),
+        STEP_SHAPES[1],
         *kept,
+        x_left,
+        x_right,
         up,
         down,
         from_right,

time: 74 us -> 71.4 us (0.965)
  Pallas kernels: 13.7 us -> 11 us
    pallas_call x5, Pallas kernels: 13.7 us -> 11 us  [call(): pl.pallas_call(kernel, name=name, out_shape=outs, in_specs=in_specs or in...]
  transfers between devices with their start and end apart: 10 -> 10, of which waited for: 6 -> 6; matrix products, arithmetic and copies ran while one was open for 0% -> 0% of each run, Pallas kernels for 1% -> 2%
where the time goes in v4:
time: 71.4 us; the launch traced here: 71.2 us
  blocking collectives  27.4 us (38%)
  starting transfers between devices  21.3 us (30%)
  Pallas kernels  11 us (15%)
  waiting for transfers between devices  10.9 us (15%)
    all_to_all x1, blocking collectives, local(): rows = lax.all_to_all(rows, ('gx', 'gy'), 0, 0, tiled=True)  27.4 us
    ppermute x10, starting transfers between devices, send(): lax.ppermute(block, axis, [(i, (i + step) % count) for i in range(count)])  21.3 us
    pallas_call x5, Pallas kernels, call(): pl.pallas_call(kernel, name=name, out_shape=outs, in_specs=in_specs or in...  11 us
    ppermute x10, waiting for transfers between devices, send(): lax.ppermute(block, axis, [(i, (i + step) % count) for i in range(count)])  10.9 us
  transfers between devices with their start and end apart: 10, of which 6 were waited for; matrix products, arithmetic and copies ran while one was open for 0% of the time, Pallas kernels for 2%

profile of v4, /device:TPU:1, one launch (start us, length us, event | category | flops | bytes accessed | tf_op | source)
XLA Modules:
  0.0 71.2 jit_solution(8582485372605801154)
XLA Ops:
  0.6 1.6 %pack.1 = (f32[19,8,8,128]{3,2,1,0:T(8,128)S(1)}, f32[3,8,8,128]{3,2,1,0:T(8,128)S(1)}, f32[8,8,128]{2,1,0:T(8,128)S(1)}, s32[8,8,128]{2,1,0:T(8,128)S(1)}, s32[...) custom-call(f32[19,8,8,128]{3,2,1,0:T(8,128)} %refs_0_.1, ...), custom_call_target="tpu_custom_call" | custom-call | tf_op jit(solution)/shard_map/pack/pallas_call | solution.py:557
  2.3 5.8 %collective-permute-start = (f32[100,8,128]{2,1,0:T(8,128)S(1)}, f32[100,8,128]{2,1,0:T(8,128)S(1)}, u32[]{:S(2)}, u32[]{:S(2)}) collective-permute-start(f32[100,8,128]{2,1,0:T(8,128)S(1)} %get-tuple-element.28), channel_id=1, source_target_pairs={{0,15},{1,0},{2,1},{3,2},{4,3},{5,4},{6,5},{7,6},{8,7},{9,8},{10,9... | collective-permute-start | bytes 1228808 | tf_op jit(solution)/shard_map/ppermute | solution.py:573
  8.1 0.0 collective-permute-start.1
  8.1 1.0 %collective-permute-start.2 = (f32[7,8,128]{2,1,0:T(8,128)S(1)}, f32[7,8,128]{2,1,0:T(8,128)S(1)}, u32[]{:S(2)}, u32[]{:S(2)}) collective-permute-start(f32[7,8,128]{2,1,0:T(8,128)S(1)} %get-tuple-element.26.x_left), channel_id=1, source_target_pairs={{0,240},{16,0},{32,16},{48,32},{64,48},{80,64},{96,80},{112,96},{1... | collective-permute-start | bytes 86024 | tf_op jit(solution)/shard_map/ppermute | solution.py:573
  9.1 1.5 %collective-permute-start.3 = (f32[7,8,128]{2,1,0:T(8,128)S(1)}, f32[7,8,128]{2,1,0:T(8,128)S(1)}, u32[]{:S(2)}, u32[]{:S(2)}) collective-permute-start(f32[7,8,128]{2,1,0:T(8,128)S(1)} %get-tuple-element.27.x_right), channel_id=1, source_target_pairs={{0,16},{16,32},{32,48},{48,64},{64,80},{80,96},{96,112},{112,128},... | collective-permute-start | bytes 86024 | tf_op jit(solution)/shard_map/ppermute | solution.py:573
  10.6 1.8 %collective-permute-done.2.from_right = f32[7,8,128]{2,1,0:T(8,128)S(1)} collective-permute-done((f32[7,8,128]{2,1,0:T(8,128)S(1)}, f32[7,8,128]{2,1,0:T(8,128)S(1)}, u32[]{:S(2)}, u32[]{:S(2)}) %collective-permute-start.2) | collective-permute-done | bytes 28704 | tf_op jit(solution)/shard_map/ppermute | solution.py:573
  12.5 2.3 %collective-permute-done.3.from_left = f32[7,8,128]{2,1,0:T(8,128)S(1)} collective-permute-done((f32[7,8,128]{2,1,0:T(8,128)S(1)}, f32[7,8,128]{2,1,0:T(8,128)S(1)}, u32[]{:S(2)}, u32[]{:S(2)}) %collective-permute-start.3) | collective-permute-done | bytes 28704 | tf_op jit(solution)/shard_map/ppermute | solution.py:573
  14.8 0.0 collective-permute-start.5
  14.8 4.8 %collective-permute-start.4 = (f32[14,8,128]{2,1,0:T(8,128)S(1)}, f32[14,8,128]{2,1,0:T(8,128)S(1)}, u32[]{:S(2)}, u32[]{:S(2)}) collective-permute-start(f32[14,8,128]{2,1,0:T(8,128)S(1)} %constant_dynamic-update-slice_fusion), channel_id=1, source_target_pairs={{0,15},{1,0},{2,1},{3,2},{4,3},{5,4},{6,5},{7,6},{8,7},{9,8},{10,9... | collective-permute-start | bytes 172040 | tf_op jit(solution)/shard_map/ppermute | solution.py:573
  19.6 3.1 %collective-permute-done.5.corner_down = f32[14,8,128]{2,1,0:T(8,128)S(1)} collective-permute-done((f32[14,8,128]{2,1,0:T(8,128)S(1)}, f32[14,8,128]{2,1,0:T(8,128)S(1)}, u32[]{:S(2)}, u32[]{:S(2)}) %collective-permute-start.5) | collective-permute-done | bytes 57376 | tf_op jit(solution)/shard_map/ppermute | solution.py:573
  22.7 0.0 collective-permute-done.4.corner_up
  22.7 0.0 collective-permute-done.up
  22.7 0.0 collective-permute-done.1.down
  22.7 6.1 %steps.1 = (f32[19,18,8,128]{3,2,1,0:T(8,128)S(1)}, f32[18,18,8,128]{3,2,1,0:T(8,128)S(1)}, f32[3,8,8,128]{3,2,1,0:T(8,128)}, f32[9,8,128]{2,1,0:T(8,128)S(1)}) custom-call(f32[19,8,8,128]{3,2,1,0:T(8,128)S(1)} %get-tuple-element.21.pop, f32[3,8,8,128]{3,2,1,0:T(8,128)S(1)} %get-tuple-element.22.conc, f32[8,8,128]{2,1,0:T(8,128)S(1)} %get-tuple-element.23.pot, ...), custom_call_target="tpu_custom_call" | custom-call | tf_op jit(solution)/shard_map/steps/pallas_call | solution.py:557
  28.8 3.4 %collective-permute-start.7 = (f32[1,8,128]{2,1,0:T(8,128)S(1)}, f32[1,8,128]{2,1,0:T(8,128)S(1)}, u32[]{:S(2)}, u32[]{:S(2)}) collective-permute-start(f32[1,8,128]{2,1,0:T(8,128)S(1)} %slice.3), channel_id=1, source_target_pairs={{0,240},{16,0},{32,16},{48,32},{64,48},{80,64},{96,80},{112,96},{1... | collective-permute-start | bytes 12296 | tf_op jit(solution)/shard_map/ppermute | solution.py:573
  32.2 0.0 collective-permute-start.6
  32.2 1.1 %finish.1 = f32[19,8,8,128]{3,2,1,0:T(8,128)} custom-call(f32[19,18,8,128]{3,2,1,0:T(8,128)S(1)} %get-tuple-element.31.g, f32[18,18,8,128]{3,2,1,0:T(8,128)S(1)} %get-tuple-element.32.mask), custom_call_target="tpu_custom_call" | custom-call | tf_op jit(solution)/shard_map/finish/pallas_call | solution.py:557
  33.3 0.2 collective-permute-done.7.right
  33.5 2.0 %collective-permute-done.6.left = f32[1,8,128]{2,1,0:T(8,128)S(1)} collective-permute-done((f32[1,8,128]{2,1,0:T(8,128)S(1)}, f32[1,8,128]{2,1,0:T(8,128)S(1)}, u32[]{:S(2)}, u32[]{:S(2)}) %collective-permute-start.6) | collective-permute-done | bytes 4128 | tf_op jit(solution)/shard_map/ppermute | solution.py:573
  35.4 0.0 collective-permute-start.9
  35.4 4.8 %collective-permute-start.8 = (f32[11,8,128]{2,1,0:T(8,128)S(1)}, f32[11,8,128]{2,1,0:T(8,128)S(1)}, u32[]{:S(2)}, u32[]{:S(2)}) collective-permute-start(f32[11,8,128]{2,1,0:T(8,128)S(1)} %constant_dynamic-update-slice_fusion.2), channel_id=1, source_target_pairs={{0,15},{1,0},{2,1},{3,2},{4,3},{5,4},{6,5},{7,6},{8,7},{9,8},{10,9... | collective-permute-start | bytes 135176 | tf_op jit(solution)/shard_map/ppermute | solution.py:573
  40.2 1.4 %collective-permute-done.9.down = f32[11,8,128]{2,1,0:T(8,128)S(1)} collective-permute-done((f32[11,8,128]{2,1,0:T(8,128)S(1)}, f32[11,8,128]{2,1,0:T(8,128)S(1)}, u32[]{:S(2)}, u32[]{:S(2)}) %collective-permute-start.9) | collective-permute-done | bytes 45088 | tf_op jit(solution)/shard_map/ppermute | solution.py:573
  41.6 0.0 collective-permute-done.8.up
  41.6 1.1 %levels.1 = (f32[8,8,8,128]{3,2,1,0:T(8,128)S(1)}, f32[256,128]{1,0:T(8,128)S(1)}) custom-call(f32[9,8,128]{2,1,0:T(8,128)S(1)} %get-tuple-element.30.own, f32[1,8,128]{2,1,0:T(8,128)S(1)} %collective-permute-done.6.left, f32[1,8,128]{2,1,0:T(8,128)S(1)} %collective-permute-done.7.right, f32[11,8,128]{2,1,0:T(8,128)S(1)} %collective-permute-done.8.up, ...), custom_call_target="tpu_custom_call" | custom-call | tf_op jit(solution)/shard_map/levels/pallas_call | solution.py:557
  42.8 27.4 %all_to_all.11 = f32[256,1,128]{2,1,0:T(1,128)S(1)} all-to-all(f32[256,1,128]{2,1,0:T(1,128)S(1)} %bitcast.5), channel_id=1, replica_groups=mesh['gx'=16,'gy'=16] {'gx','gy'}, dimensions={0} | all-to-all | bytes 262144 | tf_op jit(solution)/shard_map/all_to_all | solution.py:633
  70.1 1.1 %combine.1 = f32[8,8,128]{2,1,0:T(8,128)} custom-call(f32[256,128]{1,0:T(8,128)S(1)} %bitcast.4, f32[8,8,8,128]{3,2,1,0:T(8,128)S(1)} %get-tuple-element.38.levels, f32[8,8,128]{2,1,0:T(8,128)S(1)} %get-tuple-element.23.pot), custom_call_target="tpu_custom_call" | custom-call | tf_op jit(solution)/shard_map/combine/pallas_call | solution.py:557
  (6 shorter events, 0.0 us)
Async XLA Ops:
  2.3 20.4 %collective-permute-start = (f32[100,8,128]{2,1,0:T(8,128)S(1)}, f32[100,8,128]{2,1,0:T(8,128)S(1)}, u32[]{:S(2)}, u32[]{:S(2)}) collective-permute-start(f32[100,8,128]{2,1,0:T(8,128)S(1)} %get-tuple-element.28), channel_id=1, source_target_pairs={{0,15},{1,0},{2,1},{3,2},{4,3},{5,4},{6,5},{7,6},{8,7},{9,8},{10,9... | collective-permute-start | bytes 1228808 | tf_op jit(solution)/shard_map/ppermute | solution.py:573
  8.1 14.6 %collective-permute-start.1 = (f32[100,8,128]{2,1,0:T(8,128)S(1)}, f32[100,8,128]{2,1,0:T(8,128)S(1)}, u32[]{:S(2)}, u32[]{:S(2)}) collective-permute-start(f32[100,8,128]{2,1,0:T(8,128)S(1)} %get-tuple-element.29), channel_id=1, source_target_pairs={{0,1},{1,2},{2,3},{3,4},{4,5},{5,6},{6,7},{7,8},{8,9},{9,10},{10,1... | collective-permute-start | bytes 1228808 | tf_op jit(solution)/shard_map/ppermute | solution.py:573
  8.1 4.3 %collective-permute-start.2 = (f32[7,8,128]{2,1,0:T(8,128)S(1)}, f32[7,8,128]{2,1,0:T(8,128)S(1)}, u32[]{:S(2)}, u32[]{:S(2)}) collective-permute-start(f32[7,8,128]{2,1,0:T(8,128)S(1)} %get-tuple-element.26.x_left), channel_id=1, source_target_pairs={{0,240},{16,0},{32,16},{48,32},{64,48},{80,64},{96,80},{112,96},{1... | collective-permute-start | bytes 86024 | tf_op jit(solution)/shard_map/ppermute | solution.py:573
  9.1 5.7 %collective-permute-start.3 = (f32[7,8,128]{2,1,0:T(8,128)S(1)}, f32[7,8,128]{2,1,0:T(8,128)S(1)}, u32[]{:S(2)}, u32[]{:S(2)}) collective-permute-start(f32[7,8,128]{2,1,0:T(8,128)S(1)} %get-tuple-element.27.x_right), channel_id=1, source_target_pairs={{0,16},{16,32},{32,48},{48,64},{64,80},{80,96},{96,112},{112,128},... | collective-permute-start | bytes 86024 | tf_op jit(solution)/shard_map/ppermute | solution.py:573
  14.8 7.9 %collective-permute-start.5 = (f32[14,8,128]{2,1,0:T(8,128)S(1)}, f32[14,8,128]{2,1,0:T(8,128)S(1)}, u32[]{:S(2)}, u32[]{:S(2)}) collective-permute-start(f32[14,8,128]{2,1,0:T(8,128)S(1)} %constant_dynamic-update-slice_fusion), channel_id=1, source_target_pairs={{0,1},{1,2},{2,3},{3,4},{4,5},{5,6},{6,7},{7,8},{8,9},{9,10},{10,1... | collective-permute-start | bytes 172040 | tf_op jit(solution)/shard_map/ppermute | solution.py:573
  14.8 7.9 %collective-permute-start.4 = (f32[14,8,128]{2,1,0:T(8,128)S(1)}, f32[14,8,128]{2,1,0:T(8,128)S(1)}, u32[]{:S(2)}, u32[]{:S(2)}) collective-permute-start(f32[14,8,128]{2,1,0:T(8,128)S(1)} %constant_dynamic-update-slice_fusion), channel_id=1, source_target_pairs={{0,15},{1,0},{2,1},{3,2},{4,3},{5,4},{6,5},{7,6},{8,7},{9,8},{10,9... | collective-permute-start | bytes 172040 | tf_op jit(solution)/shard_map/ppermute | solution.py:573
  28.8 4.7 %collective-permute-start.7 = (f32[1,8,128]{2,1,0:T(8,128)S(1)}, f32[1,8,128]{2,1,0:T(8,128)S(1)}, u32[]{:S(2)}, u32[]{:S(2)}) collective-permute-start(f32[1,8,128]{2,1,0:T(8,128)S(1)} %slice.3), channel_id=1, source_target_pairs={{0,240},{16,0},{32,16},{48,32},{64,48},{80,64},{96,80},{112,96},{1... | collective-permute-start | bytes 12296 | tf_op jit(solution)/shard_map/ppermute | solution.py:573
  32.2 3.2 %collective-permute-start.6 = (f32[1,8,128]{2,1,0:T(8,128)S(1)}, f32[1,8,128]{2,1,0:T(8,128)S(1)}, u32[]{:S(2)}, u32[]{:S(2)}) collective-permute-start(f32[1,8,128]{2,1,0:T(8,128)S(1)} %slice.3), channel_id=1, source_target_pairs={{0,16},{16,32},{32,48},{48,64},{64,80},{80,96},{96,112},{112,128},... | collective-permute-start | bytes 12296 | tf_op jit(solution)/shard_map/ppermute | solution.py:573
  35.4 6.2 %collective-permute-start.9 = (f32[11,8,128]{2,1,0:T(8,128)S(1)}, f32[11,8,128]{2,1,0:T(8,128)S(1)}, u32[]{:S(2)}, u32[]{:S(2)}) collective-permute-start(f32[11,8,128]{2,1,0:T(8,128)S(1)} %constant_dynamic-update-slice_fusion.2), channel_id=1, source_target_pairs={{0,1},{1,2},{2,3},{3,4},{4,5},{5,6},{6,7},{7,8},{8,9},{9,10},{10,1... | collective-permute-start | bytes 135176 | tf_op jit(solution)/shard_map/ppermute | solution.py:573
  35.4 6.2 %collective-permute-start.8 = (f32[11,8,128]{2,1,0:T(8,128)S(1)}, f32[11,8,128]{2,1,0:T(8,128)S(1)}, u32[]{:S(2)}, u32[]{:S(2)}) collective-permute-start(f32[11,8,128]{2,1,0:T(8,128)S(1)} %constant_dynamic-update-slice_fusion.2), channel_id=1, source_target_pairs={{0,15},{1,0},{2,1},{3,2},{4,3},{5,4},{6,5},{7,6},{8,7},{9,8},{10,9... | collective-permute-start | bytes 135176 | tf_op jit(solution)/shard_map/ppermute | solution.py:573

commit v5 on v4

--- a/solution.py
+++ b/solution.py
@@ -40,6 +40,7 @@
 
 FIELDS = 25
 XT = 7
+YT = 97
 F_CONC, F_FLUID, F_POT, F_POT2 = 19, 22, 23, 24
 SLABS = 9
 TILE = (8, 128)
@@ -67,17 +68,19 @@
     return (lane >= start) & (lane < start + width)
 
 
-def pack_kernel(*refs):
-    sources, copies = refs[:5], refs[5:10]
-    x_left, x_right, y_down, y_up, sems = refs[10:]
-    moves = [
-        pltpu.make_async_copy(sources[i], copies[i], sems.at[i]) for i in (0, 1, 2, 3, 4)
-    ]
+def pack_kernel(
+    pop_in, conc_in, pot_in, solid_in, sign_in, pop, conc, pot, solid, sign,
+    x_left, x_right, y_down, y_up, sems,
+):
+    lane, row = lane_id(), row_id()
+    top = row < 4
+    moves = []
+    for i, (source, copy) in enumerate(
+        ((pop_in, pop), (conc_in, conc), (pot_in, pot), (solid_in, solid), (sign_in, sign))
+    ):
+        moves.append(pltpu.make_async_copy(source, copy, sems.at[i]))
     for move in moves:
         move.start()
-    pop, conc, pot, solid = copies[:4]
-    lane, row = lane_id(), row_id()
-    top = row < 4
     for move in moves:
         move.wait()
 
@@ -103,17 +106,21 @@
                 here = in_lanes(lane, at, 4)
                 left = jnp.where(here, rl(v, at - inner), left)
                 right = jnp.where(here, rl(v, at - (124 - inner)), right)
+            if k == F_POT2:
+                low, high = tile(k, 0), tile(k, 0)
+                low, high = rs(low, -4), rs(high, -3)
+                for z in range(1, 8):
+                    low = jnp.where(row == z, rs(tile(k, z), z - 4), low)
+                    high = jnp.where(row == z, rs(tile(k, z), z - 3), high)
+                y_down[4 * k] = low
+                y_up[4 * k] = high
+                continue
+            for pair in range(4):
+                a, b = tile(k, 2 * pair), tile(k, 2 * pair + 1)
+                y_down[4 * k + pair] = jnp.where(top, a, rs(b, 4))
+                y_up[4 * k + pair] = jnp.where(top, rs(a, 4), b)
         x_left[t] = left
         x_right[t] = right
-    for k in range(FIELDS):
-        for pair in range(4):
-            a, b = tile(k, 2 * pair), tile(k, 2 * pair + 1)
-            low = jnp.where(top, a, rs(b, 4))
-            high = jnp.where(top, rs(a, 4), b)
-            if k == F_POT2:
-                low, high = high, low
-            y_down[4 * k + pair] = low
-            y_up[4 * k + pair] = high
 
 
 def y_shift(a, b, cy, halves=(0, 1)):
@@ -161,8 +168,8 @@
 
 def step_kernel(
     pop, conc, pot, solid, sign, x_left, x_right, up, down, from_right, from_left, corner_up,
-    corner_down, g, mask, conc_out, edge_out,
-    f, below_rows, vel, cc, cn, fluid, pt, dpot, field, flux,
+    corner_down, g, mask, cn, edge_out,
+    f, below_rows, vel, cc, fluid, pt, dpot, field, flux,
 ):
     lane, row = lane_id(), row_id()
     top = row < 4
@@ -221,11 +228,12 @@
             for h in range(2):
                 mask[i - 1, 2 * s + h] = moved[s][h] * fluid[2 * s + h]
 
-    far = [halves(F_POT2, z) for z in range(8)]
+    u, d = up[4 * F_POT2], down[4 * F_POT2]
+    far = [jnp.where(row == 3, rs(u, 3 - z), rs(d, 4 - z)) for z in range(8)]
     t2, q2 = F_POT2 // 4, F_POT2 % 4
     tp = F_POT // 4
-    far_low = jnp.where(top, rs(corner_up[XT + tp], 4), rs(corner_down[XT + tp], 4))
-    far_high = jnp.where(top, rs(corner_up[tp], 4), rs(corner_down[tp], 4))
+    far_low = jnp.where(row == 3, rs(corner_up[XT + tp], -1), rs(corner_down[XT + tp], 1))
+    far_high = jnp.where(row == 3, rs(corner_up[tp], -1), rs(corner_down[tp], 1))
     far.append(strip(F_POT, far, far_low, far_high))
     edge_low = (from_left[t2], jnp.where(top, corner_up[XT + t2], corner_down[XT + t2]))
     edge_high = (from_right[t2], jnp.where(top, corner_up[t2], corner_down[t2]))
@@ -238,8 +246,8 @@
             for h in range(2):
                 lo, hi = below[s][h], above[s][h]
                 if axis == 1 and h == 1:
-                    lo = jnp.where(row == 4, rs(far[s], -3), lo)
-                    hi = jnp.where(row == 3, rs(far[s], 3), hi)
+                    lo = jnp.where(row == 4, far[s], lo)
+                    hi = jnp.where(row == 3, far[s], hi)
                 if axis == 2 and s == 8:
                     lo = jnp.where(slot == 0, rl(edge_low[h], -4 * q2 - 3), lo)
                     hi = jnp.where(slot == 15, rl(edge_high[h], 15 - 4 * q2), hi)
@@ -377,8 +385,6 @@
     for z in range(8):
         n = 2 * z
         c = [cn[k, n] for k in range(3)]
-        for k in range(3):
-            conc_out[k, z] = c[k]
         open_cell = fluid[n]
         target = open_cell * (
             valences[0] * c[0] + valences[1] * c[1] + valences[2] * c[2]
@@ -397,13 +403,12 @@
     (
         (19, 2 * SLABS, 8, 128),
         (18, 2 * SLABS, 8, 128),
-        (3, 8, 8, 128),
+        (3, 2 * SLABS, 8, 128),
         (9, 8, 128),
     ),
     (
         (19, 2 * SLABS, 8, 128),
         (19, 8, 8, 128),
-        (3, 2 * SLABS, 8, 128),
         (3, 2 * SLABS, 8, 128),
         (3, 2 * SLABS, 8, 128),
         (2 * SLABS, 8, 128),
@@ -415,8 +420,10 @@
 )
 
 
-def finish_kernel(g, mask, pop_out):
+def finish_kernel(g, mask, conc, pop_out, conc_out):
     for z in range(8):
+        for k in range(3):
+            conc_out[k, z] = conc[k, 2 * z]
         pop_out[0, z] = g[0, 2 * z]
     for i in range(1, 19):
         moved = shifted(lambda s, i=i: g[i, s], lattice_velocity[i], own=True)
@@ -504,16 +511,18 @@
             if i + j < 16:
                 gram[i, j] = gram[j, i] = 0.5 * (moment[i + j] + moment[j - i])
 
+    def add_up(terms):
+        while len(terms) > 1:
+            terms = [
+                terms[i] + terms[i + 1] if i + 1 < len(terms) else terms[i]
+                for i in range(0, len(terms), 2)
+            ]
+        return terms[0]
+
     def inner(a, b):
-        running = None
-        for i, x in enumerate(a):
-            row = None
-            for j, y in enumerate(b):
-                term = gram[i, j] * y
-                row = term if row is None else row + term
-            row = x * row
-            running = row if running is None else running + row
-        return running
+        return add_up(
+            [x * add_up([gram[i, j] * y for j, y in enumerate(b)]) for i, x in enumerate(a)]
+        )
 
     one, zero = jnp.ones(TILE, jnp.float32), jnp.zeros(TILE, jnp.float32)
     search, rest, found = [one], [one], []
@@ -582,7 +591,7 @@
         pack_kernel,
         "pack",
         tuple(jax.ShapeDtypeStruct(a.shape, a.dtype) for a in inputs)
-        + (f32(XT, 8, 128), f32(XT, 8, 128), f32(4 * FIELDS, 8, 128), f32(4 * FIELDS, 8, 128)),
+        + (f32(XT, 8, 128), f32(XT, 8, 128), f32(YT, 8, 128), f32(YT, 8, 128)),
         [pltpu.SemaphoreType.DMA((5,))],
         *inputs,
         in_specs=[pl.BlockSpec(memory_space=pltpu.HBM)] * 5,
@@ -595,7 +604,7 @@
     corner = jnp.concatenate([from_right, from_left])
     corner_up = send(corner, "gy", -1)
     corner_down = send(corner, "gy", 1)
-    relaxed, mask, conc_new, edge = call(
+    relaxed, mask, conc_last, edge = call(
         step_kernel,
         "steps",
         tuple(f32(*shape) for shape in STEP_SHAPES[0]),
@@ -613,8 +622,16 @@
     strip = edge[8:]
     left = send(strip, "gx", 1)
     right = send(strip, "gx", -1)
-    (pop_new,) = call(finish_kernel, "finish", (f32(19, 8, 8, 128),), [], relaxed, mask)
-    left, right, pop_new = lax.optimization_barrier((left, right, pop_new))
+    pop_new, conc_new = call(
+        finish_kernel,
+        "finish",
+        (f32(19, 8, 8, 128), f32(3, 8, 8, 128)),
+        [],
+        relaxed,
+        mask,
+        conc_last,
+    )
+    left, right, pop_new, conc_new = lax.optimization_barrier((left, right, pop_new, conc_new))
     wide = jnp.concatenate([edge, left, right])
     above = send(wide, "gy", -1)
     below = send(wide, "gy", 1)

time: 71.4 us -> 70.6 us (0.989)
  transfers between devices with their start and end apart: 10 -> 10, of which waited for: 6 -> 5; matrix products, arithmetic and copies ran while one was open for 0% -> 0% of each run, Pallas kernels for 2% -> 2%
where the time goes in v5:
time: 70.6 us; the launch traced here: 70.5 us
  blocking collectives  27.4 us (39%)
  starting transfers between devices  21.6 us (31%)
  Pallas kernels  10.5 us (15%)
  waiting for transfers between devices  10.3 us (15%)
    all_to_all x1, blocking collectives, local(): rows = lax.all_to_all(rows, ('gx', 'gy'), 0, 0, tiled=True)  27.4 us
    ppermute x10, starting transfers between devices, send(): lax.ppermute(block, axis, [(i, (i + step) % count) for i in range(count)])  21.6 us
    pallas_call x5, Pallas kernels, call(): pl.pallas_call(kernel, name=name, out_shape=outs, in_specs=in_specs or in...  10.5 us
    ppermute x10, waiting for transfers between devices, send(): lax.ppermute(block, axis, [(i, (i + step) % count) for i in range(count)])  10.3 us
  transfers between devices with their start and end apart: 10, of which 5 were waited for; matrix products, arithmetic and copies ran while one was open for 0% of the time, Pallas kernels for 2%

profile of v5, /device:TPU:1, one launch (start us, length us, event | category | flops | bytes accessed | tf_op | source)
XLA Modules:
  0.0 70.5 jit_solution(17669147470119801738)
XLA Ops:
  0.6 1.6 %pack.1 = (f32[19,8,8,128]{3,2,1,0:T(8,128)S(1)}, f32[3,8,8,128]{3,2,1,0:T(8,128)S(1)}, f32[8,8,128]{2,1,0:T(8,128)S(1)}, s32[8,8,128]{2,1,0:T(8,128)S(1)}, s32[...) custom-call(f32[19,8,8,128]{3,2,1,0:T(8,128)} %pop_in.1, ...), custom_call_target="tpu_custom_call" | custom-call | tf_op jit(solution)/shard_map/pack/pallas_call | solution.py:566
  2.3 5.8 %collective-permute-start = (f32[97,8,128]{2,1,0:T(8,128)S(1)}, f32[97,8,128]{2,1,0:T(8,128)S(1)}, u32[]{:S(2)}, u32[]{:S(2)}) collective-permute-start(f32[97,8,128]{2,1,0:T(8,128)S(1)} %get-tuple-element.31), channel_id=1, source_target_pairs={{0,15},{1,0},{2,1},{3,2},{4,3},{5,4},{6,5},{7,6},{8,7},{9,8},{10,9... | collective-permute-start | bytes 1191944 | tf_op jit(solution)/shard_map/ppermute | solution.py:582
  8.1 0.0 collective-permute-start.1
  8.1 1.0 %collective-permute-start.2 = (f32[7,8,128]{2,1,0:T(8,128)S(1)}, f32[7,8,128]{2,1,0:T(8,128)S(1)}, u32[]{:S(2)}, u32[]{:S(2)}) collective-permute-start(f32[7,8,128]{2,1,0:T(8,128)S(1)} %get-tuple-element.29.x_left), channel_id=1, source_target_pairs={{0,240},{16,0},{32,16},{48,32},{64,48},{80,64},{96,80},{112,96},{1... | collective-permute-start | bytes 86024 | tf_op jit(solution)/shard_map/ppermute | solution.py:582
  9.1 1.5 %collective-permute-start.3 = (f32[7,8,128]{2,1,0:T(8,128)S(1)}, f32[7,8,128]{2,1,0:T(8,128)S(1)}, u32[]{:S(2)}, u32[]{:S(2)}) collective-permute-start(f32[7,8,128]{2,1,0:T(8,128)S(1)} %get-tuple-element.30.x_right), channel_id=1, source_target_pairs={{0,16},{16,32},{32,48},{48,64},{64,80},{80,96},{96,112},{112,128},... | collective-permute-start | bytes 86024 | tf_op jit(solution)/shard_map/ppermute | solution.py:582
  10.6 1.8 %collective-permute-done.2.from_right = f32[7,8,128]{2,1,0:T(8,128)S(1)} collective-permute-done((f32[7,8,128]{2,1,0:T(8,128)S(1)}, f32[7,8,128]{2,1,0:T(8,128)S(1)}, u32[]{:S(2)}, u32[]{:S(2)}) %collective-permute-start.2) | collective-permute-done | bytes 28704 | tf_op jit(solution)/shard_map/ppermute | solution.py:582
  12.4 2.3 %collective-permute-done.3.from_left = f32[7,8,128]{2,1,0:T(8,128)S(1)} collective-permute-done((f32[7,8,128]{2,1,0:T(8,128)S(1)}, f32[7,8,128]{2,1,0:T(8,128)S(1)}, u32[]{:S(2)}, u32[]{:S(2)}) %collective-permute-start.3) | collective-permute-done | bytes 28704 | tf_op jit(solution)/shard_map/ppermute | solution.py:582
  14.8 0.0 collective-permute-start.5
  14.8 4.8 %collective-permute-start.4 = (f32[14,8,128]{2,1,0:T(8,128)S(1)}, f32[14,8,128]{2,1,0:T(8,128)S(1)}, u32[]{:S(2)}, u32[]{:S(2)}) collective-permute-start(f32[14,8,128]{2,1,0:T(8,128)S(1)} %constant_dynamic-update-slice_fusion), channel_id=1, source_target_pairs={{0,15},{1,0},{2,1},{3,2},{4,3},{5,4},{6,5},{7,6},{8,7},{9,8},{10,9... | collective-permute-start | bytes 172040 | tf_op jit(solution)/shard_map/ppermute | solution.py:582
  19.6 2.8 %collective-permute-done.5.corner_down = f32[14,8,128]{2,1,0:T(8,128)S(1)} collective-permute-done((f32[14,8,128]{2,1,0:T(8,128)S(1)}, f32[14,8,128]{2,1,0:T(8,128)S(1)}, u32[]{:S(2)}, u32[]{:S(2)}) %collective-permute-start.5) | collective-permute-done | bytes 57376 | tf_op jit(solution)/shard_map/ppermute | solution.py:582
  22.4 0.0 collective-permute-done.4.corner_up
  22.4 0.0 collective-permute-done.up
  22.4 0.0 collective-permute-done.1.down
  22.4 5.6 %steps.1 = (f32[19,18,8,128]{3,2,1,0:T(8,128)S(1)}, f32[18,18,8,128]{3,2,1,0:T(8,128)S(1)}, f32[3,18,8,128]{3,2,1,0:T(8,128)S(1)}, f32[9,8,128]{2,1,0:T(8,128)S(1)}) custom-call(f32[19,8,8,128]{3,2,1,0:T(8,128)S(1)} %get-tuple-element.24.pop, f32[3,8,8,128]{3,2,1,0:T(8,128)S(1)} %get-tuple-element.25.conc, f32[8,8,128]{2,1,0:T(8,128)S(1)} %get-tuple-element.26.pot, ...), custom_call_target="tpu_custom_call" | custom-call | tf_op jit(solution)/shard_map/steps/pallas_call | solution.py:566
  28.0 3.7 %collective-permute-start.7 = (f32[1,8,128]{2,1,0:T(8,128)S(1)}, f32[1,8,128]{2,1,0:T(8,128)S(1)}, u32[]{:S(2)}, u32[]{:S(2)}) collective-permute-start(f32[1,8,128]{2,1,0:T(8,128)S(1)} %slice.3), channel_id=1, source_target_pairs={{0,240},{16,0},{32,16},{48,32},{64,48},{80,64},{96,80},{112,96},{1... | collective-permute-start | bytes 12296 | tf_op jit(solution)/shard_map/ppermute | solution.py:582
  31.7 0.0 collective-permute-start.6
  31.7 1.1 %finish.1 = (f32[19,8,8,128]{3,2,1,0:T(8,128)}, f32[3,8,8,128]{3,2,1,0:T(8,128)}) custom-call(f32[19,18,8,128]{3,2,1,0:T(8,128)S(1)} %get-tuple-element.34.g, f32[18,18,8,128]{3,2,1,0:T(8,128)S(1)} %get-tuple-element.35.mask, f32[3,18,8,128]{3,2,1,0:T(8,128)S(1)} %get-tuple-element.36.conc), custom_call_target="tpu_custom_call" | custom-call | tf_op jit(solution)/shard_map/finish/pallas_call | solution.py:566
  32.8 0.0 collective-permute-done.7.right
  32.8 1.9 %collective-permute-done.6.left = f32[1,8,128]{2,1,0:T(8,128)S(1)} collective-permute-done((f32[1,8,128]{2,1,0:T(8,128)S(1)}, f32[1,8,128]{2,1,0:T(8,128)S(1)}, u32[]{:S(2)}, u32[]{:S(2)}) %collective-permute-start.6) | collective-permute-done | bytes 4128 | tf_op jit(solution)/shard_map/ppermute | solution.py:582
  34.7 0.0 collective-permute-start.9
  34.7 4.8 %collective-permute-start.8 = (f32[11,8,128]{2,1,0:T(8,128)S(1)}, f32[11,8,128]{2,1,0:T(8,128)S(1)}, u32[]{:S(2)}, u32[]{:S(2)}) collective-permute-start(f32[11,8,128]{2,1,0:T(8,128)S(1)} %constant_dynamic-update-slice_fusion.2), channel_id=1, source_target_pairs={{0,15},{1,0},{2,1},{3,2},{4,3},{5,4},{6,5},{7,6},{8,7},{9,8},{10,9... | collective-permute-start | bytes 135176 | tf_op jit(solution)/shard_map/ppermute | solution.py:582
  39.4 1.4 %collective-permute-done.9.down = f32[11,8,128]{2,1,0:T(8,128)S(1)} collective-permute-done((f32[11,8,128]{2,1,0:T(8,128)S(1)}, f32[11,8,128]{2,1,0:T(8,128)S(1)}, u32[]{:S(2)}, u32[]{:S(2)}) %collective-permute-start.9) | collective-permute-done | bytes 45088 | tf_op jit(solution)/shard_map/ppermute | solution.py:582
  40.9 0.0 collective-permute-done.8.up
  40.9 1.1 %levels.1 = (f32[8,8,8,128]{3,2,1,0:T(8,128)S(1)}, f32[256,128]{1,0:T(8,128)S(1)}) custom-call(f32[9,8,128]{2,1,0:T(8,128)S(1)} %get-tuple-element.33.own, f32[1,8,128]{2,1,0:T(8,128)S(1)} %collective-permute-done.6.left, f32[1,8,128]{2,1,0:T(8,128)S(1)} %collective-permute-done.7.right, f32[11,8,128]{2,1,0:T(8,128)S(1)} %collective-permute-done.8.up, ...), custom_call_target="tpu_custom_call" | custom-call | tf_op jit(solution)/shard_map/levels/pallas_call | solution.py:566
  42.0 27.4 %all_to_all.11 = f32[256,1,128]{2,1,0:T(1,128)S(1)} all-to-all(f32[256,1,128]{2,1,0:T(1,128)S(1)} %bitcast.5), channel_id=1, replica_groups=mesh['gx'=16,'gy'=16] {'gx','gy'}, dimensions={0} | all-to-all | bytes 262144 | tf_op jit(solution)/shard_map/all_to_all | solution.py:650
  69.4 1.1 %combine.1 = f32[8,8,128]{2,1,0:T(8,128)} custom-call(f32[256,128]{1,0:T(8,128)S(1)} %bitcast.4, f32[8,8,8,128]{3,2,1,0:T(8,128)S(1)} %get-tuple-element.44.levels, f32[8,8,128]{2,1,0:T(8,128)S(1)} %get-tuple-element.26.pot), custom_call_target="tpu_custom_call" | custom-call | tf_op jit(solution)/shard_map/combine/pallas_call | solution.py:566
  (6 shorter events, 0.0 us)
Async XLA Ops:
  2.3 20.1 %collective-permute-start = (f32[97,8,128]{2,1,0:T(8,128)S(1)}, f32[97,8,128]{2,1,0:T(8,128)S(1)}, u32[]{:S(2)}, u32[]{:S(2)}) collective-permute-start(f32[97,8,128]{2,1,0:T(8,128)S(1)} %get-tuple-element.31), channel_id=1, source_target_pairs={{0,15},{1,0},{2,1},{3,2},{4,3},{5,4},{6,5},{7,6},{8,7},{9,8},{10,9... | collective-permute-start | bytes 1191944 | tf_op jit(solution)/shard_map/ppermute | solution.py:582
  8.1 14.3 %collective-permute-start.1 = (f32[97,8,128]{2,1,0:T(8,128)S(1)}, f32[97,8,128]{2,1,0:T(8,128)S(1)}, u32[]{:S(2)}, u32[]{:S(2)}) collective-permute-start(f32[97,8,128]{2,1,0:T(8,128)S(1)} %get-tuple-element.32), channel_id=1, source_target_pairs={{0,1},{1,2},{2,3},{3,4},{4,5},{5,6},{6,7},{7,8},{8,9},{9,10},{10,1... | collective-permute-start | bytes 1191944 | tf_op jit(solution)/shard_map/ppermute | solution.py:582
  8.1 4.3 %collective-permute-start.2 = (f32[7,8,128]{2,1,0:T(8,128)S(1)}, f32[7,8,128]{2,1,0:T(8,128)S(1)}, u32[]{:S(2)}, u32[]{:S(2)}) collective-permute-start(f32[7,8,128]{2,1,0:T(8,128)S(1)} %get-tuple-element.29.x_left), channel_id=1, source_target_pairs={{0,240},{16,0},{32,16},{48,32},{64,48},{80,64},{96,80},{112,96},{1... | collective-permute-start | bytes 86024 | tf_op jit(solution)/shard_map/ppermute | solution.py:582
  9.1 5.7 %collective-permute-start.3 = (f32[7,8,128]{2,1,0:T(8,128)S(1)}, f32[7,8,128]{2,1,0:T(8,128)S(1)}, u32[]{:S(2)}, u32[]{:S(2)}) collective-permute-start(f32[7,8,128]{2,1,0:T(8,128)S(1)} %get-tuple-element.30.x_right), channel_id=1, source_target_pairs={{0,16},{16,32},{32,48},{48,64},{64,80},{80,96},{96,112},{112,128},... | collective-permute-start | bytes 86024 | tf_op jit(solution)/shard_map/ppermute | solution.py:582
  14.8 7.6 %collective-permute-start.5 = (f32[14,8,128]{2,1,0:T(8,128)S(1)}, f32[14,8,128]{2,1,0:T(8,128)S(1)}, u32[]{:S(2)}, u32[]{:S(2)}) collective-permute-start(f32[14,8,128]{2,1,0:T(8,128)S(1)} %constant_dynamic-update-slice_fusion), channel_id=1, source_target_pairs={{0,1},{1,2},{2,3},{3,4},{4,5},{5,6},{6,7},{7,8},{8,9},{9,10},{10,1... | collective-permute-start | bytes 172040 | tf_op jit(solution)/shard_map/ppermute | solution.py:582
  14.8 7.6 %collective-permute-start.4 = (f32[14,8,128]{2,1,0:T(8,128)S(1)}, f32[14,8,128]{2,1,0:T(8,128)S(1)}, u32[]{:S(2)}, u32[]{:S(2)}) collective-permute-start(f32[14,8,128]{2,1,0:T(8,128)S(1)} %constant_dynamic-update-slice_fusion), channel_id=1, source_target_pairs={{0,15},{1,0},{2,1},{3,2},{4,3},{5,4},{6,5},{7,6},{8,7},{9,8},{10,9... | collective-permute-start | bytes 172040 | tf_op jit(solution)/shard_map/ppermute | solution.py:582
  28.0 4.8 %collective-permute-start.7 = (f32[1,8,128]{2,1,0:T(8,128)S(1)}, f32[1,8,128]{2,1,0:T(8,128)S(1)}, u32[]{:S(2)}, u32[]{:S(2)}) collective-permute-start(f32[1,8,128]{2,1,0:T(8,128)S(1)} %slice.3), channel_id=1, source_target_pairs={{0,240},{16,0},{32,16},{48,32},{64,48},{80,64},{96,80},{112,96},{1... | collective-permute-start | bytes 12296 | tf_op jit(solution)/shard_map/ppermute | solution.py:582
  31.7 2.9 %collective-permute-start.6 = (f32[1,8,128]{2,1,0:T(8,128)S(1)}, f32[1,8,128]{2,1,0:T(8,128)S(1)}, u32[]{:S(2)}, u32[]{:S(2)}) collective-permute-start(f32[1,8,128]{2,1,0:T(8,128)S(1)} %slice.3), channel_id=1, source_target_pairs={{0,16},{16,32},{32,48},{48,64},{64,80},{80,96},{96,112},{112,128},... | collective-permute-start | bytes 12296 | tf_op jit(solution)/shard_map/ppermute | solution.py:582
  34.7 6.2 %collective-permute-start.9 = (f32[11,8,128]{2,1,0:T(8,128)S(1)}, f32[11,8,128]{2,1,0:T(8,128)S(1)}, u32[]{:S(2)}, u32[]{:S(2)}) collective-permute-start(f32[11,8,128]{2,1,0:T(8,128)S(1)} %constant_dynamic-update-slice_fusion.2), channel_id=1, source_target_pairs={{0,1},{1,2},{2,3},{3,4},{4,5},{5,6},{6,7},{7,8},{8,9},{9,10},{10,1... | collective-permute-start | bytes 135176 | tf_op jit(solution)/shard_map/ppermute | solution.py:582
  34.7 6.2 %collective-permute-start.8 = (f32[11,8,128]{2,1,0:T(8,128)S(1)}, f32[11,8,128]{2,1,0:T(8,128)S(1)}, u32[]{:S(2)}, u32[]{:S(2)}) collective-permute-start(f32[11,8,128]{2,1,0:T(8,128)S(1)} %constant_dynamic-update-slice_fusion.2), channel_id=1, source_target_pairs={{0,15},{1,0},{2,1},{3,2},{4,3},{5,4},{6,5},{7,6},{8,7},{9,8},{10,9... | collective-permute-start | bytes 135176 | tf_op jit(solution)/shard_map/ppermute | solution.py:582

commit v6 on v5

--- a/solution.py
+++ b/solution.py
@@ -123,6 +123,18 @@
         x_right[t] = right
 
 
+def corner_kernel(right, left, down_out, up_out):
+    top = row_id() < 4
+    for t in range(XT):
+        a, b = right[t], rs(left[t], 4)
+        down_out[t] = jnp.where(top, a, b)
+        up_out[t] = jnp.where(top, b, a)
+    tp = F_POT // 4
+    a, b = rs(right[tp], 4), left[tp]
+    down_out[XT] = jnp.where(top, a, b)
+    up_out[XT] = jnp.where(top, b, a)
+
+
 def y_shift(a, b, cy, halves=(0, 1)):
     if cy == 0:
         return a, b
@@ -167,7 +179,7 @@
 
 
 def step_kernel(
-    pop, conc, pot, solid, sign, x_left, x_right, up, down, from_right, from_left, corner_up,
+    pop, conc, pot, solid, sign, x_left, x_right, down, up, from_right, from_left, corner_up,
     corner_down, g, mask, cn, edge_out,
     f, below_rows, vel, cc, fluid, pt, dpot, field, flux,
 ):
@@ -189,10 +201,13 @@
             out = jnp.where(in_lanes(lane, 16 * z + 8, 4), rl(tiles[z], 16 * z + 8 - 124), out)
         return out
 
+    def corners(t):
+        u, d = corner_up[t], corner_down[t]
+        return rs(jnp.where(top, d, u), 4), jnp.where(top, u, d)
+
     def strips(k, b):
         t = k // 4
-        low = jnp.where(top, corner_up[XT + t], corner_down[XT + t])
-        high = jnp.where(top, corner_up[t], corner_down[t])
+        low, high = corners(t)
         q = k % 4
         mine = jnp.where(
             slot < 8,
@@ -231,12 +246,12 @@
     u, d = up[4 * F_POT2], down[4 * F_POT2]
     far = [jnp.where(row == 3, rs(u, 3 - z), rs(d, 4 - z)) for z in range(8)]
     t2, q2 = F_POT2 // 4, F_POT2 % 4
-    tp = F_POT // 4
-    far_low = jnp.where(row == 3, rs(corner_up[XT + tp], -1), rs(corner_down[XT + tp], 1))
-    far_high = jnp.where(row == 3, rs(corner_up[tp], -1), rs(corner_down[tp], 1))
+    u, d = corner_up[XT], corner_down[XT]
+    far_low = jnp.where(row == 3, rs(u, -1), rs(d, 1))
+    far_high = jnp.where(row == 3, rs(u, 3), rs(d, -3))
     far.append(strip(F_POT, far, far_low, far_high))
-    edge_low = (from_left[t2], jnp.where(top, corner_up[XT + t2], corner_down[XT + t2]))
-    edge_high = (from_right[t2], jnp.where(top, corner_up[t2], corner_down[t2]))
+    low, high = corners(t2)
+    edge_low, edge_high = (from_left[t2], low), (from_right[t2], high)
     for axis in range(3):
         plus = tuple(1 if d == axis else 0 for d in range(3))
         minus = tuple(-p for p in plus)
@@ -433,7 +448,7 @@
             )
 
 
-def levels_kernel(own, left, right, up, down, level_out, row_out, lv, part):
+def levels_kernel(own, left, right, down, up, level_out, row_out, lv, part):
     lane, row = lane_id(), row_id()
     slot = lane % 16
     first_row, last_row = row == 0, row == 7
@@ -601,9 +616,16 @@
     down = send(y_up, "gy", 1)
     from_right = send(x_left, "gx", -1)
     from_left = send(x_right, "gx", 1)
-    corner = jnp.concatenate([from_right, from_left])
-    corner_up = send(corner, "gy", -1)
-    corner_down = send(corner, "gy", 1)
+    corner_low, corner_high = call(
+        corner_kernel,
+        "corners",
+        (f32(XT + 1, 8, 128), f32(XT + 1, 8, 128)),
+        [],
+        from_right,
+        from_left,
+    )
+    corner_up = send(corner_low, "gy", -1)
+    corner_down = send(corner_high, "gy", 1)
     relaxed, mask, conc_last, edge = call(
         step_kernel,
         "steps",
@@ -612,8 +634,8 @@
         *kept,
         x_left,
         x_right,
+        down,
         up,
-        down,
         from_right,
         from_left,
         corner_up,
@@ -644,8 +666,8 @@
         edge,
         left,
         right,
+        below,
         above,
-        below,
     )
     rows = lax.all_to_all(rows, ("gx", "gy"), 0, 0, tiled=True)
     (pot_new,) = call(combine_kernel, "combine", (f32(8, 8, 128),), [], rows, levels, kept[2])

time: 70.6 us -> 66 us (0.935)
  starting transfers between devices: 21.6 us -> 17 us
  blocking collectives: 27.4 us -> 22.9 us
  waiting for transfers between devices: 10.3 us -> 14.8 us
    ppermute x10, starting transfers between devices: 21.6 us -> 17 us  [send(): lax.ppermute(block, axis, [(i, (i + step) % count) for i in range(count)])]
    ppermute x10, waiting for transfers between devices: 10.3 us -> 14.8 us  [send(): lax.ppermute(block, axis, [(i, (i + step) % count) for i in range(count)])]
    all_to_all x1, blocking collectives: 27.4 us -> 22.9 us  [local(): rows = lax.all_to_all(rows, ('gx', 'gy'), 0, 0, tiled=True)]
    pallas_call x5 -> x6, Pallas kernels: 10.5 us -> 10.5 us  [call(): pl.pallas_call(kernel, name=name, out_shape=outs, in_specs=in_specs or in...]
  transfers between devices with their start and end apart: 10 -> 10, of which waited for: 5 -> 7; matrix products, arithmetic and copies ran while one was open for 0% -> 0% of each run, Pallas kernels for 2% -> 2%
where the time goes in v6:
time: 66 us; the launch traced here: 65.9 us
  blocking collectives  22.9 us (35%)
  starting transfers between devices  17 us (26%)
  waiting for transfers between devices  14.8 us (22%)
  Pallas kernels  10.5 us (16%)
  between operations  0.68 us (1%)
    all_to_all x1, blocking collectives, local(): rows = lax.all_to_all(rows, ('gx', 'gy'), 0, 0, tiled=True)  22.9 us
    ppermute x10, starting transfers between devices, send(): lax.ppermute(block, axis, [(i, (i + step) % count) for i in range(count)])  17 us
    ppermute x10, waiting for transfers between devices, send(): lax.ppermute(block, axis, [(i, (i + step) % count) for i in range(count)])  14.8 us
    pallas_call x6, Pallas kernels, call(): pl.pallas_call(kernel, name=name, out_shape=outs, in_specs=in_specs or in...  10.5 us
  transfers between devices with their start and end apart: 10, of which 7 were waited for; matrix products, arithmetic and copies ran while one was open for 0% of the time, Pallas kernels for 2%

profile of v6, /device:TPU:1, one launch (start us, length us, event | category | flops | bytes accessed | tf_op | source)
XLA Modules:
  0.0 65.9 jit_solution(3600571811872378443)
XLA Ops:
  0.6 1.6 %pack.1 = (f32[19,8,8,128]{3,2,1,0:T(8,128)S(1)}, f32[3,8,8,128]{3,2,1,0:T(8,128)S(1)}, f32[8,8,128]{2,1,0:T(8,128)S(1)}, s32[8,8,128]{2,1,0:T(8,128)S(1)}, s32[...) custom-call(f32[19,8,8,128]{3,2,1,0:T(8,128)} %pop_in.1, ...), custom_call_target="tpu_custom_call" | custom-call | tf_op jit(solution)/shard_map/pack/pallas_call | solution.py:581
  2.3 2.1 %collective-permute-start = (f32[97,8,128]{2,1,0:T(8,128)S(1)}, f32[97,8,128]{2,1,0:T(8,128)S(1)}, u32[]{:S(2)}, u32[]{:S(2)}) collective-permute-start(f32[97,8,128]{2,1,0:T(8,128)S(1)} %get-tuple-element.33), channel_id=1, source_target_pairs={{0,1},{1,2},{2,3},{3,4},{4,5},{5,6},{6,7},{7,8},{8,9},{9,10},{10,1... | collective-permute-start | bytes 1191944 | tf_op jit(solution)/shard_map/ppermute | solution.py:597
  4.4 3.8 %collective-permute-start.1 = (f32[97,8,128]{2,1,0:T(8,128)S(1)}, f32[97,8,128]{2,1,0:T(8,128)S(1)}, u32[]{:S(2)}, u32[]{:S(2)}) collective-permute-start(f32[97,8,128]{2,1,0:T(8,128)S(1)} %get-tuple-element.34), channel_id=1, source_target_pairs={{0,15},{1,0},{2,1},{3,2},{4,3},{5,4},{6,5},{7,6},{8,7},{9,8},{10,9... | collective-permute-start | bytes 1191944 | tf_op jit(solution)/shard_map/ppermute | solution.py:597
  8.2 2.7 %collective-permute-start.2 = (f32[7,8,128]{2,1,0:T(8,128)S(1)}, f32[7,8,128]{2,1,0:T(8,128)S(1)}, u32[]{:S(2)}, u32[]{:S(2)}) collective-permute-start(f32[7,8,128]{2,1,0:T(8,128)S(1)} %get-tuple-element.31.x_left), channel_id=1, source_target_pairs={{0,240},{16,0},{32,16},{48,32},{64,48},{80,64},{96,80},{112,96},{1... | collective-permute-start | bytes 86024 | tf_op jit(solution)/shard_map/ppermute | solution.py:597
  10.9 0.0 collective-permute-start.3
  11.0 1.6 %collective-permute-done.2.right.from_right = f32[7,8,128]{2,1,0:T(8,128)S(1)} collective-permute-done((f32[7,8,128]{2,1,0:T(8,128)S(1)}, f32[7,8,128]{2,1,0:T(8,128)S(1)}, u32[]{:S(2)}, u32[]{:S(2)}) %collective-permute-start.2) | collective-permute-done | bytes 28704 | tf_op jit(solution)/shard_map/ppermute | solution.py:597
  12.6 2.3 %collective-permute-done.3.left.from_left = f32[7,8,128]{2,1,0:T(8,128)S(1)} collective-permute-done((f32[7,8,128]{2,1,0:T(8,128)S(1)}, f32[7,8,128]{2,1,0:T(8,128)S(1)}, u32[]{:S(2)}, u32[]{:S(2)}) %collective-permute-start.3) | collective-permute-done | bytes 28704 | tf_op jit(solution)/shard_map/ppermute | solution.py:597
  14.9 1.5 %collective-permute-start.4 = (f32[8,8,128]{2,1,0:T(8,128)S(1)}, f32[8,8,128]{2,1,0:T(8,128)S(1)}, u32[]{:S(2)}, u32[]{:S(2)}) collective-permute-start(f32[8,8,128]{2,1,0:T(8,128)S(1)} %get-tuple-element.35), channel_id=1, source_target_pairs={{0,15},{1,0},{2,1},{3,2},{4,3},{5,4},{6,5},{7,6},{8,7},{9,8},{10,9... | collective-permute-start | bytes 98312 | tf_op jit(solution)/shard_map/ppermute | solution.py:597
  16.3 0.1 collective-permute-start.5
  16.4 1.6 %collective-permute-done.4.corner_up = f32[8,8,128]{2,1,0:T(8,128)S(1)} collective-permute-done((f32[8,8,128]{2,1,0:T(8,128)S(1)}, f32[8,8,128]{2,1,0:T(8,128)S(1)}, u32[]{:S(2)}, u32[]{:S(2)}) %collective-permute-start.4) | collective-permute-done | bytes 32800 | tf_op jit(solution)/shard_map/ppermute | solution.py:597
  18.0 4.4 %collective-permute-done.5.corner_down = f32[8,8,128]{2,1,0:T(8,128)S(1)} collective-permute-done((f32[8,8,128]{2,1,0:T(8,128)S(1)}, f32[8,8,128]{2,1,0:T(8,128)S(1)}, u32[]{:S(2)}, u32[]{:S(2)}) %collective-permute-start.5) | collective-permute-done | bytes 32800 | tf_op jit(solution)/shard_map/ppermute | solution.py:597
  22.4 0.0 collective-permute-done.down
  22.4 0.0 collective-permute-done.1.up
  22.4 5.6 %steps.1 = (f32[19,18,8,128]{3,2,1,0:T(8,128)S(1)}, f32[18,18,8,128]{3,2,1,0:T(8,128)S(1)}, f32[3,18,8,128]{3,2,1,0:T(8,128)S(1)}, f32[9,8,128]{2,1,0:T(8,128)S(1)}) custom-call(f32[19,8,8,128]{3,2,1,0:T(8,128)S(1)} %get-tuple-element.26.pop, f32[3,8,8,128]{3,2,1,0:T(8,128)S(1)} %get-tuple-element.27.conc, f32[8,8,128]{2,1,0:T(8,128)S(1)} %get-tuple-element.28.pot, ...), custom_call_target="tpu_custom_call" | custom-call | tf_op jit(solution)/shard_map/steps/pallas_call | solution.py:581
  28.0 5.3 %collective-permute-start.7 = (f32[1,8,128]{2,1,0:T(8,128)S(1)}, f32[1,8,128]{2,1,0:T(8,128)S(1)}, u32[]{:S(2)}, u32[]{:S(2)}) collective-permute-start(f32[1,8,128]{2,1,0:T(8,128)S(1)} %slice.3), channel_id=1, source_target_pairs={{0,240},{16,0},{32,16},{48,32},{64,48},{80,64},{96,80},{112,96},{1... | collective-permute-start | bytes 12296 | tf_op jit(solution)/shard_map/ppermute | solution.py:597
  33.3 0.0 collective-permute-start.6
  33.3 1.1 %finish.1 = (f32[19,8,8,128]{3,2,1,0:T(8,128)}, f32[3,8,8,128]{3,2,1,0:T(8,128)}) custom-call(f32[19,18,8,128]{3,2,1,0:T(8,128)S(1)} %get-tuple-element.38.g, f32[18,18,8,128]{3,2,1,0:T(8,128)S(1)} %get-tuple-element.39.mask, f32[3,18,8,128]{3,2,1,0:T(8,128)S(1)} %get-tuple-element.40.conc), custom_call_target="tpu_custom_call" | custom-call | tf_op jit(solution)/shard_map/finish/pallas_call | solution.py:581
  34.4 0.0 collective-permute-done.7.right
  34.4 0.1 collective-permute-done.6.left
  34.5 0.1 collective-permute-start.9
  34.5 1.4 %collective-permute-start.8 = (f32[11,8,128]{2,1,0:T(8,128)S(1)}, f32[11,8,128]{2,1,0:T(8,128)S(1)}, u32[]{:S(2)}, u32[]{:S(2)}) collective-permute-start(f32[11,8,128]{2,1,0:T(8,128)S(1)} %constant_dynamic-update-slice_fusion), channel_id=1, source_target_pairs={{0,1},{1,2},{2,3},{3,4},{4,5},{5,6},{6,7},{7,8},{8,9},{9,10},{10,1... | collective-permute-start | bytes 135176 | tf_op jit(solution)/shard_map/ppermute | solution.py:597
  35.9 1.4 %collective-permute-done.9.up = f32[11,8,128]{2,1,0:T(8,128)S(1)} collective-permute-done((f32[11,8,128]{2,1,0:T(8,128)S(1)}, f32[11,8,128]{2,1,0:T(8,128)S(1)}, u32[]{:S(2)}, u32[]{:S(2)}) %collective-permute-start.9) | collective-permute-done | bytes 45088 | tf_op jit(solution)/shard_map/ppermute | solution.py:597
  37.4 3.4 %collective-permute-done.8.down = f32[11,8,128]{2,1,0:T(8,128)S(1)} collective-permute-done((f32[11,8,128]{2,1,0:T(8,128)S(1)}, f32[11,8,128]{2,1,0:T(8,128)S(1)}, u32[]{:S(2)}, u32[]{:S(2)}) %collective-permute-start.8) | collective-permute-done | bytes 45088 | tf_op jit(solution)/shard_map/ppermute | solution.py:597
  40.8 1.1 %levels.1 = (f32[8,8,8,128]{3,2,1,0:T(8,128)S(1)}, f32[256,128]{1,0:T(8,128)S(1)}) custom-call(f32[9,8,128]{2,1,0:T(8,128)S(1)} %get-tuple-element.37.own, f32[1,8,128]{2,1,0:T(8,128)S(1)} %collective-permute-done.6.left, f32[1,8,128]{2,1,0:T(8,128)S(1)} %collective-permute-done.7.right, f32[11,8,128]{2,1,0:T(8,128)S(1)} %collective-permute-done.8.down, ...), custom_call_target="tpu_custom_call" | custom-call | tf_op jit(solution)/shard_map/levels/pallas_call | solution.py:581
  41.9 22.9 %all_to_all.11 = f32[256,1,128]{2,1,0:T(1,128)S(1)} all-to-all(f32[256,1,128]{2,1,0:T(1,128)S(1)} %bitcast.5), channel_id=1, replica_groups=mesh['gx'=16,'gy'=16] {'gx','gy'}, dimensions={0} | all-to-all | bytes 262144 | tf_op jit(solution)/shard_map/all_to_all | solution.py:672
  64.8 1.1 %combine.1 = f32[8,8,128]{2,1,0:T(8,128)} custom-call(f32[256,128]{1,0:T(8,128)S(1)} %bitcast.4, f32[8,8,8,128]{3,2,1,0:T(8,128)S(1)} %get-tuple-element.48.levels, f32[8,8,128]{2,1,0:T(8,128)S(1)} %get-tuple-element.28.pot), custom_call_target="tpu_custom_call" | custom-call | tf_op jit(solution)/shard_map/combine/pallas_call | solution.py:581
  (5 shorter events, 0.0 us)
Async XLA Ops:
  2.3 20.1 %collective-permute-start = (f32[97,8,128]{2,1,0:T(8,128)S(1)}, f32[97,8,128]{2,1,0:T(8,128)S(1)}, u32[]{:S(2)}, u32[]{:S(2)}) collective-permute-start(f32[97,8,128]{2,1,0:T(8,128)S(1)} %get-tuple-element.33), channel_id=1, source_target_pairs={{0,1},{1,2},{2,3},{3,4},{4,5},{5,6},{6,7},{7,8},{8,9},{9,10},{10,1... | collective-permute-start | bytes 1191944 | tf_op jit(solution)/shard_map/ppermute | solution.py:597
  4.4 18.0 %collective-permute-start.1 = (f32[97,8,128]{2,1,0:T(8,128)S(1)}, f32[97,8,128]{2,1,0:T(8,128)S(1)}, u32[]{:S(2)}, u32[]{:S(2)}) collective-permute-start(f32[97,8,128]{2,1,0:T(8,128)S(1)} %get-tuple-element.34), channel_id=1, source_target_pairs={{0,15},{1,0},{2,1},{3,2},{4,3},{5,4},{6,5},{7,6},{8,7},{9,8},{10,9... | collective-permute-start | bytes 1191944 | tf_op jit(solution)/shard_map/ppermute | solution.py:597
  8.2 4.4 %collective-permute-start.2 = (f32[7,8,128]{2,1,0:T(8,128)S(1)}, f32[7,8,128]{2,1,0:T(8,128)S(1)}, u32[]{:S(2)}, u32[]{:S(2)}) collective-permute-start(f32[7,8,128]{2,1,0:T(8,128)S(1)} %get-tuple-element.31.x_left), channel_id=1, source_target_pairs={{0,240},{16,0},{32,16},{48,32},{64,48},{80,64},{96,80},{112,96},{1... | collective-permute-start | bytes 86024 | tf_op jit(solution)/shard_map/ppermute | solution.py:597
  10.9 3.9 %collective-permute-start.3 = (f32[7,8,128]{2,1,0:T(8,128)S(1)}, f32[7,8,128]{2,1,0:T(8,128)S(1)}, u32[]{:S(2)}, u32[]{:S(2)}) collective-permute-start(f32[7,8,128]{2,1,0:T(8,128)S(1)} %get-tuple-element.32.x_right), channel_id=1, source_target_pairs={{0,16},{16,32},{32,48},{48,64},{64,80},{80,96},{96,112},{112,128},... | collective-permute-start | bytes 86024 | tf_op jit(solution)/shard_map/ppermute | solution.py:597
  14.9 3.1 %collective-permute-start.4 = (f32[8,8,128]{2,1,0:T(8,128)S(1)}, f32[8,8,128]{2,1,0:T(8,128)S(1)}, u32[]{:S(2)}, u32[]{:S(2)}) collective-permute-start(f32[8,8,128]{2,1,0:T(8,128)S(1)} %get-tuple-element.35), channel_id=1, source_target_pairs={{0,15},{1,0},{2,1},{3,2},{4,3},{5,4},{6,5},{7,6},{8,7},{9,8},{10,9... | collective-permute-start | bytes 98312 | tf_op jit(solution)/shard_map/ppermute | solution.py:597
  16.3 6.1 %collective-permute-start.5 = (f32[8,8,128]{2,1,0:T(8,128)S(1)}, f32[8,8,128]{2,1,0:T(8,128)S(1)}, u32[]{:S(2)}, u32[]{:S(2)}) collective-permute-start(f32[8,8,128]{2,1,0:T(8,128)S(1)} %get-tuple-element.36), channel_id=1, source_target_pairs={{0,1},{1,2},{2,3},{3,4},{4,5},{5,6},{6,7},{7,8},{8,9},{9,10},{10,1... | collective-permute-start | bytes 98312 | tf_op jit(solution)/shard_map/ppermute | solution.py:597
  28.0 6.3 %collective-permute-start.7 = (f32[1,8,128]{2,1,0:T(8,128)S(1)}, f32[1,8,128]{2,1,0:T(8,128)S(1)}, u32[]{:S(2)}, u32[]{:S(2)}) collective-permute-start(f32[1,8,128]{2,1,0:T(8,128)S(1)} %slice.3), channel_id=1, source_target_pairs={{0,240},{16,0},{32,16},{48,32},{64,48},{80,64},{96,80},{112,96},{1... | collective-permute-start | bytes 12296 | tf_op jit(solution)/shard_map/ppermute | solution.py:597
  33.3 1.2 %collective-permute-start.6 = (f32[1,8,128]{2,1,0:T(8,128)S(1)}, f32[1,8,128]{2,1,0:T(8,128)S(1)}, u32[]{:S(2)}, u32[]{:S(2)}) collective-permute-start(f32[1,8,128]{2,1,0:T(8,128)S(1)} %slice.3), channel_id=1, source_target_pairs={{0,16},{16,32},{32,48},{48,64},{64,80},{80,96},{96,112},{112,128},... | collective-permute-start | bytes 12296 | tf_op jit(solution)/shard_map/ppermute | solution.py:597
  34.5 2.9 %collective-permute-start.9 = (f32[11,8,128]{2,1,0:T(8,128)S(1)}, f32[11,8,128]{2,1,0:T(8,128)S(1)}, u32[]{:S(2)}, u32[]{:S(2)}) collective-permute-start(f32[11,8,128]{2,1,0:T(8,128)S(1)} %constant_dynamic-update-slice_fusion), channel_id=1, source_target_pairs={{0,15},{1,0},{2,1},{3,2},{4,3},{5,4},{6,5},{7,6},{8,7},{9,8},{10,9... | collective-permute-start | bytes 135176 | tf_op jit(solution)/shard_map/ppermute | solution.py:597
  34.5 6.3 %collective-permute-start.8 = (f32[11,8,128]{2,1,0:T(8,128)S(1)}, f32[11,8,128]{2,1,0:T(8,128)S(1)}, u32[]{:S(2)}, u32[]{:S(2)}) collective-permute-start(f32[11,8,128]{2,1,0:T(8,128)S(1)} %constant_dynamic-update-slice_fusion), channel_id=1, source_target_pairs={{0,1},{1,2},{2,3},{3,4},{4,5},{5,6},{6,7},{7,8},{8,9},{9,10},{10,1... | collective-permute-start | bytes 135176 | tf_op jit(solution)/shard_map/ppermute | solution.py:597

commit v7 on v6

--- a/solution.py
+++ b/solution.py
@@ -455,8 +455,8 @@
     first_lane, last_lane = lane == 0, lane == 127
     sources = (
         (own, left[0], right[0]),
-        (up, up[9], up[10]),
-        (down, down[9], down[10]),
+        (up, up[10], up[9]),
+        (down, down[10], down[9]),
     )
     for r, (main, low, high) in enumerate(sources):
         for s in range(8):
@@ -642,8 +642,8 @@
         corner_down,
     )
     strip = edge[8:]
+    right = send(strip, "gx", -1)
     left = send(strip, "gx", 1)
-    right = send(strip, "gx", -1)
     pop_new, conc_new = call(
         finish_kernel,
         "finish",
@@ -653,8 +653,8 @@
         mask,
         conc_last,
     )
-    left, right, pop_new, conc_new = lax.optimization_barrier((left, right, pop_new, conc_new))
-    wide = jnp.concatenate([edge, left, right])
+    right, left, pop_new, conc_new = lax.optimization_barrier((right, left, pop_new, conc_new))
+    wide = jnp.concatenate([edge, right, left])
     above = send(wide, "gy", -1)
     below = send(wide, "gy", 1)
     devices = lax.axis_size("gx") * lax.axis_size("gy")

time: 66 us -> 65.7 us (level)
  transfers between devices with their start and end apart: 10 -> 10, of which waited for: 7 -> 6; matrix products, arithmetic and copies ran while one was open for 0% -> 0% of each run, Pallas kernels for 2% -> 2%
where the time goes in v7:
time: 65.7 us; the launch traced here: 65.6 us
  blocking collectives  22.6 us (34%)
  starting transfers between devices  17 us (26%)
  waiting for transfers between devices  14.8 us (23%)
  Pallas kernels  10.5 us (16%)
  between operations  0.7 us (1%)
    all_to_all x1, blocking collectives, local(): rows = lax.all_to_all(rows, ('gx', 'gy'), 0, 0, tiled=True)  22.6 us
    ppermute x10, starting transfers between devices, send(): lax.ppermute(block, axis, [(i, (i + step) % count) for i in range(count)])  17 us
    ppermute x10, waiting for transfers between devices, send(): lax.ppermute(block, axis, [(i, (i + step) % count) for i in range(count)])  14.8 us
    pallas_call x6, Pallas kernels, call(): pl.pallas_call(kernel, name=name, out_shape=outs, in_specs=in_specs or in...  10.5 us
  transfers between devices with their start and end apart: 10, of which 6 were waited for; matrix products, arithmetic and copies ran while one was open for 0% of the time, Pallas kernels for 2%

profile of v7, /device:TPU:1, one launch (start us, length us, event | category | flops | bytes accessed | tf_op | source)
XLA Modules:
  0.0 65.6 jit_solution(17613217422851952413)
XLA Ops:
  0.6 1.6 %pack.1 = (f32[19,8,8,128]{3,2,1,0:T(8,128)S(1)}, f32[3,8,8,128]{3,2,1,0:T(8,128)S(1)}, f32[8,8,128]{2,1,0:T(8,128)S(1)}, s32[8,8,128]{2,1,0:T(8,128)S(1)}, s32[...) custom-call(f32[19,8,8,128]{3,2,1,0:T(8,128)} %pop_in.1, ...), custom_call_target="tpu_custom_call" | custom-call | tf_op jit(solution)/shard_map/pack/pallas_call | solution.py:581
  2.3 2.1 %collective-permute-start = (f32[97,8,128]{2,1,0:T(8,128)S(1)}, f32[97,8,128]{2,1,0:T(8,128)S(1)}, u32[]{:S(2)}, u32[]{:S(2)}) collective-permute-start(f32[97,8,128]{2,1,0:T(8,128)S(1)} %get-tuple-element.33), channel_id=1, source_target_pairs={{0,1},{1,2},{2,3},{3,4},{4,5},{5,6},{6,7},{7,8},{8,9},{9,10},{10,1... | collective-permute-start | bytes 1191944 | tf_op jit(solution)/shard_map/ppermute | solution.py:597
  4.4 3.8 %collective-permute-start.1 = (f32[97,8,128]{2,1,0:T(8,128)S(1)}, f32[97,8,128]{2,1,0:T(8,128)S(1)}, u32[]{:S(2)}, u32[]{:S(2)}) collective-permute-start(f32[97,8,128]{2,1,0:T(8,128)S(1)} %get-tuple-element.34), channel_id=1, source_target_pairs={{0,15},{1,0},{2,1},{3,2},{4,3},{5,4},{6,5},{7,6},{8,7},{9,8},{10,9... | collective-permute-start | bytes 1191944 | tf_op jit(solution)/shard_map/ppermute | solution.py:597
  8.2 2.7 %collective-permute-start.2 = (f32[7,8,128]{2,1,0:T(8,128)S(1)}, f32[7,8,128]{2,1,0:T(8,128)S(1)}, u32[]{:S(2)}, u32[]{:S(2)}) collective-permute-start(f32[7,8,128]{2,1,0:T(8,128)S(1)} %get-tuple-element.31.x_left), channel_id=1, source_target_pairs={{0,240},{16,0},{32,16},{48,32},{64,48},{80,64},{96,80},{112,96},{1... | collective-permute-start | bytes 86024 | tf_op jit(solution)/shard_map/ppermute | solution.py:597
  10.9 0.0 collective-permute-start.3
  11.0 1.6 %collective-permute-done.2.right.from_right = f32[7,8,128]{2,1,0:T(8,128)S(1)} collective-permute-done((f32[7,8,128]{2,1,0:T(8,128)S(1)}, f32[7,8,128]{2,1,0:T(8,128)S(1)}, u32[]{:S(2)}, u32[]{:S(2)}) %collective-permute-start.2) | collective-permute-done | bytes 28704 | tf_op jit(solution)/shard_map/ppermute | solution.py:597
  12.6 2.3 %collective-permute-done.3.left.from_left = f32[7,8,128]{2,1,0:T(8,128)S(1)} collective-permute-done((f32[7,8,128]{2,1,0:T(8,128)S(1)}, f32[7,8,128]{2,1,0:T(8,128)S(1)}, u32[]{:S(2)}, u32[]{:S(2)}) %collective-permute-start.3) | collective-permute-done | bytes 28704 | tf_op jit(solution)/shard_map/ppermute | solution.py:597
  14.9 1.5 %collective-permute-start.4 = (f32[8,8,128]{2,1,0:T(8,128)S(1)}, f32[8,8,128]{2,1,0:T(8,128)S(1)}, u32[]{:S(2)}, u32[]{:S(2)}) collective-permute-start(f32[8,8,128]{2,1,0:T(8,128)S(1)} %get-tuple-element.35), channel_id=1, source_target_pairs={{0,15},{1,0},{2,1},{3,2},{4,3},{5,4},{6,5},{7,6},{8,7},{9,8},{10,9... | collective-permute-start | bytes 98312 | tf_op jit(solution)/shard_map/ppermute | solution.py:597
  16.3 0.1 collective-permute-start.5
  16.4 1.6 %collective-permute-done.4.corner_up = f32[8,8,128]{2,1,0:T(8,128)S(1)} collective-permute-done((f32[8,8,128]{2,1,0:T(8,128)S(1)}, f32[8,8,128]{2,1,0:T(8,128)S(1)}, u32[]{:S(2)}, u32[]{:S(2)}) %collective-permute-start.4) | collective-permute-done | bytes 32800 | tf_op jit(solution)/shard_map/ppermute | solution.py:597
  18.0 4.4 %collective-permute-done.5.corner_down = f32[8,8,128]{2,1,0:T(8,128)S(1)} collective-permute-done((f32[8,8,128]{2,1,0:T(8,128)S(1)}, f32[8,8,128]{2,1,0:T(8,128)S(1)}, u32[]{:S(2)}, u32[]{:S(2)}) %collective-permute-start.5) | collective-permute-done | bytes 32800 | tf_op jit(solution)/shard_map/ppermute | solution.py:597
  22.4 0.0 collective-permute-done.down
  22.4 0.0 collective-permute-done.1.up
  22.4 5.6 %steps.1 = (f32[19,18,8,128]{3,2,1,0:T(8,128)S(1)}, f32[18,18,8,128]{3,2,1,0:T(8,128)S(1)}, f32[3,18,8,128]{3,2,1,0:T(8,128)S(1)}, f32[9,8,128]{2,1,0:T(8,128)S(1)}) custom-call(f32[19,8,8,128]{3,2,1,0:T(8,128)S(1)} %get-tuple-element.26.pop, f32[3,8,8,128]{3,2,1,0:T(8,128)S(1)} %get-tuple-element.27.conc, f32[8,8,128]{2,1,0:T(8,128)S(1)} %get-tuple-element.28.pot, ...), custom_call_target="tpu_custom_call" | custom-call | tf_op jit(solution)/shard_map/steps/pallas_call | solution.py:581
  28.0 0.8 %collective-permute-start.7 = (f32[1,8,128]{2,1,0:T(8,128)S(1)}, f32[1,8,128]{2,1,0:T(8,128)S(1)}, u32[]{:S(2)}, u32[]{:S(2)}) collective-permute-start(f32[1,8,128]{2,1,0:T(8,128)S(1)} %slice.3), channel_id=1, source_target_pairs={{0,16},{16,32},{32,48},{48,64},{64,80},{80,96},{96,112},{112,128},... | collective-permute-start | bytes 12296 | tf_op jit(solution)/shard_map/ppermute | solution.py:597
  28.9 4.4 %collective-permute-start.6 = (f32[1,8,128]{2,1,0:T(8,128)S(1)}, f32[1,8,128]{2,1,0:T(8,128)S(1)}, u32[]{:S(2)}, u32[]{:S(2)}) collective-permute-start(f32[1,8,128]{2,1,0:T(8,128)S(1)} %slice.3), channel_id=1, source_target_pairs={{0,240},{16,0},{32,16},{48,32},{64,48},{80,64},{96,80},{112,96},{1... | collective-permute-start | bytes 12296 | tf_op jit(solution)/shard_map/ppermute | solution.py:597
  33.3 1.1 %finish.1 = (f32[19,8,8,128]{3,2,1,0:T(8,128)}, f32[3,8,8,128]{3,2,1,0:T(8,128)}) custom-call(f32[19,18,8,128]{3,2,1,0:T(8,128)S(1)} %get-tuple-element.38.g, f32[18,18,8,128]{3,2,1,0:T(8,128)S(1)} %get-tuple-element.39.mask, f32[3,18,8,128]{3,2,1,0:T(8,128)S(1)} %get-tuple-element.40.conc), custom_call_target="tpu_custom_call" | custom-call | tf_op jit(solution)/shard_map/finish/pallas_call | solution.py:581
  34.4 0.0 collective-permute-done.7.left
  34.4 0.0 collective-permute-done.6.right
  34.4 0.1 collective-permute-start.9
  34.5 1.5 %collective-permute-start.8 = (f32[11,8,128]{2,1,0:T(8,128)S(1)}, f32[11,8,128]{2,1,0:T(8,128)S(1)}, u32[]{:S(2)}, u32[]{:S(2)}) collective-permute-start(f32[11,8,128]{2,1,0:T(8,128)S(1)} %constant_dynamic-update-slice_fusion), channel_id=1, source_target_pairs={{0,1},{1,2},{2,3},{3,4},{4,5},{5,6},{6,7},{7,8},{8,9},{9,10},{10,1... | collective-permute-start | bytes 135176 | tf_op jit(solution)/shard_map/ppermute | solution.py:597
  36.0 1.4 %collective-permute-done.9.up = f32[11,8,128]{2,1,0:T(8,128)S(1)} collective-permute-done((f32[11,8,128]{2,1,0:T(8,128)S(1)}, f32[11,8,128]{2,1,0:T(8,128)S(1)}, u32[]{:S(2)}, u32[]{:S(2)}) %collective-permute-start.9) | collective-permute-done | bytes 45088 | tf_op jit(solution)/shard_map/ppermute | solution.py:597
  37.4 3.4 %collective-permute-done.8.down = f32[11,8,128]{2,1,0:T(8,128)S(1)} collective-permute-done((f32[11,8,128]{2,1,0:T(8,128)S(1)}, f32[11,8,128]{2,1,0:T(8,128)S(1)}, u32[]{:S(2)}, u32[]{:S(2)}) %collective-permute-start.8) | collective-permute-done | bytes 45088 | tf_op jit(solution)/shard_map/ppermute | solution.py:597
  40.8 1.1 %levels.1 = (f32[8,8,8,128]{3,2,1,0:T(8,128)S(1)}, f32[256,128]{1,0:T(8,128)S(1)}) custom-call(f32[9,8,128]{2,1,0:T(8,128)S(1)} %get-tuple-element.37.own, f32[1,8,128]{2,1,0:T(8,128)S(1)} %collective-permute-done.7.left, f32[1,8,128]{2,1,0:T(8,128)S(1)} %collective-permute-done.6.right, f32[11,8,128]{2,1,0:T(8,128)S(1)} %collective-permute-done.8.down, ...), custom_call_target="tpu_custom_call" | custom-call | tf_op jit(solution)/shard_map/levels/pallas_call | solution.py:581
  41.9 22.6 %all_to_all.11 = f32[256,1,128]{2,1,0:T(1,128)S(1)} all-to-all(f32[256,1,128]{2,1,0:T(1,128)S(1)} %bitcast.5), channel_id=1, replica_groups=mesh['gx'=16,'gy'=16] {'gx','gy'}, dimensions={0} | all-to-all | bytes 262144 | tf_op jit(solution)/shard_map/all_to_all | solution.py:672
  64.5 1.1 %combine.1 = f32[8,8,128]{2,1,0:T(8,128)} custom-call(f32[256,128]{1,0:T(8,128)S(1)} %bitcast.4, f32[8,8,8,128]{3,2,1,0:T(8,128)S(1)} %get-tuple-element.48.levels, f32[8,8,128]{2,1,0:T(8,128)S(1)} %get-tuple-element.28.pot), custom_call_target="tpu_custom_call" | custom-call | tf_op jit(solution)/shard_map/combine/pallas_call | solution.py:581
  (5 shorter events, 0.0 us)
Async XLA Ops:
  2.3 20.1 %collective-permute-start = (f32[97,8,128]{2,1,0:T(8,128)S(1)}, f32[97,8,128]{2,1,0:T(8,128)S(1)}, u32[]{:S(2)}, u32[]{:S(2)}) collective-permute-start(f32[97,8,128]{2,1,0:T(8,128)S(1)} %get-tuple-element.33), channel_id=1, source_target_pairs={{0,1},{1,2},{2,3},{3,4},{4,5},{5,6},{6,7},{7,8},{8,9},{9,10},{10,1... | collective-permute-start | bytes 1191944 | tf_op jit(solution)/shard_map/ppermute | solution.py:597
  4.4 18.0 %collective-permute-start.1 = (f32[97,8,128]{2,1,0:T(8,128)S(1)}, f32[97,8,128]{2,1,0:T(8,128)S(1)}, u32[]{:S(2)}, u32[]{:S(2)}) collective-permute-start(f32[97,8,128]{2,1,0:T(8,128)S(1)} %get-tuple-element.34), channel_id=1, source_target_pairs={{0,15},{1,0},{2,1},{3,2},{4,3},{5,4},{6,5},{7,6},{8,7},{9,8},{10,9... | collective-permute-start | bytes 1191944 | tf_op jit(solution)/shard_map/ppermute | solution.py:597
  8.2 4.4 %collective-permute-start.2 = (f32[7,8,128]{2,1,0:T(8,128)S(1)}, f32[7,8,128]{2,1,0:T(8,128)S(1)}, u32[]{:S(2)}, u32[]{:S(2)}) collective-permute-start(f32[7,8,128]{2,1,0:T(8,128)S(1)} %get-tuple-element.31.x_left), channel_id=1, source_target_pairs={{0,240},{16,0},{32,16},{48,32},{64,48},{80,64},{96,80},{112,96},{1... | collective-permute-start | bytes 86024 | tf_op jit(solution)/shard_map/ppermute | solution.py:597
  10.9 3.9 %collective-permute-start.3 = (f32[7,8,128]{2,1,0:T(8,128)S(1)}, f32[7,8,128]{2,1,0:T(8,128)S(1)}, u32[]{:S(2)}, u32[]{:S(2)}) collective-permute-start(f32[7,8,128]{2,1,0:T(8,128)S(1)} %get-tuple-element.32.x_right), channel_id=1, source_target_pairs={{0,16},{16,32},{32,48},{48,64},{64,80},{80,96},{96,112},{112,128},... | collective-permute-start | bytes 86024 | tf_op jit(solution)/shard_map/ppermute | solution.py:597
  14.9 3.1 %collective-permute-start.4 = (f32[8,8,128]{2,1,0:T(8,128)S(1)}, f32[8,8,128]{2,1,0:T(8,128)S(1)}, u32[]{:S(2)}, u32[]{:S(2)}) collective-permute-start(f32[8,8,128]{2,1,0:T(8,128)S(1)} %get-tuple-element.35), channel_id=1, source_target_pairs={{0,15},{1,0},{2,1},{3,2},{4,3},{5,4},{6,5},{7,6},{8,7},{9,8},{10,9... | collective-permute-start | bytes 98312 | tf_op jit(solution)/shard_map/ppermute | solution.py:597
  16.3 6.1 %collective-permute-start.5 = (f32[8,8,128]{2,1,0:T(8,128)S(1)}, f32[8,8,128]{2,1,0:T(8,128)S(1)}, u32[]{:S(2)}, u32[]{:S(2)}) collective-permute-start(f32[8,8,128]{2,1,0:T(8,128)S(1)} %get-tuple-element.36), channel_id=1, source_target_pairs={{0,1},{1,2},{2,3},{3,4},{4,5},{5,6},{6,7},{7,8},{8,9},{9,10},{10,1... | collective-permute-start | bytes 98312 | tf_op jit(solution)/shard_map/ppermute | solution.py:597
  28.0 6.4 %collective-permute-start.7 = (f32[1,8,128]{2,1,0:T(8,128)S(1)}, f32[1,8,128]{2,1,0:T(8,128)S(1)}, u32[]{:S(2)}, u32[]{:S(2)}) collective-permute-start(f32[1,8,128]{2,1,0:T(8,128)S(1)} %slice.3), channel_id=1, source_target_pairs={{0,16},{16,32},{32,48},{48,64},{64,80},{80,96},{96,112},{112,128},... | collective-permute-start | bytes 12296 | tf_op jit(solution)/shard_map/ppermute | solution.py:597
  28.9 5.5 %collective-permute-start.6 = (f32[1,8,128]{2,1,0:T(8,128)S(1)}, f32[1,8,128]{2,1,0:T(8,128)S(1)}, u32[]{:S(2)}, u32[]{:S(2)}) collective-permute-start(f32[1,8,128]{2,1,0:T(8,128)S(1)} %slice.3), channel_id=1, source_target_pairs={{0,240},{16,0},{32,16},{48,32},{64,48},{80,64},{96,80},{112,96},{1... | collective-permute-start | bytes 12296 | tf_op jit(solution)/shard_map/ppermute | solution.py:597
  34.4 3.0 %collective-permute-start.9 = (f32[11,8,128]{2,1,0:T(8,128)S(1)}, f32[11,8,128]{2,1,0:T(8,128)S(1)}, u32[]{:S(2)}, u32[]{:S(2)}) collective-permute-start(f32[11,8,128]{2,1,0:T(8,128)S(1)} %constant_dynamic-update-slice_fusion), channel_id=1, source_target_pairs={{0,15},{1,0},{2,1},{3,2},{4,3},{5,4},{6,5},{7,6},{8,7},{9,8},{10,9... | collective-permute-start | bytes 135176 | tf_op jit(solution)/shard_map/ppermute | solution.py:597
  34.5 6.3 %collective-permute-start.8 = (f32[11,8,128]{2,1,0:T(8,128)S(1)}, f32[11,8,128]{2,1,0:T(8,128)S(1)}, u32[]{:S(2)}, u32[]{:S(2)}) collective-permute-start(f32[11,8,128]{2,1,0:T(8,128)S(1)} %constant_dynamic-update-slice_fusion), channel_id=1, source_target_pairs={{0,1},{1,2},{2,3},{3,4},{4,5},{5,6},{6,7},{7,8},{8,9},{9,10},{10,1... | collective-permute-start | bytes 135176 | tf_op jit(solution)/shard_map/ppermute | solution.py:597
